TPU v7x, 32 devices: a whole 2x2x4 slice. The times are simulated.
32 devices in a mesh: group: 2 (over y), clip: 4 (over z), pix: 4 (over x, core).
Axes of the slice: x: 2, y: 2, z: 4, core: 2. Of those that a mesh axis runs over, the one named last changes fastest.
Arguments:
- latents: bfloat16 [64, 256, 320], P(('group', 'clip'), 'pix'), parts along dimension 0, may hold values from -6 to 6
- sampled: int32 [8], P(('group', 'clip')), parts along dimension 0, may hold values from 0 to 7
- temporal_gain: float32 [320], replicated, may hold values from 0.5 to 1.5
- temporal_qkv: bfloat16 [320, 960], replicated, may hold values from -64 to 64
- temporal_out: bfloat16 [320, 320], replicated, may hold values from -0.3125 to 0.3125
- spatial_gain: float32 [320], replicated, may hold values from 0.5 to 1.5
- spatial_qkv: bfloat16 [320, 960], replicated, may hold values from -64 to 64
- spatial_out: bfloat16 [320, 320], replicated, may hold values from -0.3125 to 0.3125
Outputs:
- refined: bfloat16 [64, 256, 320], P(('group', 'clip', 'pix')), parts along dimension 0
There are 2 independent parts, one for each index of `group`. A program takes and returns all parts, laid end to end along the dimension named above; an argument that names none is the same for every part. Nothing has to cross between parts.
All inputs are finite; a program needn't handle non-finite values.
Results may differ from a plain program's by a relative error of at most 0.014.
The roundings to bfloat16 on the way count: a program that leaves them out, or rounds other values in their place, can miss the bound.
Values may be sent and summed in bfloat16 or wider, within the bound.
No kernel may reach another device: no remote copies, remote signals or barrier semaphores. Data moves between devices by JAX's collectives and lax.ppermute only.
A program may use at most 64 MiB of HBM per device.

v0:
```python
import math

import jax
import jax.numpy as jnp
from jax import lax
from jax.sharding import PartitionSpec as P

HEADS = 5
HEAD_DIM = 64
HALO = 4


def with_halo(block, sides, width):
    for axis, dim in sides:
        count = lax.axis_size(axis)
        forward = [(i, i + 1) for i in range(count - 1)]
        backward = [(target, source) for source, target in forward]
        low = lax.ppermute(
            lax.slice_in_dim(block, block.shape[dim] - width, None, axis=dim), axis, forward
        )
        high = lax.ppermute(lax.slice_in_dim(block, 0, width, axis=dim), axis, backward)
        block = jnp.concatenate([low, block, high], axis=dim)
    return block


def layer_norm(frame_rows, scales):
    values = frame_rows.astype(jnp.float32)
    average = jnp.mean(values, axis=-1, keepdims=True)
    centred = values - average
    spread = jnp.mean(centred * centred, axis=-1, keepdims=True)
    return (centred * lax.rsqrt(spread + 1e-05) * scales).astype(jnp.bfloat16)


def project(frame_rows, matrix):
    shape = frame_rows.shape
    flat = frame_rows.reshape(-1, shape[-1])
    result = jnp.dot(flat, matrix, preferred_element_type=jnp.float32).astype(jnp.bfloat16)
    return result.reshape(shape[:-1] + (matrix.shape[1],))


def temporal_attend(queries, key_pairs, usable):
    count, pixels, channels = queries.shape
    depth = key_pairs.shape[0]
    keys = key_pairs[..., :channels].reshape(depth, pixels, HEADS, HEAD_DIM)
    values = key_pairs[..., channels:].reshape(depth, pixels, HEADS, HEAD_DIM)
    query_heads = queries.reshape(count, pixels, HEADS, HEAD_DIM)
    scores = jnp.einsum(
        "fphd,kphd->phfk", query_heads, keys, preferred_element_type=jnp.float32
    ) / math.sqrt(HEAD_DIM)
    scores = jnp.where(usable[None, None, None, :], scores, -1e30)
    highest = jnp.max(scores, axis=-1, keepdims=True)
    expo = jnp.exp(scores - highest)
    weights = (expo / jnp.sum(expo, axis=-1, keepdims=True)).astype(jnp.bfloat16)
    mixed = jnp.einsum("phfk,kphd->fphd", weights, values, preferred_element_type=jnp.float32)
    return mixed.reshape(count, pixels, channels).astype(jnp.bfloat16)


def spatial_frame(frame_rows, scales, qkv_matrix, out_matrix):
    pixels, channels = frame_rows.shape
    normed = layer_norm(frame_rows, scales)
    packed = jnp.dot(normed, qkv_matrix, preferred_element_type=jnp.float32).astype(jnp.bfloat16)
    heads_view = packed.reshape(pixels, 3, HEADS, HEAD_DIM).transpose(1, 2, 0, 3)
    block_rows = 512 if pixels % 512 == 0 else pixels

    def one_head(triple):
        queries, keys, values = triple

        def query_block(query_rows):
            scores = jnp.dot(query_rows, keys.T, preferred_element_type=jnp.float32) / math.sqrt(
                HEAD_DIM
            )
            highest = jnp.max(scores, axis=-1, keepdims=True)
            expo = jnp.exp(scores - highest)
            weights = (expo / jnp.sum(expo, axis=-1, keepdims=True)).astype(jnp.bfloat16)
            return jnp.dot(weights, values, preferred_element_type=jnp.float32).astype(jnp.bfloat16)

        blocks = lax.map(query_block, queries.reshape(pixels // block_rows, block_rows, HEAD_DIM))
        return blocks.reshape(pixels, HEAD_DIM)

    mixed = lax.map(one_head, (heads_view[0], heads_view[1], heads_view[2]))
    mixed = mixed.transpose(1, 0, 2).reshape(pixels, channels)
    update = jnp.dot(mixed, out_matrix, preferred_element_type=jnp.float32)
    return (frame_rows.astype(jnp.float32) + update).astype(jnp.bfloat16)


def body(
    latents,
    sampled,
    temporal_gain,
    temporal_qkv,
    temporal_out,
    spatial_gain,
    spatial_qkv,
    spatial_out,
):
    frames_here, pixel_count, channels = latents.shape
    normed = layer_norm(latents, temporal_gain)
    queries = project(normed, temporal_qkv[:, :channels])
    pair_matrix = temporal_qkv[:, channels:]
    picked = lax.dynamic_slice_in_dim(normed, sampled[0], 1, 0)
    global_pairs = project(lax.all_gather(picked, "clip", axis=0, tiled=True), pair_matrix)
    border_rows = with_halo(normed, (("clip", 0),), HALO)
    border = project(border_rows, pair_matrix)
    clip_index = lax.axis_index("clip")
    clip_count = lax.axis_size("clip")
    positions = (
        clip_index * frames_here - HALO + jnp.arange(frames_here + 2 * HALO, dtype=jnp.int32)
    )
    inside = (positions >= 0) & (positions < clip_count * frames_here)
    usable = jnp.concatenate([inside, jnp.ones((global_pairs.shape[0],), jnp.bool_)])
    attended = temporal_attend(queries, jnp.concatenate([border, global_pairs], 0), usable)
    update = jnp.dot(
        attended.reshape(-1, channels), temporal_out, preferred_element_type=jnp.float32
    )
    temporal_rows = (latents.astype(jnp.float32).reshape(-1, channels) + update).astype(
        jnp.bfloat16
    )
    pix_count = lax.axis_size("pix")
    per_device = frames_here // pix_count
    grouped = temporal_rows.reshape(pix_count, per_device, pixel_count, channels)
    frame_block = lax.all_to_all(grouped, "pix", split_axis=0, concat_axis=2, tiled=True)[0]
    result = lax.map(
        lambda frame_rows: spatial_frame(frame_rows, spatial_gain, spatial_qkv, spatial_out),
        frame_block,
    )
    whole = result[None]
    return whole.reshape(whole.shape[1], whole.shape[2], channels)


def solution(mesh):
    placed = (P(("group", "clip"), "pix", None), P(("group", "clip")), P(), P(), P(), P(), P(), P())
    return jax.shard_map(
        body,
        mesh=mesh,
        in_specs=placed,
        out_specs=P(("group", "clip", "pix"), None, None),
        check_vma=False,
    )
```

profile of v0, /device:TPU:0, one launch (start us, length us, event | category | flops | bytes accessed | tf_op | source)
XLA Modules:
  0.0 77.4 jit_solution(4738823542584057212)
XLA Ops:
  0.0 1.2 %convert_reduce_fusion.1 = f32[8,64]{1,0:T(8,128)S(1)} fusion(bf16[8,64,320]{2,1,0:T(8,128)(2,1)} %param.12), kind=kLoop, calls=%fused_computation.59 | loop fusion | flops 327168 | bytes 329728 | tf_op jit(solution)/shard_map/reduce_sum | solution.py:28
  1.2 1.3 %multiply_reduce_fusion = f32[8,64]{1,0:T(8,128)S(1)} fusion(bf16[8,64,320]{2,1,0:T(8,128)(2,1)} %param.12, f32[8,64]{1,0:T(8,128)S(1)} %broadcast_multiply_fusion.1), kind=kLoop, calls=%fused_computation.57 | loop fusion | flops 654848 | bytes 331776 | tf_op jit(solution)/shard_map/reduce_sum | solution.py:30
  2.5 1.2 %multiply_convert_fusion = bf16[8,64,320]{2,1,0:T(8,128)(2,1)S(1)} fusion(bf16[8,64,320]{2,1,0:T(8,128)(2,1)} %param.12, f32[320]{0:T(512)} %param.14, f32[8,64]{1,0:T(8,128)S(1)} %add_rsqrt_fusion.1, f32[8,64]{1,0:T(8,128)S(1)} %broadcast_multiply_fusion.1), kind=kLoop, calls=%fused_computation.56 | loop fusion | flops 819200 | bytes 660736 | tf_op jit(solution)/shard_map/convert_element_type | solution.py:31
  3.7 0.8 %fusion.38 = (bf16[4,64,320]{2,1,0:T(8,128)(2,1)}, bf16[4,64,320]{2,1,0:T(8,128)(2,1)}) fusion(bf16[8,64,320]{2,1,0:T(8,128)(2,1)S(1)} %multiply_convert_fusion), kind=kLoop, calls=%fused_computation.68 | loop fusion | bytes 655360 | tf_op jit(solution)/shard_map/slice | solution.py:19
  4.5 5.0 %collective-permute-start = (bf16[4,64,320]{2,1,0:T(8,128)(2,1)}, bf16[4,64,320]{2,1,0:T(8,128)(2,1)S(1)}, u32[]{:S(2)}, u32[]{:S(2)}) collective-permute-start(bf16[4,64,320]{2,1,0:T(8,128)(2,1)} %get-tuple-element.121), channel_id=1, source_target_pairs={{0,4},{4,8},{8,12},{1,5},{5,9},{9,13},{2,6},{6,10},{10,14},{3,7},{... | collective-permute-start | bytes 491528 | tf_op jit(solution)/shard_map/ppermute | solution.py:18
  9.5 1.3 %collective-permute-start.1 = (bf16[4,64,320]{2,1,0:T(8,128)(2,1)}, bf16[4,64,320]{2,1,0:T(8,128)(2,1)}, u32[]{:S(2)}, u32[]{:S(2)}) collective-permute-start(bf16[4,64,320]{2,1,0:T(8,128)(2,1)} %get-tuple-element.122), channel_id=1, source_target_pairs={{4,0},{8,4},{12,8},{5,1},{9,5},{13,9},{6,2},{10,6},{14,10},{7,3},{... | collective-permute-start | bytes 491528 | tf_op jit(solution)/shard_map/ppermute | solution.py:21
  11.5 16.6 %all_gather.3 = bf16[4,64,320]{2,1,0:T(8,128)(2,1)S(1)} all-gather(bf16[1,64,320]{2,1,0:T(8,128)(2,1)S(1)} %constant_dynamic-slice_fusion), channel_id=1, replica_groups=mesh['group'=2,'clip'=4,'pix'=4] {'clip'}, dimensions={0}, use_global_device_ids=true | all-gather | bytes 204800 | tf_op jit(solution)/shard_map/all_gather | solution.py:101
  28.1 0.4 convolution_convert_fusion.4
  28.5 0.5 convolution_convert_fusion.5
  28.9 1.1 %copy.26 = bf16[4,64,640]{1,2,0:T(8,128)(2,1)} copy(bf16[4,64,640]{2,1,0:T(8,128)(2,1)S(1)} %bitcast.127) | data formatting | bytes 655360 | tf_op jit(solution)/shard_map/reshape | solution.py:38
  30.0 0.3 reshape_reshape.3
  30.4 0.6 copy.27
  31.0 1.0 %copy.31 = f32[512,320]{0,1:T(8,128)} copy(bf16[512,320]{1,0:T(8,128)(2,1)S(1)} %bitcast.121) | data formatting | bytes 983040 | tf_op jit(solution)/shard_map/reshape | solution.py:115
  32.0 1.1 %pad_maximum_fusion.1 = bf16[16,64,320]{2,1,0:T(8,128)(2,1)S(1)} fusion(bf16[4,64,320]{2,1,0:T(8,128)(2,1)} %collective-permute-done.1, bf16[8,64,320]{2,1,0:T(8,128)(2,1)S(1)} %multiply_convert_fusion, bf16[4,64,320]{2,1,0:T(8,128)(2,1)S(1)} %collective-permute-done), kind=kLoop, calls=%fused_computation.55 | loop fusion | flops 655360 | bytes 1310720 | tf_op jit(solution)/shard_map/concatenate | solution.py:22
  33.1 2.0 %convolution_convert_fusion.2 = bf16[1024,640]{1,0:T(8,128)(2,1)} fusion(bf16[1024,320]{1,0:T(8,128)(2,1)S(1)} %bitcast.124, bf16[320,960]{1,0:T(8,128)(2,1)S(1)} %copy-done.5), kind=kOutput, calls=%fused_computation.43 | convolution fusion | flops 420085760 | bytes 2506752 | tf_op jit(solution)/shard_map/dot_general | solution.py:37
  35.1 3.2 %copy.25 = bf16[16,64,640]{1,2,0:T(8,128)(2,1)S(1)} copy(bf16[16,64,640]{2,1,0:T(8,128)(2,1)} %bitcast.122) | data formatting | bytes 2621440 | tf_op jit(solution)/shard_map/reshape | solution.py:38
  38.4 3.6 %pad_maximum_fusion = (bf16[20,64,320]{1,2,0:T(8,128)(2,1)}, bf16[20,64,320]{1,2,0:T(8,128)(2,1)}) fusion(bf16[4,64,640]{1,2,0:T(8,128)(2,1)} %copy.26, bf16[16,64,640]{1,2,0:T(8,128)(2,1)S(1)} %copy.25), kind=kLoop, calls=%fused_computation.42 | loop fusion | flops 3276800 | bytes 3276800 | tf_op jit(solution)/shard_map/concatenate | solution.py:111
  42.0 2.9 %copy.28 = bf16[20,64,5,64]{3,0,2,1:T(8,128)(2,1)S(1)} copy(bf16[20,64,5,64]{1,3,2,0:T(8,128)(2,1)} %bitcast.120) | data formatting | bytes 1638400 | tf_op jit(solution)/shard_map/reshape | solution.py:44
  45.0 3.9 %copy.29 = bf16[20,64,5,64]{3,0,2,1:T(8,128)(2,1)} copy(bf16[20,64,5,64]{1,3,2,0:T(8,128)(2,1)} %bitcast.119) | data formatting | bytes 1638400 | tf_op jit(solution)/shard_map/reshape | solution.py:45
  48.8 2.3 %fusion.39 = (f32[64,5,8]{2,1,0:T(8,128)S(1)}, f32[64,5,8,20]{3,2,1,0:T(8,128)}) fusion(bf16[8,64,5,64]{3,0,2,1:T(8,128)(2,1)S(1)} %copy.27, bf16[20,64,5,64]{3,0,2,1:T(8,128)(2,1)S(1)} %copy.28, pred[20]{0:T(512)(128)(4,1)S(1)} %concatenate.11), kind=kOutput, calls=%fused_computation.69 | convolution fusion | flops 6758419 | bytes 1361940 | tf_op jit(solution)/shard_map/sub | solution.py:52
  51.1 2.7 %fusion.31 = bf16[8,64,5,64]{3,0,2,1:T(8,128)(2,1)S(1)} fusion(bf16[20,64,5,64]{3,0,2,1:T(8,128)(2,1)} %copy.29, f32[64,5,8,20]{3,2,1,0:T(8,128)} %get-tuple-element.124, f32[64,5,8]{2,1,0:T(8,128)S(1)} %get-tuple-element.123), kind=kOutput, calls=%fused_computation.50 | convolution fusion | flops 6819840 | bytes 1361920 | tf_op jit(solution)/shard_map/phfk,kphd->fphd/dot_general | solution.py:54
  53.8 0.6 copy.30
  54.4 0.4 convert_element_type.64
  54.8 0.1 copy-done.4
  54.9 0.4 fusion.32
  55.3 0.9 %copy.32 = bf16[512,320]{1,0:T(8,128)(2,1)} copy(bf16[512,320]{0,1:T(8,128)(2,1)S(1)} %fusion.32) | data formatting | bytes 655360 | tf_op jit(solution)/shard_map/convert_element_type | solution.py:115
  56.2 3.5 %all-to-all-start = ((bf16[4,2,64,320]{3,2,1,0:T(8,128)(2,1)}), bf16[4,2,64,320]{3,2,1,0:T(8,128)(2,1)S(1)}, u32[]{:S(2)}, u32[]{:S(2)}) async-start(bf16[4,2,64,320]{3,2,1,0:T(8,128)(2,1)} %bitcast.23), calls=%async_computation | async-start | bytes 786432 | tf_op jit(solution)/shard_map/all_to_all | solution.py:121
  59.7 7.4 %all-to-all-done = bf16[4,2,64,320]{3,2,1,0:T(8,128)(2,1)S(1)} async-done(((bf16[4,2,64,320]{3,2,1,0:T(8,128)(2,1)}), bf16[4,2,64,320]{3,2,1,0:T(8,128)(2,1)S(1)}, u32[]{:S(2)}, u32[]{:S(2)}) %all-to-all-start) | async-done | bytes 327712 | tf_op jit(solution)/shard_map/all_to_all | solution.py:121
  67.1 0.2 copy.34
  67.3 10.0 %while.25 = (s32[]{:T(128)}, bf16[2,256,320]{1,2,0:T(8,128)(2,1)}, bf16[2,256,320]{1,2,0:T(8,128)(2,1)S(1)}, f32[320]{0:T(512)S(1)}, bf16[320,960]{1,0:T(8,128)(...) while((s32[]{:T(128)}, bf16[2,256,320]{1,2,0:T(8,128)(2,1)}, ...), condition=%wide.region_11.12_spmd, body=%wide.region_4.11_spmd.sunk | while | flops 228359936 | bytes 7997730 | solution.py:122
  67.4 0.1 fusion.65
  67.5 0.5 convolution_convert_fusion.7
  68.1 0.5 copy.36
  68.5 0.1 slice_bitcast_fusion.4
  68.7 2.6 %while.26 = (s32[]{:T(128)}, bf16[5,256,64]{1,2,0:T(8,128)(2,1)S(1)}, bf16[5,256,64]{2,1,0:T(8,128)(2,1)S(1)}, bf16[5,256,64]{2,1,0:T(8,128)(2,1)S(1)}, bf16[5,256,64]{2,1,0:T(8,128)(2,1)S(1)}, /*index=5*/s32[]{:T(128)}) while((s32[]{:T(128)}, bf16[5,256,64]{1,2,0:T(8,128)(2,1)S(1)}, bf16[5,256,64]{2,1,0:T(8,128)(2,1)S(1)}, ...), condition=%wide.region_10.10_spmd, body=%wide.region_7.9_spmd.sunk | while | flops 17251840 | bytes 1023045 | solution.py:80
  68.7 0.2 fusion.68
  69.0 0.2 fusion.70
  69.2 0.2 fusion.68
  69.5 0.2 fusion.70
  69.7 0.2 fusion.68
  70.0 0.2 fusion.70
  70.3 0.2 fusion.68
  70.6 0.2 fusion.70
  70.8 0.2 fusion.68
  71.1 0.2 fusion.70
  71.3 0.3 fusion.66
  71.6 0.7 copy-done.8
  72.4 0.1 fusion.65
  72.5 0.5 convolution_convert_fusion.7
  73.1 0.5 copy.36
  73.5 0.1 slice_bitcast_fusion.4
  73.7 2.6 %while.26 = (s32[]{:T(128)}, bf16[5,256,64]{1,2,0:T(8,128)(2,1)S(1)}, bf16[5,256,64]{2,1,0:T(8,128)(2,1)S(1)}, bf16[5,256,64]{2,1,0:T(8,128)(2,1)S(1)}, bf16[5,256,64]{2,1,0:T(8,128)(2,1)S(1)}, /*index=5*/s32[]{:T(128)}) while((s32[]{:T(128)}, bf16[5,256,64]{1,2,0:T(8,128)(2,1)S(1)}, bf16[5,256,64]{2,1,0:T(8,128)(2,1)S(1)}, ...), condition=%wide.region_10.10_spmd, body=%wide.region_7.9_spmd.sunk | while | flops 17251840 | bytes 1023045 | solution.py:80
  73.7 0.2 fusion.68
  74.0 0.2 fusion.70
  74.2 0.2 fusion.68
  74.5 0.2 fusion.70
  74.7 0.2 fusion.68
  75.0 0.2 fusion.70
  75.3 0.2 fusion.68
  75.6 0.2 fusion.70
  75.8 0.2 fusion.68
  76.1 0.2 fusion.70
  76.3 0.3 fusion.66
  76.6 0.7 copy-done.8
  (46 shorter events, 1.0 us)
Async XLA Ops:
  0.0 54.8 %copy-start = (bf16[320,320]{1,0:T(8,128)(2,1)S(1)}, bf16[320,320]{1,0:T(8,128)(2,1)}, u32[]{:S(2)}) copy-start(bf16[320,320]{1,0:T(8,128)(2,1)} %param.16) | copy-start | bytes 614404
  0.0 28.1 %copy-start.5 = (bf16[320,960]{1,0:T(8,128)(2,1)S(1)}, bf16[320,960]{1,0:T(8,128)(2,1)}, u32[]{:S(2)}) copy-start(bf16[320,960]{1,0:T(8,128)(2,1)} %param.15) | copy-start | bytes 1843204
  4.5 27.5 %collective-permute-start = (bf16[4,64,320]{2,1,0:T(8,128)(2,1)}, bf16[4,64,320]{2,1,0:T(8,128)(2,1)S(1)}, u32[]{:S(2)}, u32[]{:S(2)}) collective-permute-start(bf16[4,64,320]{2,1,0:T(8,128)(2,1)} %get-tuple-element.121), channel_id=1, source_target_pairs={{0,4},{4,8},{8,12},{1,5},{5,9},{9,13},{2,6},{6,10},{10,14},{3,7},{... | collective-permute-start | bytes 491528 | tf_op jit(solution)/shard_map/ppermute | solution.py:18
  9.5 22.5 %collective-permute-start.1 = (bf16[4,64,320]{2,1,0:T(8,128)(2,1)}, bf16[4,64,320]{2,1,0:T(8,128)(2,1)}, u32[]{:S(2)}, u32[]{:S(2)}) collective-permute-start(bf16[4,64,320]{2,1,0:T(8,128)(2,1)} %get-tuple-element.122), channel_id=1, source_target_pairs={{4,0},{8,4},{12,8},{5,1},{9,5},{13,9},{6,2},{10,6},{14,10},{7,3},{... | collective-permute-start | bytes 491528 | tf_op jit(solution)/shard_map/ppermute | solution.py:21
  28.9 2.0 %copy-start.2 = (bf16[8,64,320]{2,1,0:T(8,128)(2,1)S(1)}, bf16[8,64,320]{2,1,0:T(8,128)(2,1)}, u32[]{:S(2)}) copy-start(bf16[8,64,320]{2,1,0:T(8,128)(2,1)} %param.12) | copy-start | bytes 983044
  53.8 1.1 %copy-start.4 = (f32[512,320]{0,1:T(8,128)S(1)}, f32[512,320]{0,1:T(8,128)}, u32[]{:S(2)}) copy-start(f32[512,320]{0,1:T(8,128)} %copy.31) | copy-start | bytes 1966084
  55.3 12.0 %copy-start.1 = (bf16[320,960]{1,0:T(8,128)(2,1)S(1)}, bf16[320,960]{1,0:T(8,128)(2,1)}, u32[]{:S(2)}) copy-start(bf16[320,960]{1,0:T(8,128)(2,1)} %param.18) | copy-start | bytes 1843204
  55.3 12.0 %copy-start.3 = (bf16[320,320]{1,0:T(8,128)(2,1)S(1)}, bf16[320,320]{1,0:T(8,128)(2,1)}, u32[]{:S(2)}) copy-start(bf16[320,320]{1,0:T(8,128)(2,1)} %param.19) | copy-start | bytes 614404
  55.3 12.0 %copy-start.6 = (f32[320]{0:T(512)S(1)}, f32[320]{0:T(512)}, u32[]{:S(2)}) copy-start(f32[320]{0:T(512)} %param.17) | copy-start | bytes 3844
  56.2 10.8 %all-to-all-start = ((bf16[4,2,64,320]{3,2,1,0:T(8,128)(2,1)}), bf16[4,2,64,320]{3,2,1,0:T(8,128)(2,1)S(1)}, u32[]{:S(2)}, u32[]{:S(2)}) async-start(bf16[4,2,64,320]{3,2,1,0:T(8,128)(2,1)} %bitcast.23), calls=%async_computation | async-start | bytes 786432 | tf_op jit(solution)/shard_map/all_to_all | solution.py:121
  68.6 2.7 %copy-start.7 = (bf16[2,256,320]{1,2,0:T(8,128)(2,1)S(1)}, bf16[2,256,320]{1,2,0:T(8,128)(2,1)}, u32[]{:S(2)}) copy-start(bf16[2,256,320]{1,2,0:T(8,128)(2,1)} %get-tuple-element.244) | copy-start | bytes 983044 | tf_op jit(solution)/shard_map/while
  71.6 0.7 copy-start.8
  73.6 2.7 %copy-start.7 = (bf16[2,256,320]{1,2,0:T(8,128)(2,1)S(1)}, bf16[2,256,320]{1,2,0:T(8,128)(2,1)}, u32[]{:S(2)}) copy-start(bf16[2,256,320]{1,2,0:T(8,128)(2,1)} %get-tuple-element.244) | copy-start | bytes 983044 | tf_op jit(solution)/shard_map/while
  76.6 0.7 copy-start.8
where the time goes:
time: 77.9 us; the launch traced here: 77.4 us
  local copies, waits for them, and re-layouts  18.6 us (24%)
  blocking collectives  16.6 us (21%)
  matrix products  14.3 us (18%)
  starting transfers between devices  9.71 us (12%)
  other arithmetic  9.49 us (12%)
  waiting for transfers between devices  7.37 us (9%)
  between operations  0.92 us (1%)
    all_gather x1, blocking collectives, body(): lax.all_gather(picked, 'clip', axis=0, tiled=True)  16.6 us
    all_to_all x1, waiting for transfers between devices, body(): lax.all_to_all(grouped, 'pix', split_axis=0, concat_axis=2, tiled=True)[0]  7.37 us
    ppermute x1, starting transfers between devices, with_halo(): lax.ppermute(lax.slice_in_dim(block, block.shape[dim] - width, None, axis...  4.96 us
    reshape x2, local copies, waits for them, and re-layouts, project(): return result.reshape(shape[:-1] + (matrix.shape[1],))  4.31 us
    reshape x1, local copies, waits for them, and re-layouts, temporal_attend(): values = key_pairs[..., channels:].reshape(depth, pixels, HEADS, HEAD_DIM)  3.85 us
    concatenate x1, other arithmetic, body(): jnp.concatenate([border, global_pairs], 0)  3.64 us
    all_to_all x1, starting transfers between devices, body(): lax.all_to_all(grouped, 'pix', split_axis=0, concat_axis=2, tiled=True)[0]  3.46 us
    reshape x1, local copies, waits for them, and re-layouts, temporal_attend(): keys = key_pairs[..., :channels].reshape(depth, pixels, HEADS, HEAD_DIM)  2.93 us
  transfers between devices with their start and end apart: 3, of which 1 were waited for; matrix products, arithmetic and copies ran while one was open for 5% of the time, Pallas kernels for 0%

commit v1 on v0

v1 whole, which is shorter than its diff:
```python
import functools
import math

import jax
import jax.numpy as jnp
from jax import lax
from jax.experimental import pallas as pl
from jax.experimental.pallas import tpu as pltpu
from jax.sharding import PartitionSpec as P

HEADS = 5
HEAD_DIM = 64
HALO = 4
SUB = 8
LANES = 128
NEG = -1e30
DIRECT_CLIPS = 4
LIMIT = 24 << 20
ANY = pl.BlockSpec(memory_space=pl.ANY)
VMEM = pl.BlockSpec(memory_space=pltpu.VMEM)
NT = (((1,), (1,)), ((), ()))


def up(count, step):
    return -(-count // step) * step


def tiles_of(channels):
    return [(start, min(LANES, channels - start)) for start in range(0, channels, LANES)]


def pack(rows):
    pixels, channels = rows.shape
    parts = [rows[:, start : start + width] for start, width in tiles_of(channels) if width == LANES]
    if channels % LANES:
        tail = rows[:, channels - channels % LANES :]
        parts.append(jnp.concatenate([tail[: pixels // 2], tail[pixels // 2 :]], axis=1))
    return jnp.concatenate(parts, axis=0)


def unpack(dense, pixels, channels):
    whole = channels // LANES
    parts = [dense[i * pixels : (i + 1) * pixels] for i in range(whole)]
    if channels % LANES:
        tail = dense[whole * pixels :]
        parts.append(jnp.concatenate([tail[:, : LANES // 2], tail[:, LANES // 2 :]], axis=0))
    return jnp.concatenate(parts, axis=1)


def layer_norm(values, scales):
    average = jnp.mean(values, axis=-1, keepdims=True)
    centred = values - average
    spread = jnp.mean(centred * centred, axis=-1, keepdims=True)
    return centred * lax.rsqrt(spread + 1e-05) * scales


def own_lanes(tile, slot):
    lane = lax.broadcasted_iota(jnp.int32, tile.shape, 1)
    return (lane // HEAD_DIM) == slot


def attend(queries, keys, values, bias):
    rows, width = queries.shape
    held = width // HEAD_DIM
    if held > 1:
        zero = jnp.zeros_like(queries)
        stacked = jnp.concatenate(
            [jnp.where(own_lanes(queries, slot), queries, zero) for slot in range(held)], axis=0
        )
    else:
        stacked = queries
    scores = lax.dot_general(stacked, keys, NT, preferred_element_type=jnp.float32)
    if bias is not None:
        scores = scores + (jnp.concatenate([bias] * held, axis=0) if held > 1 else bias)
    highest = jnp.max(scores, axis=-1, keepdims=True)
    expo = jnp.exp((scores - highest) * (1.0 / math.sqrt(HEAD_DIM)))
    total = jnp.sum(expo, axis=-1, keepdims=True)
    mixed = jnp.dot(expo.astype(jnp.bfloat16), values, preferred_element_type=jnp.float32) / total
    result = mixed[:rows]
    for slot in range(1, held):
        part = mixed[slot * rows : (slot + 1) * rows]
        result = jnp.where(own_lanes(part, slot), part, result)
    return result.astype(jnp.bfloat16)


def prep_kernel(border, axis, x_hbm, s_hbm, x_ref, e_ref, o_ref, p_ref, s_ref, x_sem, s_sem):
    copy_x = pltpu.make_async_copy(x_hbm, x_ref, x_sem)
    copy_s = pltpu.make_async_copy(s_hbm, s_ref, s_sem)
    copy_x.start()
    copy_s.start()
    copy_s.wait()
    copy_x.wait()
    odd = lax.rem(lax.axis_index(axis), 2)
    frames = x_ref.shape[0]
    for i in range(border):
        e_ref[i] = pack(x_ref[(1 - odd) * (frames - border) + i])
        o_ref[i] = pack(x_ref[odd * (frames - border) + i])
    picked = pack(x_ref[s_ref[0]])
    p_ref[0] = picked
    if e_ref.shape[0] > border:
        e_ref[border] = picked
        o_ref[border] = picked


def prep(latents, sampled, with_pick):
    frames, pixels, channels = latents.shape
    dense = (pixels * channels // LANES, LANES)
    sent = HALO + (1 if with_pick else 0)
    kind = latents.dtype
    return pl.pallas_call(
        functools.partial(prep_kernel, HALO, "clip"),
        out_shape=[
            pltpu.VMEM(latents.shape, kind),
            pltpu.VMEM((sent,) + dense, kind),
            pltpu.VMEM((sent,) + dense, kind),
            pltpu.VMEM((1,) + dense, kind),
        ],
        in_specs=[ANY, ANY],
        out_specs=[VMEM] * 4,
        scratch_shapes=[
            pltpu.SMEM((1,), jnp.int32),
            pltpu.SemaphoreType.DMA,
            pltpu.SemaphoreType.DMA,
        ],
        compiler_params=pltpu.CompilerParams(vmem_limit_bytes=LIMIT),
        name="prep",
    )(latents, sampled)


def local_kernel(
    x_ref, gain_ref, tq_hbm, to_hbm, sq_hbm, so_hbm,
    q_ref, k_ref, v_ref, xg_ref, tw_ref, sw_ref, to_ref, so_ref,
    tq_ref, sq_ref, normed_ref, sems,
):
    copies = [
        pltpu.make_async_copy(source, target, sems.at[i])
        for i, (source, target) in enumerate(
            ((tq_hbm, tq_ref), (sq_hbm, sq_ref), (to_hbm, to_ref), (so_hbm, so_ref))
        )
    ]
    for copy in copies:
        copy.start()
    frames, pixels, channels = x_ref.shape
    groups = pixels // SUB
    gain = gain_ref[...]
    for f in range(frames):
        values = x_ref[f].astype(jnp.float32)
        normed = layer_norm(values, gain)
        for g in range(groups):
            xg_ref[g, f] = values[g * SUB : (g + 1) * SUB]
            normed_ref[g, f] = normed[g * SUB : (g + 1) * SUB]
    step = up(channels, LANES)

    def spread(source, target):
        target[...] = jnp.zeros_like(target)
        for part in range(3):
            target[:, part * step : part * step + channels] = source[
                :, part * channels : (part + 1) * channels
            ]

    copies[0].wait()
    spread(tq_ref, tw_ref)
    rows = normed_ref[...].reshape(groups * frames * SUB, channels).astype(jnp.bfloat16)
    packed = jnp.dot(rows, tw_ref[...], preferred_element_type=jnp.float32).astype(jnp.bfloat16)
    for part, target in enumerate((q_ref, k_ref, v_ref)):
        target[...] = packed[:, part * step : part * step + channels]
    copies[1].wait()
    spread(sq_ref, sw_ref)
    copies[2].wait()
    copies[3].wait()


def local(latents, gain, temporal_qkv, temporal_out, spatial_qkv, spatial_out):
    frames, pixels, channels = latents.shape
    count = frames * pixels
    kind = latents.dtype
    wide = (channels, 3 * up(channels, LANES))
    return pl.pallas_call(
        local_kernel,
        out_shape=[pltpu.VMEM((count, channels), kind)] * 3
        + [pltpu.VMEM((pixels // SUB, frames, SUB, channels), jnp.float32)]
        + [pltpu.VMEM(wide, kind)] * 2
        + [pltpu.VMEM((channels, channels), kind)] * 2,
        in_specs=[VMEM, pl.BlockSpec()] + [ANY] * 4,
        out_specs=[VMEM] * 8,
        scratch_shapes=[
            pltpu.VMEM(temporal_qkv.shape, kind),
            pltpu.VMEM(spatial_qkv.shape, kind),
            pltpu.VMEM((pixels // SUB, frames, SUB, channels), jnp.float32),
            pltpu.SemaphoreType.DMA((4,)),
        ],
        cost_estimate=pl.CostEstimate(
            flops=2 * count * channels * 3 * channels, bytes_accessed=4 << 20, transcendentals=0
        ),
        compiler_params=pltpu.CompilerParams(vmem_limit_bytes=LIMIT),
        name="local",
    )(latents, gain.reshape(1, channels), temporal_qkv, temporal_out, spatial_qkv, spatial_out)


def temporal_kernel(
    clips, gathered, far_steps, pix_count,
    q_ref, k_ref, v_ref, xg_ref, gain_ref, tw_ref, to_ref, e_ref, o_ref, *rest,
):
    pick_refs = rest[: 1 + (0 if gathered else len(far_steps))]
    rest = rest[len(pick_refs) :]
    sends, (normed_ref, att_ref, rows_ref) = rest[:pix_count], rest[pix_count:]
    groups, frames, _, channels = xg_ref.shape
    pixels = groups * SUB
    slots = normed_ref.shape[1]
    me = lax.axis_index("clip")
    odd = lax.rem(me, 2)
    outer = jnp.where(odd == 1, me + 1, me - 1)
    inner = jnp.where(odd == 1, me - 1, me + 1)
    outer_there = (outer >= 0) & (outer < clips)
    inner_there = inner < clips
    gain = gain_ref[...]

    dense = [e_ref[i] for i in range(HALO)] + [o_ref[i] for i in range(HALO)]
    if gathered:
        dense += [pick_refs[0][i] for i in range(clips)]
    else:
        dense += [pick_refs[0][0]]
        if clips > 1:
            dense += [e_ref[HALO]]
        for step, ref in zip(far_steps, pick_refs[1:]):
            other = jnp.bitwise_xor(me, step)
            near = jnp.abs(other - me) == 1
            dense += [jnp.where(near, o_ref[HALO], ref[0])]
    for j, frame in enumerate(dense):
        normed = layer_norm(unpack(frame, pixels, channels).astype(jnp.float32), gain)
        for g in range(groups):
            normed_ref[g, j] = normed[g * SUB : (g + 1) * SUB]
    step = up(channels, LANES)
    rows = normed_ref[...].reshape(groups * slots * SUB, channels).astype(jnp.bfloat16)
    pairs = jnp.dot(rows, tw_ref[:, step:], preferred_element_type=jnp.float32).astype(jnp.bfloat16)

    own, more = frames * SUB, slots * SUB
    shape = (own, own + more)
    row = lax.broadcasted_iota(jnp.int32, shape, 0)
    column = lax.broadcasted_iota(jnp.int32, shape, 1)
    usable = lax.rem(row, SUB) == lax.rem(column, SUB)
    slot = column // SUB - frames
    usable &= (slot < 0) | (slot >= HALO) | inner_there
    usable &= (slot < HALO) | (slot >= 2 * HALO) | outer_there
    bias = jnp.where(usable, 0.0, NEG).astype(jnp.float32)

    for g in range(groups):
        for start, width in tiles_of(channels):
            span = slice(start, start + width)
            keys = jnp.concatenate(
                [k_ref[g * own : (g + 1) * own, span], pairs[g * more : (g + 1) * more, span]], axis=0
            )
            values = jnp.concatenate(
                [
                    v_ref[g * own : (g + 1) * own, span],
                    pairs[g * more : (g + 1) * more, step + start : step + start + width],
                ],
                axis=0,
            )
            att_ref[g * own : (g + 1) * own, span] = attend(
                q_ref[g * own : (g + 1) * own, span], keys, values, bias
            )
    update = jnp.dot(att_ref[...], to_ref[...], preferred_element_type=jnp.float32)
    for g in range(groups):
        for f in range(frames):
            first = (g * frames + f) * SUB
            rows_ref[f, g * SUB : (g + 1) * SUB] = xg_ref[g, f] + update[first : first + SUB]
    place = lax.axis_index("pix")
    per_device = sends[0].shape[0]
    for k, ref in enumerate(sends):
        target = jnp.bitwise_xor(place, k)
        for i in range(per_device):
            ref[i] = pack(rows_ref[target * per_device + i].astype(jnp.bfloat16))


def temporal(parts, gain, weights, out_matrix, e, o, picks, clips, gathered, far_steps, pix_count):
    q, k, v, xg = parts
    groups, frames, _, channels = xg.shape
    pixels = groups * SUB
    slots = 2 * HALO + clips
    count = frames * pixels
    kind = q.dtype
    dense = (pixels * channels // LANES, LANES)
    return pl.pallas_call(
        functools.partial(temporal_kernel, clips, gathered, far_steps, pix_count),
        out_shape=[pltpu.VMEM((frames // pix_count,) + dense, kind)] * pix_count,
        in_specs=[VMEM] * 4 + [pl.BlockSpec()] + [VMEM] * (4 + len(picks)),
        out_specs=[VMEM] * pix_count,
        scratch_shapes=[
            pltpu.VMEM((groups, slots, SUB, channels), jnp.float32),
            pltpu.VMEM((count, channels), kind),
            pltpu.VMEM((frames, pixels, channels), jnp.float32),
        ],
        cost_estimate=pl.CostEstimate(
            flops=2 * count * channels * 4 * channels, bytes_accessed=8 << 20, transcendentals=0
        ),
        compiler_params=pltpu.CompilerParams(vmem_limit_bytes=LIMIT),
        name="temporal",
    )(q, k, v, xg, gain.reshape(1, channels), weights, out_matrix, e, o, *picks)


def spatial_kernel(pix_count, gain_ref, sw_ref, so_ref, *rest):
    chunks, out_ref, att_ref = rest[:pix_count], rest[pix_count], rest[pix_count + 1]
    per_device, pixels, channels = out_ref.shape
    each = pixels // pix_count
    step = up(channels, LANES)
    place = lax.axis_index("pix")
    gain = gain_ref[...]
    for i in range(per_device):
        rows = jnp.concatenate(
            [unpack(ref[i], each, channels) for ref in chunks], axis=0
        ).astype(jnp.float32)
        normed = layer_norm(rows, gain).astype(jnp.bfloat16)
        packed = jnp.dot(normed, sw_ref[...], preferred_element_type=jnp.float32).astype(jnp.bfloat16)
        for start, width in tiles_of(channels):
            att_ref[i, :, start : start + width] = attend(
                packed[:, start : start + width],
                packed[:, step + start : step + start + width],
                packed[:, 2 * step + start : 2 * step + start + width],
                None,
            )
        update = jnp.dot(att_ref[i], so_ref[...], preferred_element_type=jnp.float32)
        result = (rows + update).astype(jnp.bfloat16)
        for k in range(pix_count):
            first = pl.multiple_of(jnp.bitwise_xor(place, k) * each, each)
            out_ref[i, pl.ds(first, each), :] = result[k * each : (k + 1) * each]


def spatial(gain, weights, out_matrix, chunks, pixels):
    pix_count = len(chunks)
    per_device = chunks[0].shape[0]
    channels = out_matrix.shape[0]
    kind = chunks[0].dtype
    shape = (per_device, pixels, channels)
    return pl.pallas_call(
        functools.partial(spatial_kernel, pix_count),
        out_shape=jax.ShapeDtypeStruct(shape, kind),
        in_specs=[pl.BlockSpec()] + [VMEM] * (2 + pix_count),
        out_specs=pl.BlockSpec(),
        scratch_shapes=[pltpu.VMEM(shape, kind)],
        cost_estimate=pl.CostEstimate(
            flops=2 * per_device * pixels * channels * (4 * channels + 2 * pixels),
            bytes_accessed=4 << 20,
            transcendentals=0,
        ),
        compiler_params=pltpu.CompilerParams(vmem_limit_bytes=LIMIT),
        name="spatial",
    )(gain.reshape(1, channels), weights, out_matrix, *chunks)


def both_ways(pairs):
    return [pair for a, b in pairs for pair in ((a, b), (b, a))]


def body(
    latents,
    sampled,
    temporal_gain,
    temporal_qkv,
    temporal_out,
    spatial_gain,
    spatial_qkv,
    spatial_out,
):
    clips, pix_count = lax.axis_size("clip"), lax.axis_size("pix")
    pixels = latents.shape[1] * pix_count
    gathered = clips > DIRECT_CLIPS or clips & (clips - 1) != 0
    x, e, o, p = prep(latents, sampled, not gathered)
    picks, far_steps = [], ()
    if gathered:
        picks = [lax.all_gather(p, "clip", axis=0, tiled=True)]
    else:
        picks = [p]
        far_steps = tuple(range(2, clips))
        for step in far_steps:
            far = [(a, a ^ step) for a in range(clips) if (a ^ step) - a > 1]
            picks.append(lax.ppermute(p, "clip", both_ways(far)))
    e = lax.ppermute(e, "clip", both_ways([(a, a + 1) for a in range(0, clips - 1, 2)]))
    o = lax.ppermute(o, "clip", both_ways([(a, a + 1) for a in range(1, clips - 1, 2)]))
    q, k, v, xg, tw, sw, to, so = local(
        x, temporal_gain, temporal_qkv, temporal_out, spatial_qkv, spatial_out
    )
    sends = temporal(
        (q, k, v, xg), temporal_gain, tw, to, e, o, picks, clips, gathered, far_steps, pix_count
    )
    chunks = [sends[0]]
    for step in range(1, pix_count):
        chunks.append(
            lax.ppermute(sends[step], "pix", [(a, a ^ step) for a in range(pix_count)])
        )
    return spatial(spatial_gain, sw, so, chunks, pixels)


def solution(mesh):
    placed = (P(("group", "clip"), "pix", None), P(("group", "clip")), P(), P(), P(), P(), P(), P())
    return jax.shard_map(
        body,
        mesh=mesh,
        in_specs=placed,
        out_specs=P(("group", "clip", "pix"), None, None),
        check_vma=False,
    )
```

time: 77.9 us -> 36.3 us (0.47)
  blocking collectives: 16.6 us -> 0 us
  matrix products: 14.3 us -> 0 us
  local copies, waits for them, and re-layouts: 18.6 us -> 5.03 us
  Pallas kernels: 0 us -> 11.3 us
  other arithmetic: 9.49 us -> 0 us
  starting transfers between devices: 9.71 us -> 14.4 us
  waiting for transfers between devices: 7.37 us -> 4.45 us
    all_gather x1 -> x0, blocking collectives: 16.6 us -> none  [body(): lax.all_gather(picked, 'clip', axis=0, tiled=True)]
    reshape x7 -> x2, local copies, waits for them, and re-layouts: 13.1 us -> 0.01 us  [the longest x1 0.01 us: local(): gain.reshape(1, channels)]
    dot_general x29 -> x0, matrix products: 12 us -> none  [the longest x3 2.88 us: project(): jnp.dot(flat, matrix, preferred_element_type=jnp.float32)]
    pallas_call x0 -> x4, Pallas kernels: none -> 11.3 us  [the longest x1 5.35 us: temporal(): pl.pallas_call(functools.partial(temporal_kernel, clips, gathered, far_st...]
    ppermute x2 -> x7, starting transfers between devices: 6.25 us -> 14.4 us  [the longest x2 8.71 us: body(): picks.append(lax.ppermute(p, 'clip', both_ways(far)))]
    all_to_all x1 -> x0, waiting for transfers between devices: 7.37 us -> none  [body(): lax.all_to_all(grouped, 'pix', split_axis=0, concat_axis=2, tiled=True)[0]]
    concatenate x2 -> x0, other arithmetic: 4.73 us -> none  [the longest x1 3.64 us: body(): jnp.concatenate([border, global_pairs], 0)]
    ppermute x2 -> x7, waiting for transfers between devices: 0.01 us -> 4.45 us  [the longest x3 4.44 us: body(): lax.ppermute(sends[step], 'pix', [(a, a ^ step) for a in range(pix_count)])]
  transfers between devices with their start and end apart: 3 -> 7, of which waited for: 1 -> 2; matrix products, arithmetic and copies ran while one was open for 5% -> 0% of each run, Pallas kernels for 0% -> 7%
where the time goes in v1:
time: 36.3 us; the launch traced here: 36 us
  starting transfers between devices  14.4 us (40%)
  Pallas kernels  11.3 us (31%)
  local copies, waits for them, and re-layouts  5.03 us (14%)
  waiting for transfers between devices  4.45 us (12%)
  between operations  0.8 us (2%)
    ppermute x2, starting transfers between devices, body(): picks.append(lax.ppermute(p, 'clip', both_ways(far)))  8.71 us
    pallas_call x1, Pallas kernels, temporal(): pl.pallas_call(functools.partial(temporal_kernel, clips, gathered, far_st...  5.35 us
    ppermute x3, waiting for transfers between devices, body(): lax.ppermute(sends[step], 'pix', [(a, a ^ step) for a in range(pix_count)])  4.44 us
    unnamed x14, local copies, waits for them, and re-layouts  4.12 us
    ppermute x1, starting transfers between devices, body(): lax.ppermute(e, 'clip', both_ways([(a, a + 1) for a in range(0, clips - 1...  3.12 us
    pallas_call x1, Pallas kernels, spatial(): pl.pallas_call(functools.partial(spatial_kernel, pix_count), out_shape=ja...  2.61 us
    pallas_call x1, Pallas kernels, local(): pl.pallas_call(local_kernel, out_shape=[pltpu.VMEM((count, channels), kin...  2.52 us
    ppermute x3, starting transfers between devices, body(): lax.ppermute(sends[step], 'pix', [(a, a ^ step) for a in range(pix_count)])  1.92 us
  transfers between devices with their start and end apart: 7, of which 2 were waited for; matrix products, arithmetic and copies ran while one was open for 0% of the time, Pallas kernels for 7%

profile of v1, /device:TPU:0, one launch (start us, length us, event | category | flops | bytes accessed | tf_op | source)
XLA Modules:
  0.0 36.0 jit_solution(4479030930226737763)
XLA Ops:
  0.7 0.0 copy-start.2
  0.7 1.0 %copy-done.2 = bf16[8,64,320]{2,1,0:T(8,128)(2,1)S(1)} copy-done((bf16[8,64,320]{2,1,0:T(8,128)(2,1)S(1)}, bf16[8,64,320]{2,1,0:T(8,128)(2,1)}, u32[]{:S(2)}) %copy-start.2) | copy-done | bytes 327704
  1.6 0.0 copy-start.3
  1.7 0.9 %prep.1 = (bf16[8,64,320]{2,1,0:T(8,128)(2,1)S(1)}, bf16[5,160,128]{2,1,0:T(8,128)(2,1)S(1)}, bf16[5,160,128]{2,1,0:T(8,128)(2,1)S(1)}, bf16[1,160,128]{2,1,0:T(8,128)(2,1)S(1)}) custom-call(bf16[8,64,320]{2,1,0:T(8,128)(2,1)S(1)} %copy-done.2, s32[1]{0:T(128)S(6)} %copy.10.s_hbm), custom_call_target="tpu_custom_call" | custom-call | tf_op jit(solution)/shard_map/prep/pallas_call | solution.py:110
  2.5 0.0 copy-start.5
  2.5 3.1 %collective-permute-start = (bf16[5,160,128]{2,1,0:T(8,128)(2,1)S(1)}, bf16[5,160,128]{2,1,0:T(8,128)(2,1)S(1)}, u32[]{:S(2)}, u32[]{:S(2)}) collective-permute-start(bf16[5,160,128]{2,1,0:T(8,128)(2,1)S(1)} %get-tuple-element.30), channel_id=1, source_target_pairs={{0,4},{4,0},{8,12},{12,8},{1,5},{5,1},{9,13},{13,9},{2,6},{6,2},{1... | collective-permute-start | bytes 614408 | tf_op jit(solution)/shard_map/ppermute | solution.py:378
  5.7 0.7 %collective-permute-start.1 = (bf16[5,160,128]{2,1,0:T(8,128)(2,1)S(1)}, bf16[5,160,128]{2,1,0:T(8,128)(2,1)S(1)}, u32[]{:S(2)}, u32[]{:S(2)}) collective-permute-start(bf16[5,160,128]{2,1,0:T(8,128)(2,1)S(1)} %get-tuple-element.31), channel_id=1, source_target_pairs={{4,8},{8,4},{5,9},{9,5},{6,10},{10,6},{7,11},{11,7},{20,24},{24,20... | collective-permute-start | bytes 614408 | tf_op jit(solution)/shard_map/ppermute | solution.py:379
  6.3 3.9 %collective-permute-start.2 = (bf16[1,160,128]{2,1,0:T(8,128)(2,1)S(1)}, bf16[1,160,128]{2,1,0:T(8,128)(2,1)S(1)}, u32[]{:S(2)}, u32[]{:S(2)}) collective-permute-start(bf16[1,160,128]{2,1,0:T(8,128)(2,1)S(1)} %get-tuple-element.32.rest_0_), channel_id=1, source_target_pairs={{0,8},{8,0},{4,12},{12,4},{1,9},{9,1},{5,13},{13,5},{2,10},{10,2},... | collective-permute-start | bytes 122888 | tf_op jit(solution)/shard_map/ppermute | solution.py:377
  10.2 4.8 %collective-permute-start.3 = (bf16[1,160,128]{2,1,0:T(8,128)(2,1)S(1)}, bf16[1,160,128]{2,1,0:T(8,128)(2,1)S(1)}, u32[]{:S(2)}, u32[]{:S(2)}) collective-permute-start(bf16[1,160,128]{2,1,0:T(8,128)(2,1)S(1)} %get-tuple-element.32.rest_0_), channel_id=1, source_target_pairs={{0,12},{12,0},{1,13},{13,1},{2,14},{14,2},{3,15},{15,3},{16,28},{2... | collective-permute-start | bytes 122888 | tf_op jit(solution)/shard_map/ppermute | solution.py:377
  15.0 0.0 copy-done.5
  15.1 0.0 copy-done.3
  15.1 0.0 copy-start
  15.1 1.1 %copy-done = bf16[320,960]{1,0:T(8,128)(2,1)S(1)} copy-done((bf16[320,960]{1,0:T(8,128)(2,1)S(1)}, bf16[320,960]{1,0:T(8,128)(2,1)}, u32[]{:S(2)}) %copy-start) | copy-done | bytes 614424
  16.2 0.0 copy-start.1
  16.2 1.1 %copy-done.1 = bf16[320,960]{1,0:T(8,128)(2,1)S(1)} copy-done((bf16[320,960]{1,0:T(8,128)(2,1)S(1)}, bf16[320,960]{1,0:T(8,128)(2,1)}, u32[]{:S(2)}) %copy-start.1) | copy-done | bytes 614424
  17.3 0.0 copy-start.4
  17.3 0.9 %copy-done.4 = bf16[320,320]{1,0:T(8,128)(2,1)S(1)} copy-done((bf16[320,320]{1,0:T(8,128)(2,1)S(1)}, bf16[320,320]{1,0:T(8,128)(2,1)}, u32[]{:S(2)}) %copy-start.4) | copy-done | bytes 204824
  18.2 2.5 %local.1 = (bf16[512,320]{1,0:T(8,128)(2,1)S(1)}, bf16[512,320]{1,0:T(8,128)(2,1)S(1)}, bf16[512,320]{1,0:T(8,128)(2,1)S(1)}, f32[8,8,8,320]{3,2,1,0:T(8,128)S(1...) custom-call(bf16[8,64,320]{2,1,0:T(8,128)(2,1)S(1)} %get-tuple-eleme, ...), custom_call_target="tpu_custom_call" | custom-call | flops 314572800 | bytes 4194304 | tf_op jit(solution)/shard_map/local/pallas_call | solution.py:178
  20.7 0.0 collective-permute-done.2.rest_1_
  20.7 0.0 collective-permute-done.3.rest_2_
  20.7 0.0 collective-permute-done.e_ref
  20.8 0.0 collective-permute-done.1.o_ref
  20.8 5.3 %temporal.1 = (bf16[2,160,128]{2,1,0:T(8,128)(2,1)S(1)}, bf16[2,160,128]{2,1,0:T(8,128)(2,1)S(1)}, bf16[2,160,128]{2,1,0:T(8,128)(2,1)S(1)}, bf16[2,160,128]{2,1,0:T(8,128)(2,1)S(1)}) custom-call(bf16[512,320]{1,0:T(8,128)(2,1)S(1)} %get-tuple-element.24.q_ref, bf16[512,320]{1,0:T(8,128)(2,1)S(1)} %get-tuple-element.25.k_ref, ...), custom_call_target="tpu_custom_call" | custom-call | flops 419430400 | bytes 8388608 | tf_op jit(solution)/shard_map/temporal/pallas_call | solution.py:284
  26.1 0.0 copy-start.6
  26.1 0.1 collective-permute-start.4
  26.2 1.6 %collective-permute-start.5 = (bf16[2,160,128]{2,1,0:T(8,128)(2,1)S(1)}, bf16[2,160,128]{2,1,0:T(8,128)(2,1)S(1)}, u32[]{:S(2)}, u32[]{:S(2)}) collective-permute-start(bf16[2,160,128]{2,1,0:T(8,128)(2,1)S(1)} %get-tuple-element.35), channel_id=1, source_target_pairs={{0,2},{1,3},{2,0},{3,1},{4,6},{5,7},{6,4},{7,5},{8,10},{9,11},{10,... | collective-permute-start | bytes 245768 | tf_op jit(solution)/shard_map/ppermute | solution.py:389
  27.8 0.3 collective-permute-start.6
  28.1 0.0 copy-done.6
  28.1 0.0 collective-permute-done.4.rest_1_
  28.1 3.3 %collective-permute-done.5.rest_2_ = bf16[2,160,128]{2,1,0:T(8,128)(2,1)S(1)} collective-permute-done((bf16[2,160,128]{2,1,0:T(8,128)(2,1)S(1)}, bf16[2,160,128]{2,1,0:T(8,128)(2,1)S(1)}, u32[]{:S(2)}, u32[]{:S(2)}) %collective-permute-start.5) | collective-permute-done | bytes 81952 | tf_op jit(solution)/shard_map/ppermute | solution.py:389
  31.4 1.2 %collective-permute-done.6.rest_3_ = bf16[2,160,128]{2,1,0:T(8,128)(2,1)S(1)} collective-permute-done((bf16[2,160,128]{2,1,0:T(8,128)(2,1)S(1)}, bf16[2,160,128]{2,1,0:T(8,128)(2,1)S(1)}, u32[]{:S(2)}, u32[]{:S(2)}) %collective-permute-start.6) | collective-permute-done | bytes 81952 | tf_op jit(solution)/shard_map/ppermute | solution.py:389
  32.5 2.6 %spatial.1 = bf16[2,256,320]{2,1,0:T(8,128)(2,1)S(1)} custom-call(f32[1,320]{1,0:T(1,128)S(1)} %reshape.7.gain_ref, bf16[320,1152]{1,0:T(8,128)(2,1)S(1)} %get-tuple-element.22.sw_ref, bf16[320,320]{1,0:T(8,128)(2,1)S(1)} %get-tuple-element.23.so_ref, bf16[2,160,128]{2,1,0:T(8,128)(2,1)S(1)} %get-tuple-element.33.rest_0_, ...), custom_call_target="tpu_custom_call" | custom-call | flops 587202560 | bytes 4194304 | tf_op jit(solution)/shard_map/spatial/pallas_call | solution.py:335
  35.1 0.9 %copy.9 = bf16[2,256,320]{1,2,0:T(8,128)(2,1)} copy(bf16[2,256,320]{2,1,0:T(8,128)(2,1)S(1)} %spatial.1) | data formatting | bytes 655360 | tf_op jit(solution)/shard_map/spatial/pallas_call | solution.py:335
  (2 shorter events, 0.0 us)
Async XLA Ops:
  0.7 1.0 %copy-start.2 = (bf16[8,64,320]{2,1,0:T(8,128)(2,1)S(1)}, bf16[8,64,320]{2,1,0:T(8,128)(2,1)}, u32[]{:S(2)}) copy-start(bf16[8,64,320]{2,1,0:T(8,128)(2,1)} %x_hbm.1) | copy-start | bytes 983044
  1.6 13.4 %copy-start.3 = (bf16[320,320]{1,0:T(8,128)(2,1)S(1)}, bf16[320,320]{1,0:T(8,128)(2,1)}, u32[]{:S(2)}) copy-start(bf16[320,320]{1,0:T(8,128)(2,1)} %to_hbm.1) | copy-start | bytes 614404
  2.5 12.5 %copy-start.5 = (f32[320]{0:T(512)S(1)}, f32[320]{0:T(512)}, u32[]{:S(2)}) copy-start(f32[320]{0:T(512)} %param.10) | copy-start | bytes 3844
  2.5 18.2 %collective-permute-start = (bf16[5,160,128]{2,1,0:T(8,128)(2,1)S(1)}, bf16[5,160,128]{2,1,0:T(8,128)(2,1)S(1)}, u32[]{:S(2)}, u32[]{:S(2)}) collective-permute-start(bf16[5,160,128]{2,1,0:T(8,128)(2,1)S(1)} %get-tuple-element.30), channel_id=1, source_target_pairs={{0,4},{4,0},{8,12},{12,8},{1,5},{5,1},{9,13},{13,9},{2,6},{6,2},{1... | collective-permute-start | bytes 614408 | tf_op jit(solution)/shard_map/ppermute | solution.py:378
  5.7 15.1 %collective-permute-start.1 = (bf16[5,160,128]{2,1,0:T(8,128)(2,1)S(1)}, bf16[5,160,128]{2,1,0:T(8,128)(2,1)S(1)}, u32[]{:S(2)}, u32[]{:S(2)}) collective-permute-start(bf16[5,160,128]{2,1,0:T(8,128)(2,1)S(1)} %get-tuple-element.31), channel_id=1, source_target_pairs={{4,8},{8,4},{5,9},{9,5},{6,10},{10,6},{7,11},{11,7},{20,24},{24,20... | collective-permute-start | bytes 614408 | tf_op jit(solution)/shard_map/ppermute | solution.py:379
  6.3 14.4 %collective-permute-start.2 = (bf16[1,160,128]{2,1,0:T(8,128)(2,1)S(1)}, bf16[1,160,128]{2,1,0:T(8,128)(2,1)S(1)}, u32[]{:S(2)}, u32[]{:S(2)}) collective-permute-start(bf16[1,160,128]{2,1,0:T(8,128)(2,1)S(1)} %get-tuple-element.32.rest_0_), channel_id=1, source_target_pairs={{0,8},{8,0},{4,12},{12,4},{1,9},{9,1},{5,13},{13,5},{2,10},{10,2},... | collective-permute-start | bytes 122888 | tf_op jit(solution)/shard_map/ppermute | solution.py:377
  10.2 10.5 %collective-permute-start.3 = (bf16[1,160,128]{2,1,0:T(8,128)(2,1)S(1)}, bf16[1,160,128]{2,1,0:T(8,128)(2,1)S(1)}, u32[]{:S(2)}, u32[]{:S(2)}) collective-permute-start(bf16[1,160,128]{2,1,0:T(8,128)(2,1)S(1)} %get-tuple-element.32.rest_0_), channel_id=1, source_target_pairs={{0,12},{12,0},{1,13},{13,1},{2,14},{14,2},{3,15},{15,3},{16,28},{2... | collective-permute-start | bytes 122888 | tf_op jit(solution)/shard_map/ppermute | solution.py:377
  15.1 1.1 %copy-start = (bf16[320,960]{1,0:T(8,128)(2,1)S(1)}, bf16[320,960]{1,0:T(8,128)(2,1)}, u32[]{:S(2)}) copy-start(bf16[320,960]{1,0:T(8,128)(2,1)} %tq_hbm.1) | copy-start | bytes 1843204
  16.2 1.1 %copy-start.1 = (bf16[320,960]{1,0:T(8,128)(2,1)S(1)}, bf16[320,960]{1,0:T(8,128)(2,1)}, u32[]{:S(2)}) copy-start(bf16[320,960]{1,0:T(8,128)(2,1)} %sq_hbm.1) | copy-start | bytes 1843204
  17.3 0.9 %copy-start.4 = (bf16[320,320]{1,0:T(8,128)(2,1)S(1)}, bf16[320,320]{1,0:T(8,128)(2,1)}, u32[]{:S(2)}) copy-start(bf16[320,320]{1,0:T(8,128)(2,1)} %so_hbm.1) | copy-start | bytes 614404
  26.1 1.9 %copy-start.6 = (f32[320]{0:T(512)S(1)}, f32[320]{0:T(512)}, u32[]{:S(2)}) copy-start(f32[320]{0:T(512)} %param.13) | copy-start | bytes 3844
  26.1 1.9 %collective-permute-start.4 = (bf16[2,160,128]{2,1,0:T(8,128)(2,1)S(1)}, bf16[2,160,128]{2,1,0:T(8,128)(2,1)S(1)}, u32[]{:S(2)}, u32[]{:S(2)}) collective-permute-start(bf16[2,160,128]{2,1,0:T(8,128)(2,1)S(1)} %get-tuple-element.34), channel_id=1, source_target_pairs={{0,1},{1,0},{2,3},{3,2},{4,5},{5,4},{6,7},{7,6},{8,9},{9,8},{10,11... | collective-permute-start | bytes 245768 | tf_op jit(solution)/shard_map/ppermute | solution.py:389
  26.2 5.1 %collective-permute-start.5 = (bf16[2,160,128]{2,1,0:T(8,128)(2,1)S(1)}, bf16[2,160,128]{2,1,0:T(8,128)(2,1)S(1)}, u32[]{:S(2)}, u32[]{:S(2)}) collective-permute-start(bf16[2,160,128]{2,1,0:T(8,128)(2,1)S(1)} %get-tuple-element.35), channel_id=1, source_target_pairs={{0,2},{1,3},{2,0},{3,1},{4,6},{5,7},{6,4},{7,5},{8,10},{9,11},{10,... | collective-permute-start | bytes 245768 | tf_op jit(solution)/shard_map/ppermute | solution.py:389
  27.8 4.7 %collective-permute-start.6 = (bf16[2,160,128]{2,1,0:T(8,128)(2,1)S(1)}, bf16[2,160,128]{2,1,0:T(8,128)(2,1)S(1)}, u32[]{:S(2)}, u32[]{:S(2)}) collective-permute-start(bf16[2,160,128]{2,1,0:T(8,128)(2,1)S(1)} %get-tuple-element.36), channel_id=1, source_target_pairs={{0,3},{1,2},{2,1},{3,0},{4,7},{5,6},{6,5},{7,4},{8,11},{9,10},{10,... | collective-permute-start | bytes 245768 | tf_op jit(solution)/shard_map/ppermute | solution.py:389

commit v2 on v1

--- a/solution.py
+++ b/solution.py
@@ -16,9 +16,13 @@
 NEG = -1e30
 DIRECT_CLIPS = 4
 LIMIT = 24 << 20
-ANY = pl.BlockSpec(memory_space=pl.ANY)
+FAR = pl.BlockSpec(memory_space=pltpu.HBM)
 VMEM = pl.BlockSpec(memory_space=pltpu.VMEM)
 NT = (((1,), (1,)), ((), ()))
+
+
+def far(array):
+    return pltpu.with_memory_space_constraint(array, pltpu.HBM)
 
 
 def up(count, step):
@@ -83,12 +87,9 @@
     return result.astype(jnp.bfloat16)
 
 
-def prep_kernel(border, axis, x_hbm, s_hbm, x_ref, e_ref, o_ref, p_ref, s_ref, x_sem, s_sem):
+def prep_kernel(border, axis, x_hbm, s_ref, x_ref, e_ref, o_ref, p_ref, x_sem):
     copy_x = pltpu.make_async_copy(x_hbm, x_ref, x_sem)
-    copy_s = pltpu.make_async_copy(s_hbm, s_ref, s_sem)
     copy_x.start()
-    copy_s.start()
-    copy_s.wait()
     copy_x.wait()
     odd = lax.rem(lax.axis_index(axis), 2)
     frames = x_ref.shape[0]
@@ -115,16 +116,14 @@
             pltpu.VMEM((sent,) + dense, kind),
             pltpu.VMEM((1,) + dense, kind),
         ],
-        in_specs=[ANY, ANY],
+        in_specs=[FAR, pl.BlockSpec(memory_space=pltpu.SMEM)],
         out_specs=[VMEM] * 4,
         scratch_shapes=[
-            pltpu.SMEM((1,), jnp.int32),
-            pltpu.SemaphoreType.DMA,
             pltpu.SemaphoreType.DMA,
         ],
         compiler_params=pltpu.CompilerParams(vmem_limit_bytes=LIMIT),
         name="prep",
-    )(latents, sampled)
+    )(far(latents), sampled)
 
 
 def local_kernel(
@@ -181,7 +180,7 @@
         + [pltpu.VMEM((pixels // SUB, frames, SUB, channels), jnp.float32)]
         + [pltpu.VMEM(wide, kind)] * 2
         + [pltpu.VMEM((channels, channels), kind)] * 2,
-        in_specs=[VMEM, pl.BlockSpec()] + [ANY] * 4,
+        in_specs=[VMEM, pl.BlockSpec()] + [FAR] * 4,
         out_specs=[VMEM] * 8,
         scratch_shapes=[
             pltpu.VMEM(temporal_qkv.shape, kind),
@@ -194,7 +193,11 @@
         ),
         compiler_params=pltpu.CompilerParams(vmem_limit_bytes=LIMIT),
         name="local",
-    )(latents, gain.reshape(1, channels), temporal_qkv, temporal_out, spatial_qkv, spatial_out)
+    )(
+        latents,
+        gain.reshape(1, channels),
+        *(far(w) for w in (temporal_qkv, temporal_out, spatial_qkv, spatial_out)),
+    )
 
 
 def temporal_kernel(
@@ -373,8 +376,8 @@
         picks = [p]
         far_steps = tuple(range(2, clips))
         for step in far_steps:
-            far = [(a, a ^ step) for a in range(clips) if (a ^ step) - a > 1]
-            picks.append(lax.ppermute(p, "clip", both_ways(far)))
+            distant = [(a, a ^ step) for a in range(clips) if (a ^ step) - a > 1]
+            picks.append(lax.ppermute(p, "clip", both_ways(distant)))
     e = lax.ppermute(e, "clip", both_ways([(a, a + 1) for a in range(0, clips - 1, 2)]))
     o = lax.ppermute(o, "clip", both_ways([(a, a + 1) for a in range(1, clips - 1, 2)]))
     q, k, v, xg, tw, sw, to, so = local(

time: 36.3 us -> 32.6 us (0.90)
  local copies, waits for them, and re-layouts: 5.03 us -> 0.93 us
  waiting for transfers between devices: 4.45 us -> 4.98 us
    unnamed x14 -> x4, local copies, waits for them, and re-layouts: 4.12 us -> 0.01 us
    ppermute x2, waiting for transfers between devices: 0.01 us -> 0.54 us  [body(): picks.append(lax.ppermute(p, 'clip', both_ways(distant)))]
  transfers between devices with their start and end apart: 7 -> 7, of which waited for: 2 -> 3; matrix products, arithmetic and copies ran while one was open for 0% -> 0% of each run, Pallas kernels for 7% -> 7%
where the time goes in v2:
time: 32.6 us; the launch traced here: 32.4 us
  starting transfers between devices  14.4 us (44%)
  Pallas kernels  11.4 us (35%)
  waiting for transfers between devices  4.98 us (15%)
  local copies, waits for them, and re-layouts  0.93 us (3%)
  between operations  0.75 us (2%)
    ppermute x2, starting transfers between devices, body(): picks.append(lax.ppermute(p, 'clip', both_ways(distant)))  8.71 us
    pallas_call x1, Pallas kernels, temporal(): pl.pallas_call(functools.partial(temporal_kernel, clips, gathered, far_st...  5.34 us
    ppermute x3, waiting for transfers between devices, body(): lax.ppermute(sends[step], 'pix', [(a, a ^ step) for a in range(pix_count)])  4.44 us
    ppermute x1, starting transfers between devices, body(): lax.ppermute(e, 'clip', both_ways([(a, a + 1) for a in range(0, clips - 1...  3.12 us
    pallas_call x1, Pallas kernels, spatial(): pl.pallas_call(functools.partial(spatial_kernel, pix_count), out_shape=ja...  2.61 us
    pallas_call x1, Pallas kernels, local(): pl.pallas_call(local_kernel, out_shape=[pltpu.VMEM((count, channels), kin...  2.29 us
    ppermute x3, starting transfers between devices, body(): lax.ppermute(sends[step], 'pix', [(a, a ^ step) for a in range(pix_count)])  1.92 us
    pallas_call x1, Pallas kernels, prep(): pl.pallas_call(functools.partial(prep_kernel, HALO, 'clip'), out_shape=[p...  1.12 us
  transfers between devices with their start and end apart: 7, of which 3 were waited for; matrix products, arithmetic and copies ran while one was open for 0% of the time, Pallas kernels for 7%

profile of v2, /device:TPU:0, one launch (start us, length us, event | category | flops | bytes accessed | tf_op | source)
XLA Modules:
  0.0 32.4 jit_solution(8591485336106581560)
XLA Ops:
  0.7 1.1 %prep.1 = (bf16[8,64,320]{2,1,0:T(8,128)(2,1)S(1)}, bf16[5,160,128]{2,1,0:T(8,128)(2,1)S(1)}, bf16[5,160,128]{2,1,0:T(8,128)(2,1)S(1)}, bf16[1,160,128]{2,1,0:T(8,128)(2,1)S(1)}) custom-call(bf16[8,64,320]{2,1,0:T(8,128)(2,1)} %x_hbm.1, s32[1]{0:T(128)S(6)} %copy.10.s_ref), custom_call_target="tpu_custom_call" | custom-call | tf_op jit(solution)/shard_map/prep/pallas_call | solution.py:111
  1.8 0.0 copy-start
  1.8 3.1 %collective-permute-start = (bf16[5,160,128]{2,1,0:T(8,128)(2,1)S(1)}, bf16[5,160,128]{2,1,0:T(8,128)(2,1)S(1)}, u32[]{:S(2)}, u32[]{:S(2)}) collective-permute-start(bf16[5,160,128]{2,1,0:T(8,128)(2,1)S(1)} %get-tuple-element.30), channel_id=1, source_target_pairs={{0,4},{4,0},{8,12},{12,8},{1,5},{5,1},{9,13},{13,9},{2,6},{6,2},{1... | collective-permute-start | bytes 614408 | tf_op jit(solution)/shard_map/ppermute | solution.py:381
  4.9 0.7 %collective-permute-start.1 = (bf16[5,160,128]{2,1,0:T(8,128)(2,1)S(1)}, bf16[5,160,128]{2,1,0:T(8,128)(2,1)S(1)}, u32[]{:S(2)}, u32[]{:S(2)}) collective-permute-start(bf16[5,160,128]{2,1,0:T(8,128)(2,1)S(1)} %get-tuple-element.31), channel_id=1, source_target_pairs={{4,8},{8,4},{5,9},{9,5},{6,10},{10,6},{7,11},{11,7},{20,24},{24,20... | collective-permute-start | bytes 614408 | tf_op jit(solution)/shard_map/ppermute | solution.py:382
  5.6 3.9 %collective-permute-start.2 = (bf16[1,160,128]{2,1,0:T(8,128)(2,1)S(1)}, bf16[1,160,128]{2,1,0:T(8,128)(2,1)S(1)}, u32[]{:S(2)}, u32[]{:S(2)}) collective-permute-start(bf16[1,160,128]{2,1,0:T(8,128)(2,1)S(1)} %get-tuple-element.32.rest_0_), channel_id=1, source_target_pairs={{0,8},{8,0},{4,12},{12,4},{1,9},{9,1},{5,13},{13,5},{2,10},{10,2},... | collective-permute-start | bytes 122888 | tf_op jit(solution)/shard_map/ppermute | solution.py:380
  9.5 4.8 %collective-permute-start.3 = (bf16[1,160,128]{2,1,0:T(8,128)(2,1)S(1)}, bf16[1,160,128]{2,1,0:T(8,128)(2,1)S(1)}, u32[]{:S(2)}, u32[]{:S(2)}) collective-permute-start(bf16[1,160,128]{2,1,0:T(8,128)(2,1)S(1)} %get-tuple-element.32.rest_0_), channel_id=1, source_target_pairs={{0,12},{12,0},{1,13},{13,1},{2,14},{14,2},{3,15},{15,3},{16,28},{2... | collective-permute-start | bytes 122888 | tf_op jit(solution)/shard_map/ppermute | solution.py:380
  14.3 0.0 copy-done
  14.3 2.3 %local.1 = (bf16[512,320]{1,0:T(8,128)(2,1)S(1)}, bf16[512,320]{1,0:T(8,128)(2,1)S(1)}, bf16[512,320]{1,0:T(8,128)(2,1)S(1)}, f32[8,8,8,320]{3,2,1,0:T(8,128)S(1...) custom-call(bf16[8,64,320]{2,1,0:T(8,128)(2,1)S(1)} %get-tuple-eleme, ...), custom_call_target="tpu_custom_call" | custom-call | flops 314572800 | bytes 4194304 | tf_op jit(solution)/shard_map/local/pallas_call | solution.py:177
  16.6 0.0 collective-permute-done.2.rest_1_
  16.6 0.5 %collective-permute-done.3.rest_2_ = bf16[1,160,128]{2,1,0:T(8,128)(2,1)S(1)} collective-permute-done((bf16[1,160,128]{2,1,0:T(8,128)(2,1)S(1)}, bf16[1,160,128]{2,1,0:T(8,128)(2,1)S(1)}, u32[]{:S(2)}, u32[]{:S(2)}) %collective-permute-start.3) | collective-permute-done | bytes 40992 | tf_op jit(solution)/shard_map/ppermute | solution.py:380
  17.2 0.0 collective-permute-done.e_ref
  17.2 0.0 collective-permute-done.1.o_ref
  17.2 5.3 %temporal.1 = (bf16[2,160,128]{2,1,0:T(8,128)(2,1)S(1)}, bf16[2,160,128]{2,1,0:T(8,128)(2,1)S(1)}, bf16[2,160,128]{2,1,0:T(8,128)(2,1)S(1)}, bf16[2,160,128]{2,1,0:T(8,128)(2,1)S(1)}) custom-call(bf16[512,320]{1,0:T(8,128)(2,1)S(1)} %get-tuple-element.24.q_ref, bf16[512,320]{1,0:T(8,128)(2,1)S(1)} %get-tuple-element.25.k_ref, ...), custom_call_target="tpu_custom_call" | custom-call | flops 419430400 | bytes 8388608 | tf_op jit(solution)/shard_map/temporal/pallas_call | solution.py:287
  22.5 0.0 copy-start.1
  22.5 0.1 collective-permute-start.4
  22.6 1.6 %collective-permute-start.5 = (bf16[2,160,128]{2,1,0:T(8,128)(2,1)S(1)}, bf16[2,160,128]{2,1,0:T(8,128)(2,1)S(1)}, u32[]{:S(2)}, u32[]{:S(2)}) collective-permute-start(bf16[2,160,128]{2,1,0:T(8,128)(2,1)S(1)} %get-tuple-element.35), channel_id=1, source_target_pairs={{0,2},{1,3},{2,0},{3,1},{4,6},{5,7},{6,4},{7,5},{8,10},{9,11},{10,... | collective-permute-start | bytes 245768 | tf_op jit(solution)/shard_map/ppermute | solution.py:392
  24.2 0.3 collective-permute-start.6
  24.5 0.0 copy-done.1
  24.5 0.0 collective-permute-done.4.rest_1_
  24.5 3.3 %collective-permute-done.5.rest_2_ = bf16[2,160,128]{2,1,0:T(8,128)(2,1)S(1)} collective-permute-done((bf16[2,160,128]{2,1,0:T(8,128)(2,1)S(1)}, bf16[2,160,128]{2,1,0:T(8,128)(2,1)S(1)}, u32[]{:S(2)}, u32[]{:S(2)}) %collective-permute-start.5) | collective-permute-done | bytes 81952 | tf_op jit(solution)/shard_map/ppermute | solution.py:392
  27.8 1.1 %collective-permute-done.6.rest_3_ = bf16[2,160,128]{2,1,0:T(8,128)(2,1)S(1)} collective-permute-done((bf16[2,160,128]{2,1,0:T(8,128)(2,1)S(1)}, bf16[2,160,128]{2,1,0:T(8,128)(2,1)S(1)}, u32[]{:S(2)}, u32[]{:S(2)}) %collective-permute-start.6) | collective-permute-done | bytes 81952 | tf_op jit(solution)/shard_map/ppermute | solution.py:392
  28.9 2.6 %spatial.1 = bf16[2,256,320]{2,1,0:T(8,128)(2,1)S(1)} custom-call(f32[1,320]{1,0:T(1,128)S(1)} %reshape.7.gain_ref, bf16[320,1152]{1,0:T(8,128)(2,1)S(1)} %get-tuple-element.22.sw_ref, bf16[320,320]{1,0:T(8,128)(2,1)S(1)} %get-tuple-element.23.so_ref, bf16[2,160,128]{2,1,0:T(8,128)(2,1)S(1)} %get-tuple-element.33.rest_0_, ...), custom_call_target="tpu_custom_call" | custom-call | flops 587202560 | bytes 4194304 | tf_op jit(solution)/shard_map/spatial/pallas_call | solution.py:338
  31.5 0.9 %copy.9 = bf16[2,256,320]{1,2,0:T(8,128)(2,1)} copy(bf16[2,256,320]{2,1,0:T(8,128)(2,1)S(1)} %spatial.1) | data formatting | bytes 655360 | tf_op jit(solution)/shard_map/spatial/pallas_call | solution.py:338
  (2 shorter events, 0.0 us)
Async XLA Ops:
  1.8 12.5 %copy-start = (f32[320]{0:T(512)S(1)}, f32[320]{0:T(512)}, u32[]{:S(2)}) copy-start(f32[320]{0:T(512)} %param.10) | copy-start | bytes 3844
  1.8 15.4 %collective-permute-start = (bf16[5,160,128]{2,1,0:T(8,128)(2,1)S(1)}, bf16[5,160,128]{2,1,0:T(8,128)(2,1)S(1)}, u32[]{:S(2)}, u32[]{:S(2)}) collective-permute-start(bf16[5,160,128]{2,1,0:T(8,128)(2,1)S(1)} %get-tuple-element.30), channel_id=1, source_target_pairs={{0,4},{4,0},{8,12},{12,8},{1,5},{5,1},{9,13},{13,9},{2,6},{6,2},{1... | collective-permute-start | bytes 614408 | tf_op jit(solution)/shard_map/ppermute | solution.py:381
  4.9 12.3 %collective-permute-start.1 = (bf16[5,160,128]{2,1,0:T(8,128)(2,1)S(1)}, bf16[5,160,128]{2,1,0:T(8,128)(2,1)S(1)}, u32[]{:S(2)}, u32[]{:S(2)}) collective-permute-start(bf16[5,160,128]{2,1,0:T(8,128)(2,1)S(1)} %get-tuple-element.31), channel_id=1, source_target_pairs={{4,8},{8,4},{5,9},{9,5},{6,10},{10,6},{7,11},{11,7},{20,24},{24,20... | collective-permute-start | bytes 614408 | tf_op jit(solution)/shard_map/ppermute | solution.py:382
  5.6 11.0 %collective-permute-start.2 = (bf16[1,160,128]{2,1,0:T(8,128)(2,1)S(1)}, bf16[1,160,128]{2,1,0:T(8,128)(2,1)S(1)}, u32[]{:S(2)}, u32[]{:S(2)}) collective-permute-start(bf16[1,160,128]{2,1,0:T(8,128)(2,1)S(1)} %get-tuple-element.32.rest_0_), channel_id=1, source_target_pairs={{0,8},{8,0},{4,12},{12,4},{1,9},{9,1},{5,13},{13,5},{2,10},{10,2},... | collective-permute-start | bytes 122888 | tf_op jit(solution)/shard_map/ppermute | solution.py:380
  9.5 7.7 %collective-permute-start.3 = (bf16[1,160,128]{2,1,0:T(8,128)(2,1)S(1)}, bf16[1,160,128]{2,1,0:T(8,128)(2,1)S(1)}, u32[]{:S(2)}, u32[]{:S(2)}) collective-permute-start(bf16[1,160,128]{2,1,0:T(8,128)(2,1)S(1)} %get-tuple-element.32.rest_0_), channel_id=1, source_target_pairs={{0,12},{12,0},{1,13},{13,1},{2,14},{14,2},{3,15},{15,3},{16,28},{2... | collective-permute-start | bytes 122888 | tf_op jit(solution)/shard_map/ppermute | solution.py:380
  22.5 1.9 %copy-start.1 = (f32[320]{0:T(512)S(1)}, f32[320]{0:T(512)}, u32[]{:S(2)}) copy-start(f32[320]{0:T(512)} %param.13) | copy-start | bytes 3844
  22.5 1.9 %collective-permute-start.4 = (bf16[2,160,128]{2,1,0:T(8,128)(2,1)S(1)}, bf16[2,160,128]{2,1,0:T(8,128)(2,1)S(1)}, u32[]{:S(2)}, u32[]{:S(2)}) collective-permute-start(bf16[2,160,128]{2,1,0:T(8,128)(2,1)S(1)} %get-tuple-element.34), channel_id=1, source_target_pairs={{0,1},{1,0},{2,3},{3,2},{4,5},{5,4},{6,7},{7,6},{8,9},{9,8},{10,11... | collective-permute-start | bytes 245768 | tf_op jit(solution)/shard_map/ppermute | solution.py:392
  22.6 5.1 %collective-permute-start.5 = (bf16[2,160,128]{2,1,0:T(8,128)(2,1)S(1)}, bf16[2,160,128]{2,1,0:T(8,128)(2,1)S(1)}, u32[]{:S(2)}, u32[]{:S(2)}) collective-permute-start(bf16[2,160,128]{2,1,0:T(8,128)(2,1)S(1)} %get-tuple-element.35), channel_id=1, source_target_pairs={{0,2},{1,3},{2,0},{3,1},{4,6},{5,7},{6,4},{7,5},{8,10},{9,11},{10,... | collective-permute-start | bytes 245768 | tf_op jit(solution)/shard_map/ppermute | solution.py:392
  24.2 4.7 %collective-permute-start.6 = (bf16[2,160,128]{2,1,0:T(8,128)(2,1)S(1)}, bf16[2,160,128]{2,1,0:T(8,128)(2,1)S(1)}, u32[]{:S(2)}, u32[]{:S(2)}) collective-permute-start(bf16[2,160,128]{2,1,0:T(8,128)(2,1)S(1)} %get-tuple-element.36), channel_id=1, source_target_pairs={{0,3},{1,2},{2,1},{3,0},{4,7},{5,6},{6,5},{7,4},{8,11},{9,10},{10,... | collective-permute-start | bytes 245768 | tf_op jit(solution)/shard_map/ppermute | solution.py:392

commit v3 on v2

v3 whole, which is shorter than its diff:
```python
import functools
import math

import jax
import jax.numpy as jnp
from jax import lax
from jax.experimental import pallas as pl
from jax.experimental.pallas import tpu as pltpu
from jax.sharding import PartitionSpec as P

HEAD_DIM = 64
HALO = 4
SUB = 8
LANES = 128
NEG = -1e30
DIRECT_CLIPS = 4
LIMIT = 24 << 20
LEAD = 1
FAR = pl.BlockSpec(memory_space=pltpu.HBM)
VMEM = pl.BlockSpec(memory_space=pltpu.VMEM)
NT = (((1,), (1,)), ((), ()))


def far(array):
    return pltpu.with_memory_space_constraint(array, pltpu.HBM)


def up(count, step):
    return -(-count // step) * step


def tiles_of(channels):
    return [(start, min(LANES, channels - start)) for start in range(0, channels, LANES)]


def pack(rows):
    pixels, channels = rows.shape
    parts = [rows[:, start : start + width] for start, width in tiles_of(channels) if width == LANES]
    if channels % LANES:
        tail = rows[:, channels - channels % LANES :]
        parts.append(jnp.concatenate([tail[: pixels // 2], tail[pixels // 2 :]], axis=1))
    return jnp.concatenate(parts, axis=0)


def unpack(dense, pixels, channels):
    whole = channels // LANES
    parts = [dense[i * pixels : (i + 1) * pixels] for i in range(whole)]
    if channels % LANES:
        tail = dense[whole * pixels :]
        parts.append(jnp.concatenate([tail[:, : LANES // 2], tail[:, LANES // 2 :]], axis=0))
    return jnp.concatenate(parts, axis=1)


def layer_norm(values, scales):
    share = 1.0 / values.shape[-1]
    average = jnp.sum(values, axis=-1, keepdims=True) * share
    centred = values - average
    spread = jnp.sum(centred * centred, axis=-1, keepdims=True) * share
    return centred * lax.rsqrt(spread + 1e-05) * scales


def own_lanes(shape, slot):
    return (lax.broadcasted_iota(jnp.int32, shape, 1) // HEAD_DIM) == slot


def stack_heads(queries):
    held = queries.shape[1] // HEAD_DIM
    if held == 1:
        return queries
    zero = jnp.zeros_like(queries)
    return jnp.concatenate(
        [jnp.where(own_lanes(queries.shape, slot), queries, zero) for slot in range(held)], axis=0
    )


def unstack_heads(mixed, held):
    rows = mixed.shape[0] // held
    result = mixed[:rows]
    for slot in range(1, held):
        part = mixed[slot * rows : (slot + 1) * rows]
        result = jnp.where(own_lanes(part.shape, slot), part, result)
    return result


def soften(scores):
    highest = jnp.max(scores, axis=-1, keepdims=True)
    expo = jnp.exp((scores - highest) * (1.0 / math.sqrt(HEAD_DIM)))
    return expo.astype(jnp.bfloat16), 1.0 / jnp.sum(expo, axis=-1, keepdims=True)


def pipelined(count, score, mix, lead=1):
    scores, weights = {}, {}
    for i in range(count + 2 * lead):
        if i < count:
            scores[i] = score(i)
        if 0 <= i - lead < count:
            weights[i - lead] = soften(scores.pop(i - lead))
        if 0 <= i - 2 * lead < count:
            mix(i - 2 * lead, *weights.pop(i - 2 * lead))


def neighbours(clips):
    me = lax.axis_index("clip")
    odd = lax.rem(me, 2)
    outer = jnp.where(odd == 1, me + 1, me - 1)
    inner = jnp.where(odd == 1, me - 1, me + 1)
    outer_there = (outer >= 0) & (outer < clips)
    inner_there = inner < clips
    return me, odd, inner_there, outer_there


def prep_kernel(clips, x_hbm, s_ref, x_ref, a_ref, b_ref, p_ref, x_sem):
    copy_x = pltpu.make_async_copy(x_hbm, x_ref, x_sem)
    copy_x.start()
    _, odd, _, _ = neighbours(clips)
    copy_x.wait()
    span = x_ref.shape[0] - HALO
    for i in range(HALO):
        a_ref[i] = pack(x_ref[(1 - odd) * span + i])
        b_ref[i] = pack(x_ref[odd * span + i])
    picked = pack(x_ref[s_ref[0]])
    p_ref[0] = picked
    if a_ref.shape[0] > HALO:
        a_ref[HALO] = picked
        b_ref[HALO] = picked


def prep(latents, sampled, clips, with_pick):
    _, pixels, channels = latents.shape
    dense = (pixels * channels // LANES, LANES)
    sent = HALO + (1 if with_pick else 0)
    kind = latents.dtype
    return pl.pallas_call(
        functools.partial(prep_kernel, clips),
        out_shape=[
            pltpu.VMEM(latents.shape, kind),
            pltpu.VMEM((sent,) + dense, kind),
            pltpu.VMEM((sent,) + dense, kind),
            pltpu.VMEM((1,) + dense, kind),
        ],
        in_specs=[FAR, pl.BlockSpec(memory_space=pltpu.SMEM)],
        out_specs=[VMEM] * 4,
        scratch_shapes=[pltpu.SemaphoreType.DMA],
        compiler_params=pltpu.CompilerParams(vmem_limit_bytes=LIMIT),
        name="prep",
    )(far(latents), sampled)


def local_kernel(
    x_ref, gain_ref, tq_hbm, to_hbm, sq_hbm, so_hbm,
    q_ref, k_ref, v_ref, xg_ref, tw_ref, sw_ref, to_ref, so_ref,
    tq_ref, sq_ref, sp_ref, normed_ref, sems,
):
    copies = [
        pltpu.make_async_copy(source, target, sems.at[i])
        for i, (source, target) in enumerate(
            ((tq_hbm, tq_ref), (sq_hbm, sq_ref), (to_hbm, to_ref), (so_hbm, sp_ref))
        )
    ]
    for copy in copies:
        copy.start()
    frames, pixels, channels = x_ref.shape
    groups = pixels // SUB
    gain = gain_ref[...]
    for f in range(frames):
        values = x_ref[f].astype(jnp.float32)
        normed = layer_norm(values, gain)
        for g in range(groups):
            xg_ref[g, f] = values[g * SUB : (g + 1) * SUB]
            normed_ref[g, f] = normed[g * SUB : (g + 1) * SUB]
    step = up(channels, LANES)

    def spread(source, target):
        for part in range(3):
            target[:, part * step : part * step + channels] = source[
                :, part * channels : (part + 1) * channels
            ]
            if step > channels:
                target[:, part * step + channels : (part + 1) * step] = jnp.zeros(
                    (channels, step - channels), target.dtype
                )

    copies[0].wait()
    spread(tq_ref, tw_ref)
    rows = normed_ref[...].reshape(groups * frames * SUB, channels).astype(jnp.bfloat16)
    packed = jnp.dot(rows, tw_ref[...], preferred_element_type=jnp.float32).astype(jnp.bfloat16)
    own = frames * SUB
    for g in range(groups):
        for start, width in tiles_of(channels):
            stacked = stack_heads(packed[g * own : (g + 1) * own, start : start + width])
            q_ref[g, start // HEAD_DIM * own : start // HEAD_DIM * own + stacked.shape[0], :width] = stacked
    k_ref[...] = packed[:, step : step + channels]
    v_ref[...] = packed[:, 2 * step : 2 * step + channels]
    copies[1].wait()
    spread(sq_ref, sw_ref)
    copies[2].wait()
    copies[3].wait()
    so_ref[...] = sp_ref[...].T


def local(latents, gain, temporal_qkv, temporal_out, spatial_qkv, spatial_out):
    frames, pixels, channels = latents.shape
    groups = pixels // SUB
    count = frames * pixels
    kind = latents.dtype
    wide = (channels, 3 * up(channels, LANES))
    square = (channels, channels)
    return pl.pallas_call(
        local_kernel,
        out_shape=[pltpu.VMEM((groups, channels // HEAD_DIM * frames * SUB, LANES), kind)]
        + [pltpu.VMEM((count, channels), kind)] * 2
        + [pltpu.VMEM((groups, frames, SUB, channels), jnp.float32)]
        + [pltpu.VMEM(wide, kind)] * 2
        + [pltpu.VMEM(square, kind)] * 2,
        in_specs=[VMEM, pl.BlockSpec()] + [FAR] * 4,
        out_specs=[VMEM] * 8,
        scratch_shapes=[
            pltpu.VMEM(temporal_qkv.shape, kind),
            pltpu.VMEM(spatial_qkv.shape, kind),
            pltpu.VMEM(square, kind),
            pltpu.VMEM((groups, frames, SUB, channels), jnp.float32),
            pltpu.SemaphoreType.DMA((4,)),
        ],
        cost_estimate=pl.CostEstimate(
            flops=2 * count * channels * 3 * channels, bytes_accessed=4 << 20, transcendentals=0
        ),
        compiler_params=pltpu.CompilerParams(vmem_limit_bytes=LIMIT),
        name="local",
    )(
        latents,
        gain.reshape(1, channels),
        *(far(w) for w in (temporal_qkv, temporal_out, spatial_qkv, spatial_out)),
    )


def remote_pairs(dense, gain, tw_ref, normed_ref, pixels):
    channels = gain.shape[1]
    groups, slots = normed_ref.shape[:2]
    for j, frame in enumerate(dense):
        normed = layer_norm(unpack(frame, pixels, channels).astype(jnp.float32), gain)
        for g in range(groups):
            normed_ref[g, j] = normed[g * SUB : (g + 1) * SUB]
    for j in range(len(dense), slots):
        for g in range(groups):
            normed_ref[g, j] = jnp.zeros((SUB, channels), jnp.float32)
    step = up(channels, LANES)
    rows = normed_ref[...].reshape(groups * slots * SUB, channels).astype(jnp.bfloat16)
    return jnp.dot(rows, tw_ref[:, step:], preferred_element_type=jnp.float32).astype(jnp.bfloat16)


def early_kernel(gain_ref, tw_ref, a_ref, *rest):
    *pick_refs, kv_ref, normed_ref = rest
    dense = [a_ref[i] for i in range(a_ref.shape[0])]
    for ref in pick_refs:
        dense += [ref[i] for i in range(ref.shape[0])]
    pixels = normed_ref.shape[0] * SUB
    kv_ref[...] = remote_pairs(dense, gain_ref[...], tw_ref, normed_ref, pixels)


def early(gain, weights, a, picks, pixels, slots):
    channels = weights.shape[0]
    groups = pixels // SUB
    kind = weights.dtype
    return pl.pallas_call(
        early_kernel,
        out_shape=pltpu.VMEM((pixels * slots, 2 * up(channels, LANES)), kind),
        in_specs=[pl.BlockSpec()] + [VMEM] * (2 + len(picks)),
        out_specs=VMEM,
        scratch_shapes=[pltpu.VMEM((groups, slots, SUB, channels), jnp.float32)],
        cost_estimate=pl.CostEstimate(
            flops=2 * pixels * slots * channels * 2 * channels, bytes_accessed=2 << 20, transcendentals=0
        ),
        compiler_params=pltpu.CompilerParams(vmem_limit_bytes=LIMIT),
        name="early",
    )(gain.reshape(1, channels), weights, a, *picks)


def temporal_kernel(
    clips, far_steps, early_held, pix_count,
    q_ref, k_ref, v_ref, xg_ref, kv_ref, gain_ref, tw_ref, to_ref, b_ref, *rest,
):
    sends, (normed_ref, att_ref, rows_ref) = rest[:pix_count], rest[pix_count:]
    groups, frames, _, channels = xg_ref.shape
    pixels = groups * SUB
    me, _, first_there, second_there = neighbours(clips)
    held = b_ref.shape[0]
    dense = [b_ref[i] for i in range(held)]
    late = remote_pairs(dense, gain_ref[...], tw_ref, normed_ref, pixels)
    step = up(channels, LANES)

    own, soon, more = frames * SUB, kv_ref.shape[0] // groups, late.shape[0] // groups
    shape = (own, own + soon + more)
    row = lax.broadcasted_iota(jnp.int32, shape, 0)
    column = lax.broadcasted_iota(jnp.int32, shape, 1)
    usable = lax.rem(row, SUB) == lax.rem(column, SUB)
    slot = column // SUB - frames
    usable &= (slot < 0) | (slot >= held) | first_there
    usable &= (slot < early_held) | (slot >= soon // SUB)
    for i, hop in enumerate(far_steps):
        distant = jnp.abs(jnp.bitwise_xor(me, hop) - me) > 1
        usable &= (slot != held + 1 + i) | distant
    usable &= (slot < soon // SUB) | (slot >= soon // SUB + held) | second_there
    usable &= slot < soon // SUB + held
    bias = jnp.where(usable, 0.0, NEG).astype(jnp.float32)

    tiles = tiles_of(channels)
    blocks = [(g, start, width) for g in range(groups) for start, width in tiles]

    def score(i):
        g, start, width = blocks[i]
        span = slice(start, start + width)
        count = width // HEAD_DIM
        queries = q_ref[g, start // HEAD_DIM * own : (start + width) // HEAD_DIM * own, :width]
        keys = jnp.concatenate(
            [
                k_ref[g * own : (g + 1) * own, span],
                kv_ref[g * soon : (g + 1) * soon, span],
                late[g * more : (g + 1) * more, span],
            ],
            axis=0,
        )
        scores = lax.dot_general(queries, keys, NT, preferred_element_type=jnp.float32)
        return scores + jnp.concatenate([bias] * count, axis=0)

    def mix(i, weights, norm):
        g, start, width = blocks[i]
        values = jnp.concatenate(
            [
                v_ref[g * own : (g + 1) * own, start : start + width],
                kv_ref[g * soon : (g + 1) * soon, step + start : step + start + width],
                late[g * more : (g + 1) * more, step + start : step + start + width],
            ],
            axis=0,
        )
        mixed = jnp.dot(weights, values, preferred_element_type=jnp.float32) * norm
        att_ref[g * own : (g + 1) * own, start : start + width] = unstack_heads(
            mixed, width // HEAD_DIM
        ).astype(jnp.bfloat16)

    pipelined(len(blocks), score, mix, LEAD)
    update = jnp.dot(att_ref[...], to_ref[...], preferred_element_type=jnp.float32)
    for g in range(groups):
        for f in range(frames):
            at = (g * frames + f) * SUB
            rows_ref[f, g * SUB : (g + 1) * SUB] = xg_ref[g, f] + update[at : at + SUB]
    place = lax.axis_index("pix")
    per_device = sends[0].shape[0]
    for k, ref in enumerate(sends):
        target = jnp.bitwise_xor(place, k)
        for i in range(per_device):
            ref[i] = pack(rows_ref[target * per_device + i].astype(jnp.bfloat16))


def temporal(parts, pairs, gain, weights, out_matrix, b, clips, far_steps, early_held, pix_count):
    q, k, v, xg = parts
    groups, frames, _, channels = xg.shape
    pixels = groups * SUB
    slots = up(b.shape[0], 2)
    count = frames * pixels
    kind = q.dtype
    dense = (pixels * channels // LANES, LANES)
    return pl.pallas_call(
        functools.partial(temporal_kernel, clips, far_steps, early_held, pix_count),
        out_shape=[pltpu.VMEM((frames // pix_count,) + dense, kind)] * pix_count,
        in_specs=[VMEM] * 5 + [pl.BlockSpec()] + [VMEM] * 3,
        out_specs=[VMEM] * pix_count,
        scratch_shapes=[
            pltpu.VMEM((groups, slots, SUB, channels), jnp.float32),
            pltpu.VMEM((count, channels), kind),
            pltpu.VMEM((frames, pixels, channels), jnp.float32),
        ],
        cost_estimate=pl.CostEstimate(
            flops=2 * count * channels * 4 * channels, bytes_accessed=8 << 20, transcendentals=0
        ),
        compiler_params=pltpu.CompilerParams(vmem_limit_bytes=LIMIT),
        name="temporal",
    )(q, k, v, xg, pairs, gain.reshape(1, channels), weights, out_matrix, b)


def spatial_kernel(pix_count, gain_ref, sw_ref, so_ref, *rest):
    chunks, (out_ref, rows_ref, att_ref) = rest[:pix_count], rest[pix_count:]
    per_device, channels, pixels = out_ref.shape
    each = pixels // pix_count
    step = up(channels, LANES)
    place = lax.axis_index("pix")
    for k, ref in enumerate(chunks):
        at = pl.multiple_of(jnp.bitwise_xor(place, k) * each, each)
        for i in range(per_device):
            rows_ref[i, pl.ds(at, each), :] = unpack(ref[i], each, channels).astype(jnp.float32)
    rows = rows_ref[...].reshape(per_device * pixels, channels)
    normed = layer_norm(rows, gain_ref[...]).astype(jnp.bfloat16)
    packed = jnp.dot(normed, sw_ref[...], preferred_element_type=jnp.float32).astype(jnp.bfloat16)
    tiles = tiles_of(channels)
    blocks = [(i, start, width) for i in range(per_device) for start, width in tiles]

    def part_of(i, which):
        frame, start, width = blocks[i]
        return packed[
            frame * pixels : (frame + 1) * pixels, which * step + start : which * step + start + width
        ]

    def score(i):
        return lax.dot_general(
            stack_heads(part_of(i, 0)), part_of(i, 1), NT, preferred_element_type=jnp.float32
        )

    def mix(i, weights, norm):
        frame, start, width = blocks[i]
        mixed = jnp.dot(weights, part_of(i, 2), preferred_element_type=jnp.float32) * norm
        att_ref[frame, :, start : start + width] = unstack_heads(mixed, width // HEAD_DIM).astype(
            jnp.bfloat16
        )

    pipelined(len(blocks), score, mix)
    for i in range(per_device):
        update = lax.dot_general(so_ref[...], att_ref[i], NT, preferred_element_type=jnp.float32)
        out_ref[i] = (rows_ref[i].T + update).astype(jnp.bfloat16)


def spatial(gain, weights, out_matrix, chunks, pixels):
    pix_count = len(chunks)
    per_device = chunks[0].shape[0]
    channels = out_matrix.shape[0]
    kind = chunks[0].dtype
    return pl.pallas_call(
        functools.partial(spatial_kernel, pix_count),
        out_shape=jax.ShapeDtypeStruct((per_device, channels, pixels), kind),
        in_specs=[pl.BlockSpec()] + [VMEM] * (2 + pix_count),
        out_specs=pl.BlockSpec(),
        scratch_shapes=[
            pltpu.VMEM((per_device, pixels, channels), jnp.float32),
            pltpu.VMEM((per_device, pixels, channels), kind),
        ],
        cost_estimate=pl.CostEstimate(
            flops=2 * per_device * pixels * channels * (4 * channels + 2 * pixels),
            bytes_accessed=4 << 20,
            transcendentals=0,
        ),
        compiler_params=pltpu.CompilerParams(vmem_limit_bytes=LIMIT),
        name="spatial",
    )(gain.reshape(1, channels), weights, out_matrix, *chunks)


def both_ways(pairs, count):
    target = [device ^ 1 for device in range(count)]
    for a, b in pairs:
        target[a], target[b] = b, a
    return list(enumerate(target))


def border_pairs(clips, pix_count, turn):
    pairs = [
        (a * pix_count + place, (a + 1) * pix_count + place)
        for a in range(turn, clips - 1, 2)
        for place in range(pix_count)
    ]
    return both_ways(pairs, clips * pix_count)


def body(
    latents,
    sampled,
    temporal_gain,
    temporal_qkv,
    temporal_out,
    spatial_gain,
    spatial_qkv,
    spatial_out,
):
    clips, pix_count = lax.axis_size("clip"), lax.axis_size("pix")
    pixels = latents.shape[1] * pix_count
    gathered = clips > DIRECT_CLIPS or clips & (clips - 1) != 0
    x, a, b, p = prep(latents, sampled, clips, not gathered)
    far_steps = ()
    if gathered:
        picks = [lax.all_gather(p, "clip", axis=0, tiled=True)]
    else:
        picks = [p]
        far_steps = tuple(range(2, clips))
        for step in far_steps:
            distant = [
                (i * pix_count + place, (i ^ step) * pix_count + place)
                for i in range(clips)
                if (i ^ step) - i > 1
                for place in range(pix_count)
            ]
            picks.append(lax.ppermute(p, ("clip", "pix"), both_ways(distant, clips * pix_count)))
    a = lax.ppermute(a, ("clip", "pix"), border_pairs(clips, pix_count, 0))
    b = lax.ppermute(b, ("clip", "pix"), border_pairs(clips, pix_count, 1))
    q, k, v, xg, tw, sw, to, so = local(
        x, temporal_gain, temporal_qkv, temporal_out, spatial_qkv, spatial_out
    )
    early_held = a.shape[0] + sum(pick.shape[0] for pick in picks)
    pairs = early(temporal_gain, tw, a, picks, latents.shape[1], up(early_held, 2))
    sends = temporal(
        (q, k, v, xg), pairs, temporal_gain, tw, to, b, clips, far_steps, early_held, pix_count
    )
    chunks = [sends[0]]
    for step in range(1, pix_count):
        chunks.append(lax.ppermute(sends[step], "pix", [(i, i ^ step) for i in range(pix_count)]))
    return spatial(spatial_gain, sw, so, chunks, pixels).transpose(0, 2, 1)


def solution(mesh):
    placed = (P(("group", "clip"), "pix", None), P(("group", "clip")), P(), P(), P(), P(), P(), P())
    return jax.shard_map(
        body,
        mesh=mesh,
        in_specs=placed,
        out_specs=P(("group", "clip", "pix"), None, None),
        check_vma=False,
    )
```

time: 32.6 us -> 29 us (0.89)
  starting transfers between devices: 14.4 us -> 10.5 us
  waiting for transfers between devices: 4.98 us -> 6.53 us
  local copies, waits for them, and re-layouts: 0.93 us -> 0.02 us
  Pallas kernels: 11.4 us -> 11 us
    ppermute x7, starting transfers between devices: 14.4 us -> 10.5 us  [the longest x2 5.51 us: body(): lax.ppermute(p, ('clip', 'pix'), both_ways(distant, clips * pix_count))]
    ppermute x7, waiting for transfers between devices: 4.98 us -> 6.53 us  [the longest x3 4.44 us: body(): lax.ppermute(sends[step], 'pix', [(i, i ^ step) for i in range(pix_count)])]
    pallas_call x1 -> x0, local copies, waits for them, and re-layouts: 0.91 us -> none  [spatial(): pl.pallas_call(functools.partial(spatial_kernel, pix_count), out_shape=ja...]
    pallas_call x3 -> x4, Pallas kernels: 8.76 us -> 7.86 us  [the longest x1 3.34 us: temporal(): pl.pallas_call(functools.partial(temporal_kernel, clips, far_steps, early...]
    pallas_call x1, Pallas kernels: 2.61 us -> 3.16 us  [spatial(): pl.pallas_call(functools.partial(spatial_kernel, pix_count), out_shape=ja...]
  transfers between devices with their start and end apart: 7 -> 7, of which waited for: 3 -> 3; matrix products, arithmetic and copies ran while one was open for 0% -> 0% of each run, Pallas kernels for 7% -> 12%
where the time goes in v3:
time: 29 us; the launch traced here: 28.8 us
  Pallas kernels  11 us (38%)
  starting transfers between devices  10.5 us (36%)
  waiting for transfers between devices  6.53 us (23%)
  between operations  0.73 us (3%)
    ppermute x2, starting transfers between devices, body(): lax.ppermute(p, ('clip', 'pix'), both_ways(distant, clips * pix_count))  5.51 us
    ppermute x3, waiting for transfers between devices, body(): lax.ppermute(sends[step], 'pix', [(i, i ^ step) for i in range(pix_count)])  4.44 us
    pallas_call x1, Pallas kernels, temporal(): pl.pallas_call(functools.partial(temporal_kernel, clips, far_steps, early...  3.34 us
    pallas_call x1, Pallas kernels, spatial(): pl.pallas_call(functools.partial(spatial_kernel, pix_count), out_shape=ja...  3.16 us
    ppermute x1, starting transfers between devices, body(): a = lax.ppermute(a, ('clip', 'pix'), border_pairs(clips, pix_count, 0))  3.12 us
    pallas_call x1, Pallas kernels, local(): pl.pallas_call(local_kernel, out_shape=[pltpu.VMEM((groups, channels // H...  2.41 us
    ppermute x2, waiting for transfers between devices, body(): lax.ppermute(p, ('clip', 'pix'), both_ways(distant, clips * pix_count))  2.08 us
    ppermute x3, starting transfers between devices, body(): lax.ppermute(sends[step], 'pix', [(i, i ^ step) for i in range(pix_count)])  1.92 us
  transfers between devices with their start and end apart: 7, of which 3 were waited for; matrix products, arithmetic and copies ran while one was open for 0% of the time, Pallas kernels for 12%

profile of v3, /device:TPU:0, one launch (start us, length us, event | category | flops | bytes accessed | tf_op | source)
XLA Modules:
  0.0 28.8 jit_solution(8453308345612848201)
XLA Ops:
  0.7 1.1 %prep.1 = (bf16[8,64,320]{2,1,0:T(8,128)(2,1)S(1)}, bf16[5,160,128]{2,1,0:T(8,128)(2,1)S(1)}, bf16[5,160,128]{2,1,0:T(8,128)(2,1)S(1)}, bf16[1,160,128]{2,1,0:T(8,128)(2,1)S(1)}) custom-call(bf16[8,64,320]{2,1,0:T(8,128)(2,1)} %x_hbm.1, s32[1]{0:T(128)S(6)} %copy.9.s_ref), custom_call_target="tpu_custom_call" | custom-call | tf_op jit(solution)/shard_map/prep/pallas_call | solution.py:133
  1.8 0.0 copy-start
  1.8 3.1 %collective-permute-start = (bf16[5,160,128]{2,1,0:T(8,128)(2,1)S(1)}, bf16[5,160,128]{2,1,0:T(8,128)(2,1)S(1)}, u32[]{:S(2)}, u32[]{:S(2)}) collective-permute-start(bf16[5,160,128]{2,1,0:T(8,128)(2,1)S(1)} %get-tuple-element.29), channel_id=1, source_target_pairs={{0,4},{1,5},{2,6},{3,7},{4,0},{5,1},{6,2},{7,3},{8,12},{9,13},{10,... | collective-permute-start | bytes 614408 | tf_op jit(solution)/shard_map/ppermute | solution.py:488
  4.9 0.0 collective-permute-start.3
  4.9 2.6 %collective-permute-start.1 = (bf16[1,160,128]{2,1,0:T(8,128)(2,1)S(1)}, bf16[1,160,128]{2,1,0:T(8,128)(2,1)S(1)}, u32[]{:S(2)}, u32[]{:S(2)}) collective-permute-start(bf16[1,160,128]{2,1,0:T(8,128)(2,1)S(1)} %get-tuple-element.30.rest_0_), channel_id=1, source_target_pairs={{0,8},{1,9},{2,10},{3,11},{4,12},{5,13},{6,14},{7,15},{8,0},{9,1},... | collective-permute-start | bytes 122888 | tf_op jit(solution)/shard_map/ppermute | solution.py:487
  7.5 2.9 %collective-permute-start.2 = (bf16[1,160,128]{2,1,0:T(8,128)(2,1)S(1)}, bf16[1,160,128]{2,1,0:T(8,128)(2,1)S(1)}, u32[]{:S(2)}, u32[]{:S(2)}) collective-permute-start(bf16[1,160,128]{2,1,0:T(8,128)(2,1)S(1)} %get-tuple-element.30.rest_0_), channel_id=1, source_target_pairs={{0,12},{1,13},{2,14},{3,15},{4,5},{5,4},{6,7},{7,6},{8,9},{9,8},{1... | collective-permute-start | bytes 122888 | tf_op jit(solution)/shard_map/ppermute | solution.py:487
  10.4 0.0 copy-done
  10.4 2.4 %local.1 = (bf16[8,320,128]{2,1,0:T(8,128)(2,1)S(1)}, bf16[512,320]{1,0:T(8,128)(2,1)S(1)}, bf16[512,320]{1,0:T(8,128)(2,1)S(1)}, f32[8,8,8,320]{3,2,1,0:T(8,128...) custom-call(bf16[8,64,320]{2,1,0:T(8,128)(2,1)S(1)} %get-tuple-eleme, ...), custom_call_target="tpu_custom_call" | custom-call | flops 314572800 | bytes 4194304 | tf_op jit(solution)/shard_map/local/pallas_call | solution.py:208
  12.8 2.1 %collective-permute-done.1.rest_1_ = bf16[1,160,128]{2,1,0:T(8,128)(2,1)S(1)} collective-permute-done((bf16[1,160,128]{2,1,0:T(8,128)(2,1)S(1)}, bf16[1,160,128]{2,1,0:T(8,128)(2,1)S(1)}, u32[]{:S(2)}, u32[]{:S(2)}) %collective-permute-start.1) | collective-permute-done | bytes 40992 | tf_op jit(solution)/shard_map/ppermute | solution.py:487
  14.9 0.0 collective-permute-done.2.rest_2_
  14.9 0.0 collective-permute-done.a_ref
  14.9 1.0 %early.1.kv_ref = bf16[512,768]{1,0:T(8,128)(2,1)S(1)} custom-call(f32[1,320]{1,0:T(1,128)S(1)} %reshape.9.gain_ref, bf16[320,1152]{1,0:T(8,128)(2,1)S(1)} %get-tuple-element.28.tw_ref, bf16[5,160,128]{2,1,0:T(8,128)(2,1)S(1)} %collective-permute-done.a_ref, bf16[1,160,128]{2,1,0:T(8,128)(2,1)S(1)} %get-tuple-element.30.rest_0_, ...), custom_call_target="tpu_custom_call" | custom-call | flops 209715200 | bytes 2097152 | tf_op jit(solution)/shard_map/early/pallas_call | solution.py:264
  15.9 0.0 collective-permute-done.3.b_ref
  15.9 3.3 %temporal.1 = (bf16[2,160,128]{2,1,0:T(8,128)(2,1)S(1)}, bf16[2,160,128]{2,1,0:T(8,128)(2,1)S(1)}, bf16[2,160,128]{2,1,0:T(8,128)(2,1)S(1)}, bf16[2,160,128]{2,1,0:T(8,128)(2,1)S(1)}) custom-call(bf16[8,320,128]{2,1,0:T(8,128)(2,1)S(1)} %get-tuple-element.24.q_ref, bf16[512,320]{1,0:T(8,128)(2,1)S(1)} %get-tuple-element.25.k_ref, ...), custom_call_target="tpu_custom_call" | custom-call | flops 419430400 | bytes 8388608 | tf_op jit(solution)/shard_map/temporal/pallas_call | solution.py:362
  19.3 0.0 copy-start.1
  19.3 0.1 collective-permute-start.4
  19.4 1.6 %collective-permute-start.5 = (bf16[2,160,128]{2,1,0:T(8,128)(2,1)S(1)}, bf16[2,160,128]{2,1,0:T(8,128)(2,1)S(1)}, u32[]{:S(2)}, u32[]{:S(2)}) collective-permute-start(bf16[2,160,128]{2,1,0:T(8,128)(2,1)S(1)} %get-tuple-element.35), channel_id=1, source_target_pairs={{0,2},{1,3},{2,0},{3,1},{4,6},{5,7},{6,4},{7,5},{8,10},{9,11},{10,... | collective-permute-start | bytes 245768 | tf_op jit(solution)/shard_map/ppermute | solution.py:500
  20.9 0.3 collective-permute-start.6
  21.2 0.0 copy-done.1
  21.2 0.0 collective-permute-done.4.rest_1_
  21.2 3.3 %collective-permute-done.5.rest_2_ = bf16[2,160,128]{2,1,0:T(8,128)(2,1)S(1)} collective-permute-done((bf16[2,160,128]{2,1,0:T(8,128)(2,1)S(1)}, bf16[2,160,128]{2,1,0:T(8,128)(2,1)S(1)}, u32[]{:S(2)}, u32[]{:S(2)}) %collective-permute-start.5) | collective-permute-done | bytes 81952 | tf_op jit(solution)/shard_map/ppermute | solution.py:500
  24.5 1.2 %collective-permute-done.6.rest_3_ = bf16[2,160,128]{2,1,0:T(8,128)(2,1)S(1)} collective-permute-done((bf16[2,160,128]{2,1,0:T(8,128)(2,1)S(1)}, bf16[2,160,128]{2,1,0:T(8,128)(2,1)S(1)}, u32[]{:S(2)}, u32[]{:S(2)}) %collective-permute-start.6) | collective-permute-done | bytes 81952 | tf_op jit(solution)/shard_map/ppermute | solution.py:500
  25.7 3.2 %spatial.1 = bf16[2,320,256]{2,1,0:T(8,128)(2,1)} custom-call(f32[1,320]{1,0:T(1,128)S(1)} %reshape.8.gain_ref, bf16[320,1152]{1,0:T(8,128)(2,1)S(1)} %get-tuple-element.22.sw_ref, bf16[320,320]{1,0:T(8,128)(2,1)S(1)} %get-tuple-element.23.so_ref, bf16[2,160,128]{2,1,0:T(8,128)(2,1)S(1)} %get-tuple-element.33.rest_0_, ...), custom_call_target="tpu_custom_call" | custom-call | flops 587202560 | bytes 4194304 | tf_op jit(solution)/shard_map/spatial/pallas_call | solution.py:425
  (2 shorter events, 0.0 us)
Async XLA Ops:
  1.8 8.6 %copy-start = (f32[320]{0:T(512)S(1)}, f32[320]{0:T(512)}, u32[]{:S(2)}) copy-start(f32[320]{0:T(512)} %param.10) | copy-start | bytes 3844
  1.8 13.1 %collective-permute-start = (bf16[5,160,128]{2,1,0:T(8,128)(2,1)S(1)}, bf16[5,160,128]{2,1,0:T(8,128)(2,1)S(1)}, u32[]{:S(2)}, u32[]{:S(2)}) collective-permute-start(bf16[5,160,128]{2,1,0:T(8,128)(2,1)S(1)} %get-tuple-element.29), channel_id=1, source_target_pairs={{0,4},{1,5},{2,6},{3,7},{4,0},{5,1},{6,2},{7,3},{8,12},{9,13},{10,... | collective-permute-start | bytes 614408 | tf_op jit(solution)/shard_map/ppermute | solution.py:488
  4.9 11.0 %collective-permute-start.3 = (bf16[5,160,128]{2,1,0:T(8,128)(2,1)S(1)}, bf16[5,160,128]{2,1,0:T(8,128)(2,1)S(1)}, u32[]{:S(2)}, u32[]{:S(2)}) collective-permute-start(bf16[5,160,128]{2,1,0:T(8,128)(2,1)S(1)} %get-tuple-element.32), channel_id=1, source_target_pairs={{0,1},{1,0},{2,3},{3,2},{4,8},{5,9},{6,10},{7,11},{8,4},{9,5},{10,... | collective-permute-start | bytes 614408 | tf_op jit(solution)/shard_map/ppermute | solution.py:489
  4.9 10.0 %collective-permute-start.1 = (bf16[1,160,128]{2,1,0:T(8,128)(2,1)S(1)}, bf16[1,160,128]{2,1,0:T(8,128)(2,1)S(1)}, u32[]{:S(2)}, u32[]{:S(2)}) collective-permute-start(bf16[1,160,128]{2,1,0:T(8,128)(2,1)S(1)} %get-tuple-element.30.rest_0_), channel_id=1, source_target_pairs={{0,8},{1,9},{2,10},{3,11},{4,12},{5,13},{6,14},{7,15},{8,0},{9,1},... | collective-permute-start | bytes 122888 | tf_op jit(solution)/shard_map/ppermute | solution.py:487
  7.5 7.4 %collective-permute-start.2 = (bf16[1,160,128]{2,1,0:T(8,128)(2,1)S(1)}, bf16[1,160,128]{2,1,0:T(8,128)(2,1)S(1)}, u32[]{:S(2)}, u32[]{:S(2)}) collective-permute-start(bf16[1,160,128]{2,1,0:T(8,128)(2,1)S(1)} %get-tuple-element.30.rest_0_), channel_id=1, source_target_pairs={{0,12},{1,13},{2,14},{3,15},{4,5},{5,4},{6,7},{7,6},{8,9},{9,8},{1... | collective-permute-start | bytes 122888 | tf_op jit(solution)/shard_map/ppermute | solution.py:487
  19.3 1.9 %copy-start.1 = (f32[320]{0:T(512)S(1)}, f32[320]{0:T(512)}, u32[]{:S(2)}) copy-start(f32[320]{0:T(512)} %param.13) | copy-start | bytes 3844
  19.3 1.9 %collective-permute-start.4 = (bf16[2,160,128]{2,1,0:T(8,128)(2,1)S(1)}, bf16[2,160,128]{2,1,0:T(8,128)(2,1)S(1)}, u32[]{:S(2)}, u32[]{:S(2)}) collective-permute-start(bf16[2,160,128]{2,1,0:T(8,128)(2,1)S(1)} %get-tuple-element.34), channel_id=1, source_target_pairs={{0,1},{1,0},{2,3},{3,2},{4,5},{5,4},{6,7},{7,6},{8,9},{9,8},{10,11... | collective-permute-start | bytes 245768 | tf_op jit(solution)/shard_map/ppermute | solution.py:500
  19.4 5.1 %collective-permute-start.5 = (bf16[2,160,128]{2,1,0:T(8,128)(2,1)S(1)}, bf16[2,160,128]{2,1,0:T(8,128)(2,1)S(1)}, u32[]{:S(2)}, u32[]{:S(2)}) collective-permute-start(bf16[2,160,128]{2,1,0:T(8,128)(2,1)S(1)} %get-tuple-element.35), channel_id=1, source_target_pairs={{0,2},{1,3},{2,0},{3,1},{4,6},{5,7},{6,4},{7,5},{8,10},{9,11},{10,... | collective-permute-start | bytes 245768 | tf_op jit(solution)/shard_map/ppermute | solution.py:500
  20.9 4.7 %collective-permute-start.6 = (bf16[2,160,128]{2,1,0:T(8,128)(2,1)S(1)}, bf16[2,160,128]{2,1,0:T(8,128)(2,1)S(1)}, u32[]{:S(2)}, u32[]{:S(2)}) collective-permute-start(bf16[2,160,128]{2,1,0:T(8,128)(2,1)S(1)} %get-tuple-element.36), channel_id=1, source_target_pairs={{0,3},{1,2},{2,1},{3,0},{4,7},{5,6},{6,5},{7,4},{8,11},{9,10},{10,... | collective-permute-start | bytes 245768 | tf_op jit(solution)/shard_map/ppermute | solution.py:500

commit v4 on v3

--- a/solution.py
+++ b/solution.py
@@ -15,7 +15,8 @@
 NEG = -1e30
 DIRECT_CLIPS = 4
 LIMIT = 24 << 20
-LEAD = 1
+LEAD = 4
+SPATIAL_LEAD = 2
 FAR = pl.BlockSpec(memory_space=pltpu.HBM)
 VMEM = pl.BlockSpec(memory_space=pltpu.VMEM)
 NT = (((1,), (1,)), ((), ()))
@@ -122,7 +123,6 @@
     p_ref[0] = picked
     if a_ref.shape[0] > HALO:
         a_ref[HALO] = picked
-        b_ref[HALO] = picked
 
 
 def prep(latents, sampled, clips, with_pick):
@@ -135,7 +135,7 @@
         out_shape=[
             pltpu.VMEM(latents.shape, kind),
             pltpu.VMEM((sent,) + dense, kind),
-            pltpu.VMEM((sent,) + dense, kind),
+            pltpu.VMEM((HALO,) + dense, kind),
             pltpu.VMEM((1,) + dense, kind),
         ],
         in_specs=[FAR, pl.BlockSpec(memory_space=pltpu.SMEM)],
@@ -187,8 +187,11 @@
     own = frames * SUB
     for g in range(groups):
         for start, width in tiles_of(channels):
-            stacked = stack_heads(packed[g * own : (g + 1) * own, start : start + width])
-            q_ref[g, start // HEAD_DIM * own : start // HEAD_DIM * own + stacked.shape[0], :width] = stacked
+            for half in range(2):
+                at = g * own + half * (own // 2)
+                stacked = stack_heads(packed[at : at + own // 2, start : start + width])
+                first = start // HEAD_DIM * (own // 2)
+                q_ref[g, half, first : first + stacked.shape[0], :width] = stacked
     k_ref[...] = packed[:, step : step + channels]
     v_ref[...] = packed[:, 2 * step : 2 * step + channels]
     copies[1].wait()
@@ -207,7 +210,7 @@
     square = (channels, channels)
     return pl.pallas_call(
         local_kernel,
-        out_shape=[pltpu.VMEM((groups, channels // HEAD_DIM * frames * SUB, LANES), kind)]
+        out_shape=[pltpu.VMEM((groups, 2, channels // HEAD_DIM * frames * SUB // 2, LANES), kind)]
         + [pltpu.VMEM((count, channels), kind)] * 2
         + [pltpu.VMEM((groups, frames, SUB, channels), jnp.float32)]
         + [pltpu.VMEM(wide, kind)] * 2
@@ -276,51 +279,57 @@
 
 
 def temporal_kernel(
-    clips, far_steps, early_held, pix_count,
+    clips, early_held, pix_count, cross,
     q_ref, k_ref, v_ref, xg_ref, kv_ref, gain_ref, tw_ref, to_ref, b_ref, *rest,
 ):
-    sends, (normed_ref, att_ref, rows_ref) = rest[:pix_count], rest[pix_count:]
+    halves = pix_count // 2
+    sends, rest = rest[:halves], rest[halves:]
     groups, frames, _, channels = xg_ref.shape
     pixels = groups * SUB
-    me, _, first_there, second_there = neighbours(clips)
-    held = b_ref.shape[0]
-    dense = [b_ref[i] for i in range(held)]
-    late = remote_pairs(dense, gain_ref[...], tw_ref, normed_ref, pixels)
+    _, _, first_there, second_there = neighbours(clips)
+    if cross:
+        late_ref, normed_ref, att_ref, rows_ref = rest
+        dense = [b_ref[i] for i in range(HALO)]
+        late_ref[...] = remote_pairs(dense, gain_ref[...], tw_ref, normed_ref, pixels)
+    else:
+        late_ref = b_ref
+        att_ref, rows_ref = rest
+    place = lax.axis_index("pix")
+    upper = place // halves
+    half = 1 - upper if cross else upper
     step = up(channels, LANES)
 
-    own, soon, more = frames * SUB, kv_ref.shape[0] // groups, late.shape[0] // groups
-    shape = (own, own + soon + more)
+    part = frames // 2
+    mine, own = part * SUB, frames * SUB
+    soon, more = kv_ref.shape[0] // groups, late_ref.shape[0] // groups
+    shape = (mine, own + soon + more)
     row = lax.broadcasted_iota(jnp.int32, shape, 0)
     column = lax.broadcasted_iota(jnp.int32, shape, 1)
     usable = lax.rem(row, SUB) == lax.rem(column, SUB)
     slot = column // SUB - frames
-    usable &= (slot < 0) | (slot >= held) | first_there
+    usable &= (slot < 0) | (slot >= HALO) | first_there
     usable &= (slot < early_held) | (slot >= soon // SUB)
-    for i, hop in enumerate(far_steps):
-        distant = jnp.abs(jnp.bitwise_xor(me, hop) - me) > 1
-        usable &= (slot != held + 1 + i) | distant
-    usable &= (slot < soon // SUB) | (slot >= soon // SUB + held) | second_there
-    usable &= slot < soon // SUB + held
+    usable &= (slot < soon // SUB) | second_there
     bias = jnp.where(usable, 0.0, NEG).astype(jnp.float32)
 
-    tiles = tiles_of(channels)
-    blocks = [(g, start, width) for g in range(groups) for start, width in tiles]
+    blocks = [(g, start, width) for g in range(groups) for start, width in tiles_of(channels)]
 
     def score(i):
         g, start, width = blocks[i]
         span = slice(start, start + width)
-        count = width // HEAD_DIM
-        queries = q_ref[g, start // HEAD_DIM * own : (start + width) // HEAD_DIM * own, :width]
+        queries = q_ref[
+            g, half, start // HEAD_DIM * mine : (start + width) // HEAD_DIM * mine, :width
+        ]
         keys = jnp.concatenate(
             [
                 k_ref[g * own : (g + 1) * own, span],
                 kv_ref[g * soon : (g + 1) * soon, span],
-                late[g * more : (g + 1) * more, span],
+                late_ref[g * more : (g + 1) * more, span],
             ],
             axis=0,
         )
         scores = lax.dot_general(queries, keys, NT, preferred_element_type=jnp.float32)
-        return scores + jnp.concatenate([bias] * count, axis=0)
+        return scores + jnp.concatenate([bias] * (width // HEAD_DIM), axis=0)
 
     def mix(i, weights, norm):
         g, start, width = blocks[i]
@@ -328,107 +337,170 @@
             [
                 v_ref[g * own : (g + 1) * own, start : start + width],
                 kv_ref[g * soon : (g + 1) * soon, step + start : step + start + width],
-                late[g * more : (g + 1) * more, step + start : step + start + width],
+                late_ref[g * more : (g + 1) * more, step + start : step + start + width],
             ],
             axis=0,
         )
         mixed = jnp.dot(weights, values, preferred_element_type=jnp.float32) * norm
-        att_ref[g * own : (g + 1) * own, start : start + width] = unstack_heads(
+        att_ref[g * mine : (g + 1) * mine, start : start + width] = unstack_heads(
             mixed, width // HEAD_DIM
         ).astype(jnp.bfloat16)
 
     pipelined(len(blocks), score, mix, LEAD)
     update = jnp.dot(att_ref[...], to_ref[...], preferred_element_type=jnp.float32)
     for g in range(groups):
-        for f in range(frames):
-            at = (g * frames + f) * SUB
-            rows_ref[f, g * SUB : (g + 1) * SUB] = xg_ref[g, f] + update[at : at + SUB]
-    place = lax.axis_index("pix")
+        for f in range(part):
+            at = (g * part + f) * SUB
+            rows_ref[f, g * SUB : (g + 1) * SUB] = xg_ref[g, half * part + f] + update[at : at + SUB]
     per_device = sends[0].shape[0]
     for k, ref in enumerate(sends):
-        target = jnp.bitwise_xor(place, k)
+        target = jnp.bitwise_xor(lax.rem(place, halves), k)
         for i in range(per_device):
             ref[i] = pack(rows_ref[target * per_device + i].astype(jnp.bfloat16))
 
 
-def temporal(parts, pairs, gain, weights, out_matrix, b, clips, far_steps, early_held, pix_count):
+def temporal(parts, pairs, gain, weights, out_matrix, last, clips, early_held, pix_count, cross):
     q, k, v, xg = parts
     groups, frames, _, channels = xg.shape
     pixels = groups * SUB
-    slots = up(b.shape[0], 2)
     count = frames * pixels
     kind = q.dtype
     dense = (pixels * channels // LANES, LANES)
+    out_shape = [pltpu.VMEM((frames // pix_count,) + dense, kind)] * (pix_count // 2)
+    scratch = [
+        pltpu.VMEM((count // 2, channels), kind),
+        pltpu.VMEM((frames // 2, pixels, channels), jnp.float32),
+    ]
+    if cross:
+        out_shape = out_shape + [pltpu.VMEM((pixels * HALO, 2 * up(channels, LANES)), kind)]
+        scratch = [pltpu.VMEM((groups, HALO, SUB, channels), jnp.float32)] + scratch
     return pl.pallas_call(
-        functools.partial(temporal_kernel, clips, far_steps, early_held, pix_count),
-        out_shape=[pltpu.VMEM((frames // pix_count,) + dense, kind)] * pix_count,
+        functools.partial(temporal_kernel, clips, early_held, pix_count, cross),
+        out_shape=out_shape,
         in_specs=[VMEM] * 5 + [pl.BlockSpec()] + [VMEM] * 3,
-        out_specs=[VMEM] * pix_count,
-        scratch_shapes=[
-            pltpu.VMEM((groups, slots, SUB, channels), jnp.float32),
-            pltpu.VMEM((count, channels), kind),
-            pltpu.VMEM((frames, pixels, channels), jnp.float32),
-        ],
+        out_specs=[VMEM] * len(out_shape),
+        scratch_shapes=scratch,
         cost_estimate=pl.CostEstimate(
-            flops=2 * count * channels * 4 * channels, bytes_accessed=8 << 20, transcendentals=0
+            flops=2 * count * channels * 2 * channels, bytes_accessed=4 << 20, transcendentals=0
         ),
         compiler_params=pltpu.CompilerParams(vmem_limit_bytes=LIMIT),
-        name="temporal",
-    )(q, k, v, xg, pairs, gain.reshape(1, channels), weights, out_matrix, b)
-
-
-def spatial_kernel(pix_count, gain_ref, sw_ref, so_ref, *rest):
-    chunks, (out_ref, rows_ref, att_ref) = rest[:pix_count], rest[pix_count:]
-    per_device, channels, pixels = out_ref.shape
-    each = pixels // pix_count
-    step = up(channels, LANES)
-    place = lax.axis_index("pix")
+        name="cross" if cross else "near",
+    )(q, k, v, xg, pairs, gain.reshape(1, channels), weights, out_matrix, last)
+
+
+def gather_rows(chunks, rows_ref, channels):
+    halves = len(chunks)
+    per_device, half_pixels = rows_ref.shape[:2]
+    each = half_pixels // halves
+    place = lax.rem(lax.axis_index("pix"), halves)
     for k, ref in enumerate(chunks):
         at = pl.multiple_of(jnp.bitwise_xor(place, k) * each, each)
         for i in range(per_device):
             rows_ref[i, pl.ds(at, each), :] = unpack(ref[i], each, channels).astype(jnp.float32)
-    rows = rows_ref[...].reshape(per_device * pixels, channels)
-    normed = layer_norm(rows, gain_ref[...]).astype(jnp.bfloat16)
-    packed = jnp.dot(normed, sw_ref[...], preferred_element_type=jnp.float32).astype(jnp.bfloat16)
-    tiles = tiles_of(channels)
-    blocks = [(i, start, width) for i in range(per_device) for start, width in tiles]
-
-    def part_of(i, which):
-        frame, start, width = blocks[i]
-        return packed[
-            frame * pixels : (frame + 1) * pixels, which * step + start : which * step + start + width
-        ]
+    return rows_ref[...].reshape(per_device * half_pixels, channels)
+
+
+def project_half(rows, gain, sw_ref):
+    normed = layer_norm(rows, gain).astype(jnp.bfloat16)
+    return jnp.dot(normed, sw_ref[...], preferred_element_type=jnp.float32).astype(jnp.bfloat16)
+
+
+def ready_kernel(halves, gain_ref, sw_ref, *rest):
+    chunks, (packed_ref, flipped_ref, rows_ref) = rest[:halves], rest[halves:]
+    channels = sw_ref.shape[0]
+    rows = gather_rows(chunks, rows_ref, channels)
+    packed_ref[...] = project_half(rows, gain_ref[...], sw_ref)
+    for i in range(rows_ref.shape[0]):
+        flipped_ref[i] = rows_ref[i].T
+
+
+def ready(gain, weights, chunks, pixels):
+    halves = len(chunks)
+    per_device = chunks[0].shape[0]
+    channels = weights.shape[0]
+    kind = chunks[0].dtype
+    half = pixels // 2
+    return pl.pallas_call(
+        functools.partial(ready_kernel, halves),
+        out_shape=[
+            pltpu.VMEM((per_device * half, weights.shape[1]), kind),
+            pltpu.VMEM((per_device, channels, half), jnp.float32),
+        ],
+        in_specs=[pl.BlockSpec()] + [VMEM] * (1 + halves),
+        out_specs=[VMEM] * 2,
+        scratch_shapes=[pltpu.VMEM((per_device, half, channels), jnp.float32)],
+        cost_estimate=pl.CostEstimate(
+            flops=2 * per_device * half * channels * 3 * channels,
+            bytes_accessed=2 << 20,
+            transcendentals=0,
+        ),
+        compiler_params=pltpu.CompilerParams(vmem_limit_bytes=LIMIT),
+        name="ready",
+    )(gain.reshape(1, channels), weights, *chunks)
+
+
+def spatial_kernel(halves, gain_ref, sw_ref, so_ref, packed_ref, flipped_ref, *rest):
+    chunks, (out_ref, rows_ref, att_ref) = rest[:halves], rest[halves:]
+    per_device, channels, pixels = out_ref.shape
+    half = pixels // 2
+    step = up(channels, LANES)
+    rows = gather_rows(chunks, rows_ref, channels)
+    late = project_half(rows, gain_ref[...], sw_ref)
+    blocks = [
+        (i, start, width, side)
+        for i in range(per_device)
+        for start, width in tiles_of(channels)
+        for side in range(2)
+    ]
+
+    def part_of(frame, which, start, width, side):
+        at = which * step + start
+        source = late if side else packed_ref
+        return source[frame * half : (frame + 1) * half, at : at + width]
+
+    def both(frame, which, start, width):
+        return jnp.concatenate(
+            [part_of(frame, which, start, width, side) for side in range(2)], axis=0
+        )
 
     def score(i):
+        frame, start, width, side = blocks[i]
         return lax.dot_general(
-            stack_heads(part_of(i, 0)), part_of(i, 1), NT, preferred_element_type=jnp.float32
+            stack_heads(part_of(frame, 0, start, width, side)),
+            both(frame, 1, start, width),
+            NT,
+            preferred_element_type=jnp.float32,
         )
 
     def mix(i, weights, norm):
-        frame, start, width = blocks[i]
-        mixed = jnp.dot(weights, part_of(i, 2), preferred_element_type=jnp.float32) * norm
-        att_ref[frame, :, start : start + width] = unstack_heads(mixed, width // HEAD_DIM).astype(
-            jnp.bfloat16
-        )
-
-    pipelined(len(blocks), score, mix)
+        frame, start, width, side = blocks[i]
+        mixed = jnp.dot(weights, both(frame, 2, start, width), preferred_element_type=jnp.float32) * norm
+        att_ref[frame, side * half : (side + 1) * half, start : start + width] = unstack_heads(
+            mixed, width // HEAD_DIM
+        ).astype(jnp.bfloat16)
+
+    pipelined(len(blocks), score, mix, SPATIAL_LEAD)
+    upper = lax.axis_index("pix") // halves
     for i in range(per_device):
         update = lax.dot_general(so_ref[...], att_ref[i], NT, preferred_element_type=jnp.float32)
-        out_ref[i] = (rows_ref[i].T + update).astype(jnp.bfloat16)
-
-
-def spatial(gain, weights, out_matrix, chunks, pixels):
-    pix_count = len(chunks)
+        here = pl.multiple_of(upper * half, half)
+        there = pl.multiple_of((1 - upper) * half, half)
+        out_ref[i, :, pl.ds(here, half)] = (flipped_ref[i] + update[:, :half]).astype(jnp.bfloat16)
+        out_ref[i, :, pl.ds(there, half)] = (rows_ref[i].T + update[:, half:]).astype(jnp.bfloat16)
+
+
+def spatial(gain, weights, out_matrix, packed, flipped, chunks, pixels):
+    halves = len(chunks)
     per_device = chunks[0].shape[0]
     channels = out_matrix.shape[0]
     kind = chunks[0].dtype
     return pl.pallas_call(
-        functools.partial(spatial_kernel, pix_count),
+        functools.partial(spatial_kernel, halves),
         out_shape=jax.ShapeDtypeStruct((per_device, channels, pixels), kind),
-        in_specs=[pl.BlockSpec()] + [VMEM] * (2 + pix_count),
+        in_specs=[pl.BlockSpec()] + [VMEM] * (4 + halves),
         out_specs=pl.BlockSpec(),
         scratch_shapes=[
-            pltpu.VMEM((per_device, pixels, channels), jnp.float32),
+            pltpu.VMEM((per_device, pixels // 2, channels), jnp.float32),
             pltpu.VMEM((per_device, pixels, channels), kind),
         ],
         cost_estimate=pl.CostEstimate(
@@ -438,7 +510,7 @@
         ),
         compiler_params=pltpu.CompilerParams(vmem_limit_bytes=LIMIT),
         name="spatial",
-    )(gain.reshape(1, channels), weights, out_matrix, *chunks)
+    )(gain.reshape(1, channels), weights, out_matrix, packed, flipped, *chunks)
 
 
 def both_ways(pairs, count):
@@ -471,20 +543,12 @@
     pixels = latents.shape[1] * pix_count
     gathered = clips > DIRECT_CLIPS or clips & (clips - 1) != 0
     x, a, b, p = prep(latents, sampled, clips, not gathered)
-    far_steps = ()
     if gathered:
         picks = [lax.all_gather(p, "clip", axis=0, tiled=True)]
     else:
         picks = [p]
-        far_steps = tuple(range(2, clips))
-        for step in far_steps:
-            distant = [
-                (i * pix_count + place, (i ^ step) * pix_count + place)
-                for i in range(clips)
-                if (i ^ step) - i > 1
-                for place in range(pix_count)
-            ]
-            picks.append(lax.ppermute(p, ("clip", "pix"), both_ways(distant, clips * pix_count)))
+        for step in range(2, clips):
+            picks.append(lax.ppermute(p, "clip", [(i, i ^ step) for i in range(clips)]))
     a = lax.ppermute(a, ("clip", "pix"), border_pairs(clips, pix_count, 0))
     b = lax.ppermute(b, ("clip", "pix"), border_pairs(clips, pix_count, 1))
     q, k, v, xg, tw, sw, to, so = local(
@@ -492,13 +556,18 @@
     )
     early_held = a.shape[0] + sum(pick.shape[0] for pick in picks)
     pairs = early(temporal_gain, tw, a, picks, latents.shape[1], up(early_held, 2))
-    sends = temporal(
-        (q, k, v, xg), pairs, temporal_gain, tw, to, b, clips, far_steps, early_held, pix_count
-    )
-    chunks = [sends[0]]
-    for step in range(1, pix_count):
-        chunks.append(lax.ppermute(sends[step], "pix", [(i, i ^ step) for i in range(pix_count)]))
-    return spatial(spatial_gain, sw, so, chunks, pixels).transpose(0, 2, 1)
+    rest = ((q, k, v, xg), pairs, temporal_gain, tw, to)
+    halves = pix_count // 2
+    *sends, late = temporal(*rest, b, clips, early_held, pix_count, True)
+
+    def swap(chunk, step):
+        return lax.ppermute(chunk, "pix", [(i, i ^ step) for i in range(pix_count)])
+
+    crossed = [swap(sends[k], halves + k) for k in range(halves)]
+    kept = temporal(*rest, late, clips, early_held, pix_count, False)
+    held = [kept[0]] + [swap(kept[k], k) for k in range(1, halves)]
+    packed, flipped = ready(spatial_gain, sw, held, pixels)
+    return spatial(spatial_gain, sw, so, packed, flipped, crossed, pixels).transpose(0, 2, 1)
 
 
 def solution(mesh):

time: 29 us -> 28.4 us (0.979)
  waiting for transfers between devices: 6.53 us -> 5.3 us
  Pallas kernels: 11 us -> 11.6 us
    ppermute x5, waiting for transfers between devices: 6.52 us -> 5.3 us  [the longest x3 3.66 us: swap(): return lax.ppermute(chunk, 'pix', [(i, i ^ step) for i in range(pix_count)])]
    pallas_call x3 -> x5, Pallas kernels: 8.91 us -> 9.51 us  [the longest x2 3.53 us: temporal(): pl.pallas_call(functools.partial(temporal_kernel, clips, early_held, pix_...]
  transfers between devices with their start and end apart: 7 -> 7, of which waited for: 3 -> 3; matrix products, arithmetic and copies ran while one was open for 0% -> 0% of each run, Pallas kernels for 12% -> 15%
where the time goes in v4:
time: 28.4 us; the launch traced here: 28.2 us
  Pallas kernels  11.6 us (41%)
  starting transfers between devices  10.5 us (37%)
  waiting for transfers between devices  5.3 us (19%)
  between operations  0.72 us (3%)
    ppermute x2, starting transfers between devices, body(): picks.append(lax.ppermute(p, 'clip', [(i, i ^ step) for i in range(clips)]))  5.51 us
    ppermute x3, waiting for transfers between devices, swap(): return lax.ppermute(chunk, 'pix', [(i, i ^ step) for i in range(pix_count)])  3.66 us
    pallas_call x2, Pallas kernels, temporal(): pl.pallas_call(functools.partial(temporal_kernel, clips, early_held, pix_...  3.53 us
    ppermute x1, starting transfers between devices, body(): a = lax.ppermute(a, ('clip', 'pix'), border_pairs(clips, pix_count, 0))  3.12 us
    pallas_call x1, Pallas kernels, spatial(): pl.pallas_call(functools.partial(spatial_kernel, halves), out_shape=jax.S...  2.79 us
    pallas_call x1, Pallas kernels, local(): pl.pallas_call(local_kernel, out_shape=[pltpu.VMEM((groups, 2, channels /...  2.41 us
    ppermute x3, starting transfers between devices, swap(): return lax.ppermute(chunk, 'pix', [(i, i ^ step) for i in range(pix_count)])  1.92 us
    ppermute x2, waiting for transfers between devices, body(): picks.append(lax.ppermute(p, 'clip', [(i, i ^ step) for i in range(clips)]))  1.64 us
  transfers between devices with their start and end apart: 7, of which 3 were waited for; matrix products, arithmetic and copies ran while one was open for 0% of the time, Pallas kernels for 15%

profile of v4, /device:TPU:0, one launch (start us, length us, event | category | flops | bytes accessed | tf_op | source)
XLA Modules:
  0.0 28.2 jit_solution(10061819404996290304)
XLA Ops:
  0.7 1.1 %prep.1 = (bf16[8,64,320]{2,1,0:T(8,128)(2,1)S(1)}, bf16[5,160,128]{2,1,0:T(8,128)(2,1)S(1)}, bf16[4,160,128]{2,1,0:T(8,128)(2,1)S(1)}, bf16[1,160,128]{2,1,0:T(8,128)(2,1)S(1)}) custom-call(bf16[8,64,320]{2,1,0:T(8,128)(2,1)} %x_hbm.1, s32[1]{0:T(128)S(6)} %copy.9.s_ref), custom_call_target="tpu_custom_call" | custom-call | tf_op jit(solution)/shard_map/prep/pallas_call | solution.py:133
  1.8 0.0 copy-start
  1.8 3.1 %collective-permute-start = (bf16[5,160,128]{2,1,0:T(8,128)(2,1)S(1)}, bf16[5,160,128]{2,1,0:T(8,128)(2,1)S(1)}, u32[]{:S(2)}, u32[]{:S(2)}) collective-permute-start(bf16[5,160,128]{2,1,0:T(8,128)(2,1)S(1)} %get-tuple-element.32), channel_id=1, source_target_pairs={{0,4},{1,5},{2,6},{3,7},{4,0},{5,1},{6,2},{7,3},{8,12},{9,13},{10,... | collective-permute-start | bytes 614408 | tf_op jit(solution)/shard_map/ppermute | solution.py:552
  4.9 0.0 collective-permute-start.3
  4.9 2.6 %collective-permute-start.1 = (bf16[1,160,128]{2,1,0:T(8,128)(2,1)S(1)}, bf16[1,160,128]{2,1,0:T(8,128)(2,1)S(1)}, u32[]{:S(2)}, u32[]{:S(2)}) collective-permute-start(bf16[1,160,128]{2,1,0:T(8,128)(2,1)S(1)} %get-tuple-element.33.rest_0_), channel_id=1, source_target_pairs={{0,8},{4,12},{8,0},{12,4},{1,9},{5,13},{9,1},{13,5},{2,10},{6,14},... | collective-permute-start | bytes 122888 | tf_op jit(solution)/shard_map/ppermute | solution.py:551
  7.5 2.9 %collective-permute-start.2 = (bf16[1,160,128]{2,1,0:T(8,128)(2,1)S(1)}, bf16[1,160,128]{2,1,0:T(8,128)(2,1)S(1)}, u32[]{:S(2)}, u32[]{:S(2)}) collective-permute-start(bf16[1,160,128]{2,1,0:T(8,128)(2,1)S(1)} %get-tuple-element.33.rest_0_), channel_id=1, source_target_pairs={{0,12},{4,8},{8,4},{12,0},{1,13},{5,9},{9,5},{13,1},{2,14},{6,10},... | collective-permute-start | bytes 122888 | tf_op jit(solution)/shard_map/ppermute | solution.py:551
  10.4 0.0 copy-done
  10.4 2.4 %local.1 = (bf16[8,2,160,128]{3,2,1,0:T(8,128)(2,1)S(1)}, bf16[512,320]{1,0:T(8,128)(2,1)S(1)}, bf16[512,320]{1,0:T(8,128)(2,1)S(1)}, f32[8,8,8,320]{3,2,1,0:T(8...) custom-call(bf16[8,64,320]{2,1,0:T(8,128)(2,1)S(1)} %get-tuple-eleme, ...), custom_call_target="tpu_custom_call" | custom-call | flops 314572800 | bytes 4194304 | tf_op jit(solution)/shard_map/local/pallas_call | solution.py:211
  12.8 1.6 %collective-permute-done.1.rest_1_ = bf16[1,160,128]{2,1,0:T(8,128)(2,1)S(1)} collective-permute-done((bf16[1,160,128]{2,1,0:T(8,128)(2,1)S(1)}, bf16[1,160,128]{2,1,0:T(8,128)(2,1)S(1)}, u32[]{:S(2)}, u32[]{:S(2)}) %collective-permute-start.1) | collective-permute-done | bytes 40992 | tf_op jit(solution)/shard_map/ppermute | solution.py:551
  14.5 0.0 collective-permute-done.2.rest_2_
  14.5 0.0 collective-permute-done.a_ref
  14.5 1.0 %early.1.kv_ref = bf16[512,768]{1,0:T(8,128)(2,1)S(1)} custom-call(f32[1,320]{1,0:T(1,128)S(1)} %reshape.5.gain_ref, bf16[320,1152]{1,0:T(8,128)(2,1)S(1)} %get-tuple-element.31.tw_ref, bf16[5,160,128]{2,1,0:T(8,128)(2,1)S(1)} %collective-permute-done.a_ref, bf16[1,160,128]{2,1,0:T(8,128)(2,1)S(1)} %get-tuple-element.33.rest_0_, ...), custom_call_target="tpu_custom_call" | custom-call | flops 209715200 | bytes 2097152 | tf_op jit(solution)/shard_map/early/pallas_call | solution.py:267
  15.5 0.0 collective-permute-done.3.b_ref
  15.5 1.9 %cross.1 = (bf16[2,160,128]{2,1,0:T(8,128)(2,1)S(1)}, bf16[2,160,128]{2,1,0:T(8,128)(2,1)S(1)}, bf16[256,768]{1,0:T(8,128)(2,1)S(1)}) custom-call(bf16[8,2,160,128]{3,2,1,0:T(8,128)(2,1)S(1)} %get-tuple-element.27.q_ref, bf16[512,320]{1,0:T(8,128)(2,1)S(1)} %get-tuple-element.28.k_ref, bf16[512,320]{1,0:T(8,128)(2,1)S(1)} %get-tuple-element.29.v_ref, ...), custom_call_target="tpu_custom_call" | custom-call | flops 209715200 | bytes 4194304 | tf_op jit(solution)/shard_map/cross/pallas_call | solution.py:377
  17.4 1.6 %near.1 = (bf16[2,160,128]{2,1,0:T(8,128)(2,1)S(1)}, bf16[2,160,128]{2,1,0:T(8,128)(2,1)S(1)}) custom-call(bf16[8,2,160,128]{3,2,1,0:T(8,128)(2,1)S(1)} %get-tuple-element.27.q_ref, bf16[512,320]{1,0:T(8,128)(2,1)S(1)} %get-tuple-element.28.k_ref, bf16[512,320]{1,0:T(8,128)(2,1)S(1)} %get-tuple-element.29.v_ref, ...), custom_call_target="tpu_custom_call" | custom-call | flops 209715200 | bytes 4194304 | tf_op jit(solution)/shard_map/near/pallas_call | solution.py:377
  19.0 0.0 copy-start.1
  19.0 0.1 collective-permute-start.4
  19.1 1.6 %collective-permute-start.5 = (bf16[2,160,128]{2,1,0:T(8,128)(2,1)S(1)}, bf16[2,160,128]{2,1,0:T(8,128)(2,1)S(1)}, u32[]{:S(2)}, u32[]{:S(2)}) collective-permute-start(bf16[2,160,128]{2,1,0:T(8,128)(2,1)S(1)} %get-tuple-element.41), channel_id=1, source_target_pairs={{0,2},{1,3},{2,0},{3,1},{4,6},{5,7},{6,4},{7,5},{8,10},{9,11},{10,... | collective-permute-start | bytes 245768 | tf_op jit(solution)/shard_map/ppermute | solution.py:564
  20.7 0.3 %collective-permute-start.6 = (bf16[2,160,128]{2,1,0:T(8,128)(2,1)S(1)}, bf16[2,160,128]{2,1,0:T(8,128)(2,1)S(1)}, u32[]{:S(2)}, u32[]{:S(2)}) collective-permute-start(bf16[2,160,128]{2,1,0:T(8,128)(2,1)S(1)} %get-tuple-element.42), channel_id=1, source_target_pairs={{0,3},{1,2},{2,1},{3,0},{4,7},{5,6},{6,5},{7,4},{8,11},{9,10},{10,... | collective-permute-start | bytes 245768 | tf_op jit(solution)/shard_map/ppermute | solution.py:564
  21.0 0.0 copy-done.1
  21.0 0.0 collective-permute-done.4.rest_1_
  21.0 0.8 %ready.1 = (bf16[256,1152]{1,0:T(8,128)(2,1)S(1)}, f32[2,320,128]{2,1,0:T(8,128)S(1)}) custom-call(f32[1,320]{1,0:T(1,128)S(1)} %reshape.4.gain_ref, bf16[320,1152]{1,0:T(8,128)(2,1)S(1)} %get-tuple-element.25.sw_ref, bf16[2,160,128]{2,1,0:T(8,128)(2,1)S(1)} %get-tuple-element.37.rest_0_, bf16[2,160,128]{2,1,0:T(8,128)(2,1)S(1)} %collective-permute-done.4.rest_1_), custom_call_target="tpu_custom_call" | custom-call | flops 157286400 | bytes 2097152 | tf_op jit(solution)/shard_map/ready/pallas_call | solution.py:423
  21.8 2.5 %collective-permute-done.5.rest_0_ = bf16[2,160,128]{2,1,0:T(8,128)(2,1)S(1)} collective-permute-done((bf16[2,160,128]{2,1,0:T(8,128)(2,1)S(1)}, bf16[2,160,128]{2,1,0:T(8,128)(2,1)S(1)}, u32[]{:S(2)}, u32[]{:S(2)}) %collective-permute-start.5) | collective-permute-done | bytes 81952 | tf_op jit(solution)/shard_map/ppermute | solution.py:564
  24.3 1.2 %collective-permute-done.6.rest_1_ = bf16[2,160,128]{2,1,0:T(8,128)(2,1)S(1)} collective-permute-done((bf16[2,160,128]{2,1,0:T(8,128)(2,1)S(1)}, bf16[2,160,128]{2,1,0:T(8,128)(2,1)S(1)}, u32[]{:S(2)}, u32[]{:S(2)}) %collective-permute-start.6) | collective-permute-done | bytes 81952 | tf_op jit(solution)/shard_map/ppermute | solution.py:564
  25.4 2.8 %spatial.1 = bf16[2,320,256]{2,1,0:T(8,128)(2,1)} custom-call(f32[1,320]{1,0:T(1,128)S(1)} %reshape.4.gain_ref, bf16[320,1152]{1,0:T(8,128)(2,1)S(1)} %get-tuple-element.25.sw_ref, bf16[320,320]{1,0:T(8,128)(2,1)S(1)} %get-tuple-element.26.so_ref, bf16[256,1152]{1,0:T(8,128)(2,1)S(1)} %get-tuple-element.39.packed_ref, ...), custom_call_target="tpu_custom_call" | custom-call | flops 587202560 | bytes 4194304 | tf_op jit(solution)/shard_map/spatial/pallas_call | solution.py:497
  (2 shorter events, 0.0 us)
Async XLA Ops:
  1.8 8.6 %copy-start = (f32[320]{0:T(512)S(1)}, f32[320]{0:T(512)}, u32[]{:S(2)}) copy-start(f32[320]{0:T(512)} %param.10) | copy-start | bytes 3844
  1.8 12.7 %collective-permute-start = (bf16[5,160,128]{2,1,0:T(8,128)(2,1)S(1)}, bf16[5,160,128]{2,1,0:T(8,128)(2,1)S(1)}, u32[]{:S(2)}, u32[]{:S(2)}) collective-permute-start(bf16[5,160,128]{2,1,0:T(8,128)(2,1)S(1)} %get-tuple-element.32), channel_id=1, source_target_pairs={{0,4},{1,5},{2,6},{3,7},{4,0},{5,1},{6,2},{7,3},{8,12},{9,13},{10,... | collective-permute-start | bytes 614408 | tf_op jit(solution)/shard_map/ppermute | solution.py:552
  4.9 10.6 %collective-permute-start.3 = (bf16[4,160,128]{2,1,0:T(8,128)(2,1)S(1)}, bf16[4,160,128]{2,1,0:T(8,128)(2,1)S(1)}, u32[]{:S(2)}, u32[]{:S(2)}) collective-permute-start(bf16[4,160,128]{2,1,0:T(8,128)(2,1)S(1)} %get-tuple-element.35), channel_id=1, source_target_pairs={{0,1},{1,0},{2,3},{3,2},{4,8},{5,9},{6,10},{7,11},{8,4},{9,5},{10,... | collective-permute-start | bytes 491528 | tf_op jit(solution)/shard_map/ppermute | solution.py:553
  4.9 9.6 %collective-permute-start.1 = (bf16[1,160,128]{2,1,0:T(8,128)(2,1)S(1)}, bf16[1,160,128]{2,1,0:T(8,128)(2,1)S(1)}, u32[]{:S(2)}, u32[]{:S(2)}) collective-permute-start(bf16[1,160,128]{2,1,0:T(8,128)(2,1)S(1)} %get-tuple-element.33.rest_0_), channel_id=1, source_target_pairs={{0,8},{4,12},{8,0},{12,4},{1,9},{5,13},{9,1},{13,5},{2,10},{6,14},... | collective-permute-start | bytes 122888 | tf_op jit(solution)/shard_map/ppermute | solution.py:551
  7.5 7.0 %collective-permute-start.2 = (bf16[1,160,128]{2,1,0:T(8,128)(2,1)S(1)}, bf16[1,160,128]{2,1,0:T(8,128)(2,1)S(1)}, u32[]{:S(2)}, u32[]{:S(2)}) collective-permute-start(bf16[1,160,128]{2,1,0:T(8,128)(2,1)S(1)} %get-tuple-element.33.rest_0_), channel_id=1, source_target_pairs={{0,12},{4,8},{8,4},{12,0},{1,13},{5,9},{9,5},{13,1},{2,14},{6,10},... | collective-permute-start | bytes 122888 | tf_op jit(solution)/shard_map/ppermute | solution.py:551
  19.0 1.9 %copy-start.1 = (f32[320]{0:T(512)S(1)}, f32[320]{0:T(512)}, u32[]{:S(2)}) copy-start(f32[320]{0:T(512)} %param.13) | copy-start | bytes 3844
  19.0 1.9 %collective-permute-start.4 = (bf16[2,160,128]{2,1,0:T(8,128)(2,1)S(1)}, bf16[2,160,128]{2,1,0:T(8,128)(2,1)S(1)}, u32[]{:S(2)}, u32[]{:S(2)}) collective-permute-start(bf16[2,160,128]{2,1,0:T(8,128)(2,1)S(1)} %get-tuple-element.38), channel_id=1, source_target_pairs={{0,1},{1,0},{2,3},{3,2},{4,5},{5,4},{6,7},{7,6},{8,9},{9,8},{10,11... | collective-permute-start | bytes 245768 | tf_op jit(solution)/shard_map/ppermute | solution.py:564
  19.1 5.1 %collective-permute-start.5 = (bf16[2,160,128]{2,1,0:T(8,128)(2,1)S(1)}, bf16[2,160,128]{2,1,0:T(8,128)(2,1)S(1)}, u32[]{:S(2)}, u32[]{:S(2)}) collective-permute-start(bf16[2,160,128]{2,1,0:T(8,128)(2,1)S(1)} %get-tuple-element.41), channel_id=1, source_target_pairs={{0,2},{1,3},{2,0},{3,1},{4,6},{5,7},{6,4},{7,5},{8,10},{9,11},{10,... | collective-permute-start | bytes 245768 | tf_op jit(solution)/shard_map/ppermute | solution.py:564
  20.7 4.7 %collective-permute-start.6 = (bf16[2,160,128]{2,1,0:T(8,128)(2,1)S(1)}, bf16[2,160,128]{2,1,0:T(8,128)(2,1)S(1)}, u32[]{:S(2)}, u32[]{:S(2)}) collective-permute-start(bf16[2,160,128]{2,1,0:T(8,128)(2,1)S(1)} %get-tuple-element.42), channel_id=1, source_target_pairs={{0,3},{1,2},{2,1},{3,0},{4,7},{5,6},{6,5},{7,4},{8,11},{9,10},{10,... | collective-permute-start | bytes 245768 | tf_op jit(solution)/shard_map/ppermute | solution.py:564

commit v5 on v4

--- a/solution.py
+++ b/solution.py
@@ -15,8 +15,9 @@
 NEG = -1e30
 DIRECT_CLIPS = 4
 LIMIT = 24 << 20
-LEAD = 4
+LEAD = 8
 SPATIAL_LEAD = 2
+SIDES = ((0, 1),)
 FAR = pl.BlockSpec(memory_space=pltpu.HBM)
 VMEM = pl.BlockSpec(memory_space=pltpu.VMEM)
 NT = (((1,), (1,)), ((), ()))
@@ -32,6 +33,28 @@
 
 def tiles_of(channels):
     return [(start, min(LANES, channels - start)) for start in range(0, channels, LANES)]
+
+
+class Tile:
+    def __init__(self, query, key, value, start, width):
+        self.query, self.key, self.value = query, key, value
+        self.start, self.width = start, width
+        self.held, self.head = width // HEAD_DIM, start // HEAD_DIM
+
+
+def plan(channels):
+    whole = channels // LANES * LANES
+    tiles = [
+        Tile(start, whole + start, 2 * whole + start, start, LANES) for start in range(0, whole, LANES)
+    ]
+    if channels > whole:
+        tiles.append(Tile(3 * whole, 3 * whole + LANES, 3 * whole, whole, channels - whole))
+    return tiles
+
+
+def planned_width(channels):
+    whole = channels // LANES * LANES
+    return 3 * whole + (2 * LANES if channels > whole else 0)
 
 
 def pack(rows):
@@ -64,8 +87,7 @@
     return (lax.broadcasted_iota(jnp.int32, shape, 1) // HEAD_DIM) == slot
 
 
-def stack_heads(queries):
-    held = queries.shape[1] // HEAD_DIM
+def stack_heads(queries, held):
     if held == 1:
         return queries
     zero = jnp.zeros_like(queries)
@@ -148,7 +170,7 @@
 
 def local_kernel(
     x_ref, gain_ref, tq_hbm, to_hbm, sq_hbm, so_hbm,
-    q_ref, k_ref, v_ref, xg_ref, tw_ref, sw_ref, to_ref, so_ref,
+    q_ref, kv_ref, xg_ref, tw_ref, sw_ref, to_ref, so_ref,
     tq_ref, sq_ref, sp_ref, normed_ref, sems,
 ):
     copies = [
@@ -168,17 +190,17 @@
         for g in range(groups):
             xg_ref[g, f] = values[g * SUB : (g + 1) * SUB]
             normed_ref[g, f] = normed[g * SUB : (g + 1) * SUB]
-    step = up(channels, LANES)
+    whole = channels // LANES * LANES
 
     def spread(source, target):
-        for part in range(3):
-            target[:, part * step : part * step + channels] = source[
-                :, part * channels : (part + 1) * channels
-            ]
-            if step > channels:
-                target[:, part * step + channels : (part + 1) * step] = jnp.zeros(
-                    (channels, step - channels), target.dtype
-                )
+        parts = [source[:, i * channels : (i + 1) * channels] for i in range(3)]
+        for i, part in enumerate(parts):
+            target[:, i * whole : (i + 1) * whole] = part[:, :whole]
+        if channels > whole:
+            queries, keys, values = (part[:, whole:] for part in parts)
+            tail = jnp.concatenate([values, queries], axis=1)
+            target[:, 3 * whole : 3 * whole + LANES] = tail
+            target[:, 3 * whole + LANES :] = jnp.concatenate([jnp.zeros_like(keys), keys], axis=1)
 
     copies[0].wait()
     spread(tq_ref, tw_ref)
@@ -186,14 +208,15 @@
     packed = jnp.dot(rows, tw_ref[...], preferred_element_type=jnp.float32).astype(jnp.bfloat16)
     own = frames * SUB
     for g in range(groups):
-        for start, width in tiles_of(channels):
+        for tile in plan(channels):
             for half in range(2):
                 at = g * own + half * (own // 2)
-                stacked = stack_heads(packed[at : at + own // 2, start : start + width])
-                first = start // HEAD_DIM * (own // 2)
-                q_ref[g, half, first : first + stacked.shape[0], :width] = stacked
-    k_ref[...] = packed[:, step : step + channels]
-    v_ref[...] = packed[:, 2 * step : 2 * step + channels]
+                stacked = stack_heads(
+                    packed[at : at + own // 2, tile.query : tile.query + LANES], tile.held
+                )
+                first = tile.head * (own // 2)
+                q_ref[g, half, first : first + stacked.shape[0], :] = stacked
+    kv_ref[...] = packed[:, whole:]
     copies[1].wait()
     spread(sq_ref, sw_ref)
     copies[2].wait()
@@ -206,17 +229,18 @@
     groups = pixels // SUB
     count = frames * pixels
     kind = latents.dtype
-    wide = (channels, 3 * up(channels, LANES))
+    wide = (channels, planned_width(channels))
     square = (channels, channels)
+    pair_width = wide[1] - channels // LANES * LANES
     return pl.pallas_call(
         local_kernel,
         out_shape=[pltpu.VMEM((groups, 2, channels // HEAD_DIM * frames * SUB // 2, LANES), kind)]
-        + [pltpu.VMEM((count, channels), kind)] * 2
+        + [pltpu.VMEM((count, pair_width), kind)]
         + [pltpu.VMEM((groups, frames, SUB, channels), jnp.float32)]
         + [pltpu.VMEM(wide, kind)] * 2
         + [pltpu.VMEM(square, kind)] * 2,
         in_specs=[VMEM, pl.BlockSpec()] + [FAR] * 4,
-        out_specs=[VMEM] * 8,
+        out_specs=[VMEM] * 7,
         scratch_shapes=[
             pltpu.VMEM(temporal_qkv.shape, kind),
             pltpu.VMEM(spatial_qkv.shape, kind),
@@ -246,9 +270,9 @@
     for j in range(len(dense), slots):
         for g in range(groups):
             normed_ref[g, j] = jnp.zeros((SUB, channels), jnp.float32)
-    step = up(channels, LANES)
+    whole = channels // LANES * LANES
     rows = normed_ref[...].reshape(groups * slots * SUB, channels).astype(jnp.bfloat16)
-    return jnp.dot(rows, tw_ref[:, step:], preferred_element_type=jnp.float32).astype(jnp.bfloat16)
+    return jnp.dot(rows, tw_ref[:, whole:], preferred_element_type=jnp.float32).astype(jnp.bfloat16)
 
 
 def early_kernel(gain_ref, tw_ref, a_ref, *rest):
@@ -266,7 +290,7 @@
     kind = weights.dtype
     return pl.pallas_call(
         early_kernel,
-        out_shape=pltpu.VMEM((pixels * slots, 2 * up(channels, LANES)), kind),
+        out_shape=pltpu.VMEM((pixels * slots, weights.shape[1] - channels // LANES * LANES), kind),
         in_specs=[pl.BlockSpec()] + [VMEM] * (2 + len(picks)),
         out_specs=VMEM,
         scratch_shapes=[pltpu.VMEM((groups, slots, SUB, channels), jnp.float32)],
@@ -279,25 +303,30 @@
 
 
 def temporal_kernel(
-    clips, early_held, pix_count, cross,
-    q_ref, k_ref, v_ref, xg_ref, kv_ref, gain_ref, tw_ref, to_ref, b_ref, *rest,
+    clips, early_held, late_held, pix_count, cross,
+    q_ref, own_ref, xg_ref, kv_ref, gain_ref, tw_ref, to_ref, *rest,
 ):
     halves = pix_count // 2
-    sends, rest = rest[:halves], rest[halves:]
+    scratch = 4 if cross else 2
+    last_refs, sends, rest = (
+        rest[: len(rest) - halves - scratch],
+        rest[len(rest) - halves - scratch : len(rest) - scratch],
+        rest[len(rest) - scratch :],
+    )
     groups, frames, _, channels = xg_ref.shape
     pixels = groups * SUB
     _, _, first_there, second_there = neighbours(clips)
     if cross:
         late_ref, normed_ref, att_ref, rows_ref = rest
-        dense = [b_ref[i] for i in range(HALO)]
+        dense = [ref[i] for ref in last_refs for i in range(ref.shape[0])]
         late_ref[...] = remote_pairs(dense, gain_ref[...], tw_ref, normed_ref, pixels)
     else:
-        late_ref = b_ref
+        (late_ref,) = last_refs
         att_ref, rows_ref = rest
     place = lax.axis_index("pix")
     upper = place // halves
     half = 1 - upper if cross else upper
-    step = up(channels, LANES)
+    whole = channels // LANES * LANES
 
     part = frames // 2
     mine, own = part * SUB, frames * SUB
@@ -309,42 +338,37 @@
     slot = column // SUB - frames
     usable &= (slot < 0) | (slot >= HALO) | first_there
     usable &= (slot < early_held) | (slot >= soon // SUB)
-    usable &= (slot < soon // SUB) | second_there
+    usable &= (slot < soon // SUB) | (slot >= soon // SUB + HALO) | second_there
+    usable &= slot < soon // SUB + late_held
     bias = jnp.where(usable, 0.0, NEG).astype(jnp.float32)
 
-    blocks = [(g, start, width) for g in range(groups) for start, width in tiles_of(channels)]
-
-    def score(i):
-        g, start, width = blocks[i]
-        span = slice(start, start + width)
-        queries = q_ref[
-            g, half, start // HEAD_DIM * mine : (start + width) // HEAD_DIM * mine, :width
-        ]
-        keys = jnp.concatenate(
+    blocks = [(g, tile) for g in range(groups) for tile in plan(channels)]
+
+    def pairs_of(g, column):
+        span = slice(column - whole, column - whole + LANES)
+        return jnp.concatenate(
             [
-                k_ref[g * own : (g + 1) * own, span],
+                own_ref[g * own : (g + 1) * own, span],
                 kv_ref[g * soon : (g + 1) * soon, span],
                 late_ref[g * more : (g + 1) * more, span],
             ],
             axis=0,
         )
-        scores = lax.dot_general(queries, keys, NT, preferred_element_type=jnp.float32)
-        return scores + jnp.concatenate([bias] * (width // HEAD_DIM), axis=0)
+
+    def score(i):
+        g, tile = blocks[i]
+        queries = q_ref[g, half, tile.head * mine : (tile.head + tile.held) * mine, :]
+        scores = lax.dot_general(
+            queries, pairs_of(g, tile.key), NT, preferred_element_type=jnp.float32
+        )
+        return scores + jnp.concatenate([bias] * tile.held, axis=0)
 
     def mix(i, weights, norm):
-        g, start, width = blocks[i]
-        values = jnp.concatenate(
-            [
-                v_ref[g * own : (g + 1) * own, start : start + width],
-                kv_ref[g * soon : (g + 1) * soon, step + start : step + start + width],
-                late_ref[g * more : (g + 1) * more, step + start : step + start + width],
-            ],
-            axis=0,
-        )
-        mixed = jnp.dot(weights, values, preferred_element_type=jnp.float32) * norm
-        att_ref[g * mine : (g + 1) * mine, start : start + width] = unstack_heads(
-            mixed, width // HEAD_DIM
-        ).astype(jnp.bfloat16)
+        g, tile = blocks[i]
+        mixed = jnp.dot(weights, pairs_of(g, tile.value), preferred_element_type=jnp.float32) * norm
+        att_ref[g * mine : (g + 1) * mine, tile.start : tile.start + tile.width] = unstack_heads(
+            mixed, tile.held
+        )[:, : tile.width].astype(jnp.bfloat16)
 
     pipelined(len(blocks), score, mix, LEAD)
     update = jnp.dot(att_ref[...], to_ref[...], preferred_element_type=jnp.float32)
@@ -359,8 +383,10 @@
             ref[i] = pack(rows_ref[target * per_device + i].astype(jnp.bfloat16))
 
 
-def temporal(parts, pairs, gain, weights, out_matrix, last, clips, early_held, pix_count, cross):
-    q, k, v, xg = parts
+def temporal(
+    parts, pairs, gain, weights, out_matrix, last, clips, early_held, late_held, pix_count, cross
+):
+    q, own, xg = parts
     groups, frames, _, channels = xg.shape
     pixels = groups * SUB
     count = frames * pixels
@@ -372,12 +398,13 @@
         pltpu.VMEM((frames // 2, pixels, channels), jnp.float32),
     ]
     if cross:
-        out_shape = out_shape + [pltpu.VMEM((pixels * HALO, 2 * up(channels, LANES)), kind)]
-        scratch = [pltpu.VMEM((groups, HALO, SUB, channels), jnp.float32)] + scratch
+        slots = up(late_held, 2)
+        out_shape = out_shape + [pltpu.VMEM((pixels * slots, pairs.shape[1]), kind)]
+        scratch = [pltpu.VMEM((groups, slots, SUB, channels), jnp.float32)] + scratch
     return pl.pallas_call(
-        functools.partial(temporal_kernel, clips, early_held, pix_count, cross),
+        functools.partial(temporal_kernel, clips, early_held, late_held, pix_count, cross),
         out_shape=out_shape,
-        in_specs=[VMEM] * 5 + [pl.BlockSpec()] + [VMEM] * 3,
+        in_specs=[VMEM] * 4 + [pl.BlockSpec()] + [VMEM] * (2 + len(last)),
         out_specs=[VMEM] * len(out_shape),
         scratch_shapes=scratch,
         cost_estimate=pl.CostEstimate(
@@ -385,7 +412,7 @@
         ),
         compiler_params=pltpu.CompilerParams(vmem_limit_bytes=LIMIT),
         name="cross" if cross else "near",
-    )(q, k, v, xg, pairs, gain.reshape(1, channels), weights, out_matrix, last)
+    )(q, own, xg, pairs, gain.reshape(1, channels), weights, out_matrix, *last)
 
 
 def gather_rows(chunks, rows_ref, channels):
@@ -443,41 +470,43 @@
     chunks, (out_ref, rows_ref, att_ref) = rest[:halves], rest[halves:]
     per_device, channels, pixels = out_ref.shape
     half = pixels // 2
-    step = up(channels, LANES)
     rows = gather_rows(chunks, rows_ref, channels)
     late = project_half(rows, gain_ref[...], sw_ref)
     blocks = [
-        (i, start, width, side)
+        (i, tile, sides)
         for i in range(per_device)
-        for start, width in tiles_of(channels)
-        for side in range(2)
+        for tile in plan(channels)
+        for sides in SIDES
     ]
 
-    def part_of(frame, which, start, width, side):
-        at = which * step + start
-        source = late if side else packed_ref
-        return source[frame * half : (frame + 1) * half, at : at + width]
-
-    def both(frame, which, start, width):
+    def part_of(frame, column, sides):
         return jnp.concatenate(
-            [part_of(frame, which, start, width, side) for side in range(2)], axis=0
+            [
+                (late if side else packed_ref)[
+                    frame * half : (frame + 1) * half, column : column + LANES
+                ]
+                for side in sides
+            ],
+            axis=0,
         )
 
     def score(i):
-        frame, start, width, side = blocks[i]
+        frame, tile, sides = blocks[i]
         return lax.dot_general(
-            stack_heads(part_of(frame, 0, start, width, side)),
-            both(frame, 1, start, width),
+            stack_heads(part_of(frame, tile.query, sides), tile.held),
+            part_of(frame, tile.key, (0, 1)),
             NT,
             preferred_element_type=jnp.float32,
         )
 
     def mix(i, weights, norm):
-        frame, start, width, side = blocks[i]
-        mixed = jnp.dot(weights, both(frame, 2, start, width), preferred_element_type=jnp.float32) * norm
-        att_ref[frame, side * half : (side + 1) * half, start : start + width] = unstack_heads(
-            mixed, width // HEAD_DIM
-        ).astype(jnp.bfloat16)
+        frame, tile, sides = blocks[i]
+        values = part_of(frame, tile.value, (0, 1))
+        mixed = jnp.dot(weights, values, preferred_element_type=jnp.float32) * norm
+        first = sides[0] * half
+        att_ref[frame, first : first + len(sides) * half, tile.start : tile.start + tile.width] = (
+            unstack_heads(mixed, tile.held)[:, : tile.width].astype(jnp.bfloat16)
+        )
 
     pipelined(len(blocks), score, mix, SPATIAL_LEAD)
     upper = lax.axis_index("pix") // halves
@@ -544,29 +573,33 @@
     gathered = clips > DIRECT_CLIPS or clips & (clips - 1) != 0
     x, a, b, p = prep(latents, sampled, clips, not gathered)
     if gathered:
-        picks = [lax.all_gather(p, "clip", axis=0, tiled=True)]
+        soon, last = [], [lax.all_gather(p, "clip", axis=0, tiled=True)]
     else:
-        picks = [p]
+        soon, last = [], [p]
         for step in range(2, clips):
-            picks.append(lax.ppermute(p, "clip", [(i, i ^ step) for i in range(clips)]))
+            pick = lax.ppermute(p, "clip", [(i, i ^ step) for i in range(clips)])
+            (soon if step == 2 else last).append(pick)
     a = lax.ppermute(a, ("clip", "pix"), border_pairs(clips, pix_count, 0))
     b = lax.ppermute(b, ("clip", "pix"), border_pairs(clips, pix_count, 1))
-    q, k, v, xg, tw, sw, to, so = local(
+    q, own, xg, tw, sw, to, so = local(
         x, temporal_gain, temporal_qkv, temporal_out, spatial_qkv, spatial_out
     )
-    early_held = a.shape[0] + sum(pick.shape[0] for pick in picks)
-    pairs = early(temporal_gain, tw, a, picks, latents.shape[1], up(early_held, 2))
-    rest = ((q, k, v, xg), pairs, temporal_gain, tw, to)
+    last = [b] + last
+    early_held = sum(part.shape[0] for part in [a] + soon)
+    late_held = sum(part.shape[0] for part in last)
+    pairs = early(temporal_gain, tw, a, soon, latents.shape[1], up(early_held, 2))
+    rest = ((q, own, xg), pairs, temporal_gain, tw, to)
+    held = (clips, early_held, late_held, pix_count)
     halves = pix_count // 2
-    *sends, late = temporal(*rest, b, clips, early_held, pix_count, True)
+    *sends, late = temporal(*rest, last, *held, True)
 
     def swap(chunk, step):
         return lax.ppermute(chunk, "pix", [(i, i ^ step) for i in range(pix_count)])
 
     crossed = [swap(sends[k], halves + k) for k in range(halves)]
-    kept = temporal(*rest, late, clips, early_held, pix_count, False)
-    held = [kept[0]] + [swap(kept[k], k) for k in range(1, halves)]
-    packed, flipped = ready(spatial_gain, sw, held, pixels)
+    kept = temporal(*rest, [late], *held, False)
+    here = [kept[0]] + [swap(kept[k], k) for k in range(1, halves)]
+    packed, flipped = ready(spatial_gain, sw, here, pixels)
     return spatial(spatial_gain, sw, so, packed, flipped, crossed, pixels).transpose(0, 2, 1)
 
 

time: 28.4 us -> 28.1 us (0.989)
  Pallas kernels: 11.6 us -> 11.1 us
  transfers between devices with their start and end apart: 7 -> 7, of which waited for: 3 -> 3; matrix products, arithmetic and copies ran while one was open for 0% -> 0% of each run, Pallas kernels for 15% -> 14%
where the time goes in v5:
time: 28.1 us; the launch traced here: 27.9 us
  Pallas kernels  11.1 us (40%)
  starting transfers between devices  10.5 us (37%)
  waiting for transfers between devices  5.48 us (20%)
  between operations  0.73 us (3%)
    ppermute x2, starting transfers between devices, body(): pick = lax.ppermute(p, 'clip', [(i, i ^ step) for i in range(clips)])  5.51 us
    ppermute x3, waiting for transfers between devices, swap(): return lax.ppermute(chunk, 'pix', [(i, i ^ step) for i in range(pix_count)])  3.7 us
    pallas_call x2, Pallas kernels, temporal(): pl.pallas_call(functools.partial(temporal_kernel, clips, early_held, late...  3.55 us
    ppermute x1, starting transfers between devices, body(): a = lax.ppermute(a, ('clip', 'pix'), border_pairs(clips, pix_count, 0))  3.12 us
    pallas_call x1, Pallas kernels, spatial(): pl.pallas_call(functools.partial(spatial_kernel, halves), out_shape=jax.S...  2.65 us
    pallas_call x1, Pallas kernels, local(): pl.pallas_call(local_kernel, out_shape=[pltpu.VMEM((groups, 2, channels /...  2.27 us
    ppermute x3, starting transfers between devices, swap(): return lax.ppermute(chunk, 'pix', [(i, i ^ step) for i in range(pix_count)])  1.92 us
    ppermute x2, waiting for transfers between devices, body(): pick = lax.ppermute(p, 'clip', [(i, i ^ step) for i in range(clips)])  1.78 us
  transfers between devices with their start and end apart: 7, of which 3 were waited for; matrix products, arithmetic and copies ran while one was open for 0% of the time, Pallas kernels for 14%

profile of v5, /device:TPU:0, one launch (start us, length us, event | category | flops | bytes accessed | tf_op | source)
XLA Modules:
  0.0 27.9 jit_solution(787066544090666603)
XLA Ops:
  0.7 1.1 %prep.1 = (bf16[8,64,320]{2,1,0:T(8,128)(2,1)S(1)}, bf16[5,160,128]{2,1,0:T(8,128)(2,1)S(1)}, bf16[4,160,128]{2,1,0:T(8,128)(2,1)S(1)}, bf16[1,160,128]{2,1,0:T(8,128)(2,1)S(1)}) custom-call(bf16[8,64,320]{2,1,0:T(8,128)(2,1)} %x_hbm.1, s32[1]{0:T(128)S(6)} %copy.9.s_ref), custom_call_target="tpu_custom_call" | custom-call | tf_op jit(solution)/shard_map/prep/pallas_call | solution.py:155
  1.8 0.0 copy-start
  1.8 3.1 %collective-permute-start = (bf16[5,160,128]{2,1,0:T(8,128)(2,1)S(1)}, bf16[5,160,128]{2,1,0:T(8,128)(2,1)S(1)}, u32[]{:S(2)}, u32[]{:S(2)}) collective-permute-start(bf16[5,160,128]{2,1,0:T(8,128)(2,1)S(1)} %get-tuple-element.30), channel_id=1, source_target_pairs={{0,4},{1,5},{2,6},{3,7},{4,0},{5,1},{6,2},{7,3},{8,12},{9,13},{10,... | collective-permute-start | bytes 614408 | tf_op jit(solution)/shard_map/ppermute | solution.py:582
  4.9 0.0 collective-permute-start.2
  4.9 2.6 %collective-permute-start.1 = (bf16[1,160,128]{2,1,0:T(8,128)(2,1)S(1)}, bf16[1,160,128]{2,1,0:T(8,128)(2,1)S(1)}, u32[]{:S(2)}, u32[]{:S(2)}) collective-permute-start(bf16[1,160,128]{2,1,0:T(8,128)(2,1)S(1)} %get-tuple-element.31.rest_1_), channel_id=1, source_target_pairs={{0,8},{4,12},{8,0},{12,4},{1,9},{5,13},{9,1},{13,5},{2,10},{6,14},... | collective-permute-start | bytes 122888 | tf_op jit(solution)/shard_map/ppermute | solution.py:580
  7.5 2.9 %collective-permute-start.3 = (bf16[1,160,128]{2,1,0:T(8,128)(2,1)S(1)}, bf16[1,160,128]{2,1,0:T(8,128)(2,1)S(1)}, u32[]{:S(2)}, u32[]{:S(2)}) collective-permute-start(bf16[1,160,128]{2,1,0:T(8,128)(2,1)S(1)} %get-tuple-element.31.rest_1_), channel_id=1, source_target_pairs={{0,12},{4,8},{8,4},{12,0},{1,13},{5,9},{9,5},{13,1},{2,14},{6,10},... | collective-permute-start | bytes 122888 | tf_op jit(solution)/shard_map/ppermute | solution.py:580
  10.4 0.0 copy-done
  10.4 2.3 %local.1 = (bf16[8,2,160,128]{3,2,1,0:T(8,128)(2,1)S(1)}, bf16[512,768]{1,0:T(8,128)(2,1)S(1)}, f32[8,8,8,320]{3,2,1,0:T(8,128)S(1)}, bf16[320,1024]{1,0:T(8,128...) custom-call(bf16[8,64,320]{2,1,0:T(8,128)(2,1)S(1)} %get-tuple-element.23.x_re, ...), custom_call_target="tpu_custom_call" | custom-call | flops 314572800 | bytes 4194304 | tf_op jit(solution)/shard_map/local/pallas_call | solution.py:235
  12.7 1.8 %collective-permute-done.1.rest_0_ = bf16[1,160,128]{2,1,0:T(8,128)(2,1)S(1)} collective-permute-done((bf16[1,160,128]{2,1,0:T(8,128)(2,1)S(1)}, bf16[1,160,128]{2,1,0:T(8,128)(2,1)S(1)}, u32[]{:S(2)}, u32[]{:S(2)}) %collective-permute-start.1) | collective-permute-done | bytes 40992 | tf_op jit(solution)/shard_map/ppermute | solution.py:580
  14.5 0.0 collective-permute-done.a_ref
  14.5 0.8 %early.1.kv_ref = bf16[384,768]{1,0:T(8,128)(2,1)S(1)} custom-call(f32[1,320]{1,0:T(1,128)S(1)} %reshape.5.gain_ref, bf16[320,1024]{1,0:T(8,128)(2,1)S(1)} %get-tuple-element.29.tw_ref, bf16[5,160,128]{2,1,0:T(8,128)(2,1)S(1)} %collective-permute-done.a_ref, bf16[1,160,128]{2,1,0:T(8,128)(2,1)S(1)} %collective-permute-done.1.rest_0_), custom_call_target="tpu_custom_call" | custom-call | flops 157286400 | bytes 2097152 | tf_op jit(solution)/shard_map/early/pallas_call | solution.py:291
  15.3 0.0 collective-permute-done.3.rest_2_
  15.3 0.0 collective-permute-done.2.rest_0_
  15.3 2.1 %cross.1 = (bf16[2,160,128]{2,1,0:T(8,128)(2,1)S(1)}, bf16[2,160,128]{2,1,0:T(8,128)(2,1)S(1)}, bf16[384,768]{1,0:T(8,128)(2,1)S(1)}) custom-call(bf16[8,2,160,128]{3,2,1,0:T(8,128)(2,1)S(1)} %get-tuple-element.26.q_ref, bf16[512,768]{1,0:T(8,128)(2,1)S(1)} %get-tuple-element.27.own_ref, f32[8,8,8,320]{3,2,1,0:T(8,128)S(1)} %get-tuple-element.28.xg_ref, ...), custom_call_target="tpu_custom_call" | custom-call | flops 209715200 | bytes 4194304 | tf_op jit(solution)/shard_map/cross/pallas_call | solution.py:404
  17.4 1.4 %near.1 = (bf16[2,160,128]{2,1,0:T(8,128)(2,1)S(1)}, bf16[2,160,128]{2,1,0:T(8,128)(2,1)S(1)}) custom-call(bf16[8,2,160,128]{3,2,1,0:T(8,128)(2,1)S(1)} %get-tuple-element.26.q_ref, bf16[512,768]{1,0:T(8,128)(2,1)S(1)} %get-tuple-element.27.own_ref, f32[8,8,8,320]{3,2,1,0:T(8,128)S(1)} %get-tuple-element.28.xg_ref, bf16[384,768]{1,0:T(8,128)(2,1)S(1)} %early.1.kv_ref, ...), custom_call_target="tpu_custom_call" | custom-call | flops 209715200 | bytes 4194304 | tf_op jit(solution)/shard_map/near/pallas_call | solution.py:404
  18.9 0.0 copy-start.1
  18.9 0.1 collective-permute-start.4
  19.0 1.6 %collective-permute-start.5 = (bf16[2,160,128]{2,1,0:T(8,128)(2,1)S(1)}, bf16[2,160,128]{2,1,0:T(8,128)(2,1)S(1)}, u32[]{:S(2)}, u32[]{:S(2)}) collective-permute-start(bf16[2,160,128]{2,1,0:T(8,128)(2,1)S(1)} %get-tuple-element.39), channel_id=1, source_target_pairs={{0,2},{1,3},{2,0},{3,1},{4,6},{5,7},{6,4},{7,5},{8,10},{9,11},{10,... | collective-permute-start | bytes 245768 | tf_op jit(solution)/shard_map/ppermute | solution.py:597
  20.5 0.3 %collective-permute-start.6 = (bf16[2,160,128]{2,1,0:T(8,128)(2,1)S(1)}, bf16[2,160,128]{2,1,0:T(8,128)(2,1)S(1)}, u32[]{:S(2)}, u32[]{:S(2)}) collective-permute-start(bf16[2,160,128]{2,1,0:T(8,128)(2,1)S(1)} %get-tuple-element.40), channel_id=1, source_target_pairs={{0,3},{1,2},{2,1},{3,0},{4,7},{5,6},{6,5},{7,4},{8,11},{9,10},{10,... | collective-permute-start | bytes 245768 | tf_op jit(solution)/shard_map/ppermute | solution.py:597
  20.8 0.0 copy-done.1
  20.8 0.0 collective-permute-done.4.rest_1_
  20.8 0.7 %ready.1 = (bf16[256,1024]{1,0:T(8,128)(2,1)S(1)}, f32[2,320,128]{2,1,0:T(8,128)S(1)}) custom-call(f32[1,320]{1,0:T(1,128)S(1)} %reshape.4.gain_ref, bf16[320,1024]{1,0:T(8,128)(2,1)S(1)} %get-tuple-element.24.sw_ref, bf16[2,160,128]{2,1,0:T(8,128)(2,1)S(1)} %get-tuple-element.35.rest_0_, bf16[2,160,128]{2,1,0:T(8,128)(2,1)S(1)} %collective-permute-done.4.rest_1_), custom_call_target="tpu_custom_call" | custom-call | flops 157286400 | bytes 2097152 | tf_op jit(solution)/shard_map/ready/pallas_call | solution.py:450
  21.6 2.6 %collective-permute-done.5.rest_0_ = bf16[2,160,128]{2,1,0:T(8,128)(2,1)S(1)} collective-permute-done((bf16[2,160,128]{2,1,0:T(8,128)(2,1)S(1)}, bf16[2,160,128]{2,1,0:T(8,128)(2,1)S(1)}, u32[]{:S(2)}, u32[]{:S(2)}) %collective-permute-start.5) | collective-permute-done | bytes 81952 | tf_op jit(solution)/shard_map/ppermute | solution.py:597
  24.1 1.1 %collective-permute-done.6.rest_1_ = bf16[2,160,128]{2,1,0:T(8,128)(2,1)S(1)} collective-permute-done((bf16[2,160,128]{2,1,0:T(8,128)(2,1)S(1)}, bf16[2,160,128]{2,1,0:T(8,128)(2,1)S(1)}, u32[]{:S(2)}, u32[]{:S(2)}) %collective-permute-start.6) | collective-permute-done | bytes 81952 | tf_op jit(solution)/shard_map/ppermute | solution.py:597
  25.3 2.7 %spatial.1 = bf16[2,320,256]{2,1,0:T(8,128)(2,1)} custom-call(f32[1,320]{1,0:T(1,128)S(1)} %reshape.4.gain_ref, bf16[320,1024]{1,0:T(8,128)(2,1)S(1)} %get-tuple-element.24.sw_ref, bf16[320,320]{1,0:T(8,128)(2,1)S(1)} %get-tuple-element.25.so_ref, bf16[256,1024]{1,0:T(8,128)(2,1)S(1)} %get-tuple-element.37.packed_ref, ...), custom_call_target="tpu_custom_call" | custom-call | flops 587202560 | bytes 4194304 | tf_op jit(solution)/shard_map/spatial/pallas_call | solution.py:526
  (2 shorter events, 0.0 us)
Async XLA Ops:
  1.8 8.6 %copy-start = (f32[320]{0:T(512)S(1)}, f32[320]{0:T(512)}, u32[]{:S(2)}) copy-start(f32[320]{0:T(512)} %param.10) | copy-start | bytes 3844
  1.8 12.7 %collective-permute-start = (bf16[5,160,128]{2,1,0:T(8,128)(2,1)S(1)}, bf16[5,160,128]{2,1,0:T(8,128)(2,1)S(1)}, u32[]{:S(2)}, u32[]{:S(2)}) collective-permute-start(bf16[5,160,128]{2,1,0:T(8,128)(2,1)S(1)} %get-tuple-element.30), channel_id=1, source_target_pairs={{0,4},{1,5},{2,6},{3,7},{4,0},{5,1},{6,2},{7,3},{8,12},{9,13},{10,... | collective-permute-start | bytes 614408 | tf_op jit(solution)/shard_map/ppermute | solution.py:582
  4.9 10.4 %collective-permute-start.2 = (bf16[4,160,128]{2,1,0:T(8,128)(2,1)S(1)}, bf16[4,160,128]{2,1,0:T(8,128)(2,1)S(1)}, u32[]{:S(2)}, u32[]{:S(2)}) collective-permute-start(bf16[4,160,128]{2,1,0:T(8,128)(2,1)S(1)} %get-tuple-element.33), channel_id=1, source_target_pairs={{0,1},{1,0},{2,3},{3,2},{4,8},{5,9},{6,10},{7,11},{8,4},{9,5},{10,... | collective-permute-start | bytes 491528 | tf_op jit(solution)/shard_map/ppermute | solution.py:583
  4.9 9.6 %collective-permute-start.1 = (bf16[1,160,128]{2,1,0:T(8,128)(2,1)S(1)}, bf16[1,160,128]{2,1,0:T(8,128)(2,1)S(1)}, u32[]{:S(2)}, u32[]{:S(2)}) collective-permute-start(bf16[1,160,128]{2,1,0:T(8,128)(2,1)S(1)} %get-tuple-element.31.rest_1_), channel_id=1, source_target_pairs={{0,8},{4,12},{8,0},{12,4},{1,9},{5,13},{9,1},{13,5},{2,10},{6,14},... | collective-permute-start | bytes 122888 | tf_op jit(solution)/shard_map/ppermute | solution.py:580
  7.5 7.8 %collective-permute-start.3 = (bf16[1,160,128]{2,1,0:T(8,128)(2,1)S(1)}, bf16[1,160,128]{2,1,0:T(8,128)(2,1)S(1)}, u32[]{:S(2)}, u32[]{:S(2)}) collective-permute-start(bf16[1,160,128]{2,1,0:T(8,128)(2,1)S(1)} %get-tuple-element.31.rest_1_), channel_id=1, source_target_pairs={{0,12},{4,8},{8,4},{12,0},{1,13},{5,9},{9,5},{13,1},{2,14},{6,10},... | collective-permute-start | bytes 122888 | tf_op jit(solution)/shard_map/ppermute | solution.py:580
  18.9 1.9 %copy-start.1 = (f32[320]{0:T(512)S(1)}, f32[320]{0:T(512)}, u32[]{:S(2)}) copy-start(f32[320]{0:T(512)} %param.13) | copy-start | bytes 3844
  18.9 1.9 %collective-permute-start.4 = (bf16[2,160,128]{2,1,0:T(8,128)(2,1)S(1)}, bf16[2,160,128]{2,1,0:T(8,128)(2,1)S(1)}, u32[]{:S(2)}, u32[]{:S(2)}) collective-permute-start(bf16[2,160,128]{2,1,0:T(8,128)(2,1)S(1)} %get-tuple-element.36), channel_id=1, source_target_pairs={{0,1},{1,0},{2,3},{3,2},{4,5},{5,4},{6,7},{7,6},{8,9},{9,8},{10,11... | collective-permute-start | bytes 245768 | tf_op jit(solution)/shard_map/ppermute | solution.py:597
  19.0 5.1 %collective-permute-start.5 = (bf16[2,160,128]{2,1,0:T(8,128)(2,1)S(1)}, bf16[2,160,128]{2,1,0:T(8,128)(2,1)S(1)}, u32[]{:S(2)}, u32[]{:S(2)}) collective-permute-start(bf16[2,160,128]{2,1,0:T(8,128)(2,1)S(1)} %get-tuple-element.39), channel_id=1, source_target_pairs={{0,2},{1,3},{2,0},{3,1},{4,6},{5,7},{6,4},{7,5},{8,10},{9,11},{10,... | collective-permute-start | bytes 245768 | tf_op jit(solution)/shard_map/ppermute | solution.py:597
  20.5 4.7 %collective-permute-start.6 = (bf16[2,160,128]{2,1,0:T(8,128)(2,1)S(1)}, bf16[2,160,128]{2,1,0:T(8,128)(2,1)S(1)}, u32[]{:S(2)}, u32[]{:S(2)}) collective-permute-start(bf16[2,160,128]{2,1,0:T(8,128)(2,1)S(1)} %get-tuple-element.40), channel_id=1, source_target_pairs={{0,3},{1,2},{2,1},{3,0},{4,7},{5,6},{6,5},{7,4},{8,11},{9,10},{10,... | collective-permute-start | bytes 245768 | tf_op jit(solution)/shard_map/ppermute | solution.py:597

commit v6 on v5

--- a/solution.py
+++ b/solution.py
@@ -13,6 +13,7 @@
 SUB = 8
 LANES = 128
 NEG = -1e30
+SHARPNESS = 1.0 / (math.sqrt(HEAD_DIM) * math.log(2.0))
 DIRECT_CLIPS = 4
 LIMIT = 24 << 20
 LEAD = 8
@@ -107,7 +108,7 @@
 
 def soften(scores):
     highest = jnp.max(scores, axis=-1, keepdims=True)
-    expo = jnp.exp((scores - highest) * (1.0 / math.sqrt(HEAD_DIM)))
+    expo = jnp.exp2((scores - highest) * SHARPNESS)
     return expo.astype(jnp.bfloat16), 1.0 / jnp.sum(expo, axis=-1, keepdims=True)
 
 
@@ -132,40 +133,51 @@
     return me, odd, inner_there, outer_there
 
 
-def prep_kernel(clips, x_hbm, s_ref, x_ref, a_ref, b_ref, p_ref, x_sem):
-    copy_x = pltpu.make_async_copy(x_hbm, x_ref, x_sem)
-    copy_x.start()
+def pick_kernel(x_hbm, s_ref, p_ref, frame_ref, sem):
+    copy = pltpu.make_async_copy(x_hbm.at[s_ref[0]], frame_ref, sem)
+    copy.start()
+    copy.wait()
+    p_ref[0] = pack(frame_ref[...])
+
+
+def pick_frame(latents, sampled):
+    _, pixels, channels = latents.shape
+    kind = latents.dtype
+    return pl.pallas_call(
+        pick_kernel,
+        out_shape=pltpu.VMEM((1, pixels * channels // LANES, LANES), kind),
+        in_specs=[FAR, pl.BlockSpec(memory_space=pltpu.SMEM)],
+        out_specs=VMEM,
+        scratch_shapes=[pltpu.VMEM((pixels, channels), kind), pltpu.SemaphoreType.DMA],
+        compiler_params=pltpu.CompilerParams(vmem_limit_bytes=LIMIT),
+        name="pick",
+    )(far(latents), sampled)
+
+
+def prep_kernel(clips, x_ref, p_ref, a_ref, b_ref):
     _, odd, _, _ = neighbours(clips)
-    copy_x.wait()
     span = x_ref.shape[0] - HALO
     for i in range(HALO):
         a_ref[i] = pack(x_ref[(1 - odd) * span + i])
         b_ref[i] = pack(x_ref[odd * span + i])
-    picked = pack(x_ref[s_ref[0]])
-    p_ref[0] = picked
     if a_ref.shape[0] > HALO:
-        a_ref[HALO] = picked
-
-
-def prep(latents, sampled, clips, with_pick):
-    _, pixels, channels = latents.shape
-    dense = (pixels * channels // LANES, LANES)
-    sent = HALO + (1 if with_pick else 0)
+        a_ref[HALO] = p_ref[0]
+
+
+def prep(latents, picked, clips, with_pick):
+    dense = picked.shape[1:]
     kind = latents.dtype
     return pl.pallas_call(
         functools.partial(prep_kernel, clips),
         out_shape=[
-            pltpu.VMEM(latents.shape, kind),
-            pltpu.VMEM((sent,) + dense, kind),
+            pltpu.VMEM((HALO + (1 if with_pick else 0),) + dense, kind),
             pltpu.VMEM((HALO,) + dense, kind),
-            pltpu.VMEM((1,) + dense, kind),
         ],
-        in_specs=[FAR, pl.BlockSpec(memory_space=pltpu.SMEM)],
-        out_specs=[VMEM] * 4,
-        scratch_shapes=[pltpu.SemaphoreType.DMA],
+        in_specs=[VMEM, VMEM],
+        out_specs=[VMEM] * 2,
         compiler_params=pltpu.CompilerParams(vmem_limit_bytes=LIMIT),
         name="prep",
-    )(far(latents), sampled)
+    )(latents, picked)
 
 
 def local_kernel(
@@ -239,7 +251,7 @@
         + [pltpu.VMEM((groups, frames, SUB, channels), jnp.float32)]
         + [pltpu.VMEM(wide, kind)] * 2
         + [pltpu.VMEM(square, kind)] * 2,
-        in_specs=[VMEM, pl.BlockSpec()] + [FAR] * 4,
+        in_specs=[VMEM, VMEM] + [FAR] * 4,
         out_specs=[VMEM] * 7,
         scratch_shapes=[
             pltpu.VMEM(temporal_qkv.shape, kind),
@@ -291,7 +303,7 @@
     return pl.pallas_call(
         early_kernel,
         out_shape=pltpu.VMEM((pixels * slots, weights.shape[1] - channels // LANES * LANES), kind),
-        in_specs=[pl.BlockSpec()] + [VMEM] * (2 + len(picks)),
+        in_specs=[VMEM] + [VMEM] * (2 + len(picks)),
         out_specs=VMEM,
         scratch_shapes=[pltpu.VMEM((groups, slots, SUB, channels), jnp.float32)],
         cost_estimate=pl.CostEstimate(
@@ -404,7 +416,7 @@
     return pl.pallas_call(
         functools.partial(temporal_kernel, clips, early_held, late_held, pix_count, cross),
         out_shape=out_shape,
-        in_specs=[VMEM] * 4 + [pl.BlockSpec()] + [VMEM] * (2 + len(last)),
+        in_specs=[VMEM] * 4 + [VMEM] + [VMEM] * (2 + len(last)),
         out_specs=[VMEM] * len(out_shape),
         scratch_shapes=scratch,
         cost_estimate=pl.CostEstimate(
@@ -453,7 +465,7 @@
             pltpu.VMEM((per_device * half, weights.shape[1]), kind),
             pltpu.VMEM((per_device, channels, half), jnp.float32),
         ],
-        in_specs=[pl.BlockSpec()] + [VMEM] * (1 + halves),
+        in_specs=[VMEM] + [VMEM] * (1 + halves),
         out_specs=[VMEM] * 2,
         scratch_shapes=[pltpu.VMEM((per_device, half, channels), jnp.float32)],
         cost_estimate=pl.CostEstimate(
@@ -526,7 +538,7 @@
     return pl.pallas_call(
         functools.partial(spatial_kernel, halves),
         out_shape=jax.ShapeDtypeStruct((per_device, channels, pixels), kind),
-        in_specs=[pl.BlockSpec()] + [VMEM] * (4 + halves),
+        in_specs=[VMEM] + [VMEM] * (4 + halves),
         out_specs=pl.BlockSpec(),
         scratch_shapes=[
             pltpu.VMEM((per_device, pixels // 2, channels), jnp.float32),
@@ -571,7 +583,9 @@
     clips, pix_count = lax.axis_size("clip"), lax.axis_size("pix")
     pixels = latents.shape[1] * pix_count
     gathered = clips > DIRECT_CLIPS or clips & (clips - 1) != 0
-    x, a, b, p = prep(latents, sampled, clips, not gathered)
+    x = pltpu.with_memory_space_constraint(latents, pltpu.VMEM)
+    p = pick_frame(latents, sampled)
+    a, b = prep(x, p, clips, not gathered)
     if gathered:
         soon, last = [], [lax.all_gather(p, "clip", axis=0, tiled=True)]
     else:

time: 28.1 us -> 28 us (level)
    pallas_call x1, Pallas kernels: 1.11 us -> 0.1 us  [prep(): pl.pallas_call(functools.partial(prep_kernel, clips), out_shape=[pltpu.VM...]
    pallas_call x0 -> x1, Pallas kernels: none -> 0.88 us  [pick_frame(): pl.pallas_call(pick_kernel, out_shape=pltpu.VMEM((1, pixels * channels //...]
where the time goes in v6:
time: 28 us; the launch traced here: 27.9 us
  Pallas kernels  11 us (39%)
  starting transfers between devices  10.5 us (38%)
  waiting for transfers between devices  5.5 us (20%)
  between operations  0.8 us (3%)
    ppermute x2, starting transfers between devices, body(): pick = lax.ppermute(p, 'clip', [(i, i ^ step) for i in range(clips)])  5.51 us
    ppermute x3, waiting for transfers between devices, swap(): return lax.ppermute(chunk, 'pix', [(i, i ^ step) for i in range(pix_count)])  3.71 us
    pallas_call x2, Pallas kernels, temporal(): pl.pallas_call(functools.partial(temporal_kernel, clips, early_held, late...  3.56 us
    ppermute x1, starting transfers between devices, body(): a = lax.ppermute(a, ('clip', 'pix'), border_pairs(clips, pix_count, 0))  3.12 us
    pallas_call x1, Pallas kernels, spatial(): pl.pallas_call(functools.partial(spatial_kernel, halves), out_shape=jax.S...  2.64 us
    pallas_call x1, Pallas kernels, local(): pl.pallas_call(local_kernel, out_shape=[pltpu.VMEM((groups, 2, channels /...  2.27 us
    ppermute x3, starting transfers between devices, swap(): return lax.ppermute(chunk, 'pix', [(i, i ^ step) for i in range(pix_count)])  1.92 us
    ppermute x2, waiting for transfers between devices, body(): pick = lax.ppermute(p, 'clip', [(i, i ^ step) for i in range(clips)])  1.78 us
  transfers between devices with their start and end apart: 7, of which 3 were waited for; matrix products, arithmetic and copies ran while one was open for 0% of the time, Pallas kernels for 14%

profile of v6, /device:TPU:0, one launch (start us, length us, event | category | flops | bytes accessed | tf_op | source)
XLA Modules:
  0.0 27.9 jit_solution(8860840805028911428)
XLA Ops:
  0.0 0.0 copy-start
  0.7 0.9 %pick.1.p_ref.rest_1_ = bf16[1,160,128]{2,1,0:T(8,128)(2,1)S(1)} custom-call(bf16[8,64,320]{2,1,0:T(8,128)(2,1)} %x_ref.3, s32[1]{0:T(128)S(6)} %copy.9.s_ref), custom_call_target="tpu_custom_call" | custom-call | tf_op jit(solution)/shard_map/pick/pallas_call | solution.py:146
  1.6 0.0 copy-done
  1.6 0.1 prep.1
  1.7 0.0 copy-start.1
  1.7 3.1 %collective-permute-start = (bf16[5,160,128]{2,1,0:T(8,128)(2,1)S(1)}, bf16[5,160,128]{2,1,0:T(8,128)(2,1)S(1)}, u32[]{:S(2)}, u32[]{:S(2)}) collective-permute-start(bf16[5,160,128]{2,1,0:T(8,128)(2,1)S(1)} %get-tuple-element.27), channel_id=1, source_target_pairs={{0,4},{1,5},{2,6},{3,7},{4,0},{5,1},{6,2},{7,3},{8,12},{9,13},{10,... | collective-permute-start | bytes 614408 | tf_op jit(solution)/shard_map/ppermute | solution.py:596
  4.8 0.0 collective-permute-start.2
  4.8 2.6 %collective-permute-start.1 = (bf16[1,160,128]{2,1,0:T(8,128)(2,1)S(1)}, bf16[1,160,128]{2,1,0:T(8,128)(2,1)S(1)}, u32[]{:S(2)}, u32[]{:S(2)}) collective-permute-start(bf16[1,160,128]{2,1,0:T(8,128)(2,1)S(1)} %pick.1.p_ref.rest_1_), channel_id=1, source_target_pairs={{0,8},{4,12},{8,0},{12,4},{1,9},{5,13},{9,1},{13,5},{2,10},{6,14},... | collective-permute-start | bytes 122888 | tf_op jit(solution)/shard_map/ppermute | solution.py:594
  7.4 2.9 %collective-permute-start.3 = (bf16[1,160,128]{2,1,0:T(8,128)(2,1)S(1)}, bf16[1,160,128]{2,1,0:T(8,128)(2,1)S(1)}, u32[]{:S(2)}, u32[]{:S(2)}) collective-permute-start(bf16[1,160,128]{2,1,0:T(8,128)(2,1)S(1)} %pick.1.p_ref.rest_1_), channel_id=1, source_target_pairs={{0,12},{4,8},{8,4},{12,0},{1,13},{5,9},{9,5},{13,1},{2,14},{6,10},... | collective-permute-start | bytes 122888 | tf_op jit(solution)/shard_map/ppermute | solution.py:594
  10.4 0.0 copy-done.1
  10.4 2.3 %local.1 = (bf16[8,2,160,128]{3,2,1,0:T(8,128)(2,1)S(1)}, bf16[512,768]{1,0:T(8,128)(2,1)S(1)}, f32[8,8,8,320]{3,2,1,0:T(8,128)S(1)}, bf16[320,1024]{1,0:T(8,128...) custom-call(bf16[8,64,320]{2,1,0:T(8,128)(2,1)S(1)} %copy-done, ...), custom_call_target="tpu_custom_call" | custom-call | flops 314572800 | bytes 4194304 | tf_op jit(solution)/shard_map/local/pallas_call | solution.py:247
  12.6 1.8 %collective-permute-done.1.rest_0_ = bf16[1,160,128]{2,1,0:T(8,128)(2,1)S(1)} collective-permute-done((bf16[1,160,128]{2,1,0:T(8,128)(2,1)S(1)}, bf16[1,160,128]{2,1,0:T(8,128)(2,1)S(1)}, u32[]{:S(2)}, u32[]{:S(2)}) %collective-permute-start.1) | collective-permute-done | bytes 40992 | tf_op jit(solution)/shard_map/ppermute | solution.py:594
  14.4 0.0 collective-permute-done.a_ref
  14.4 0.8 %early.1.kv_ref = bf16[384,768]{1,0:T(8,128)(2,1)S(1)} custom-call(f32[1,320]{1,0:T(1,128)S(1)} %reshape.5.gain_ref, bf16[320,1024]{1,0:T(8,128)(2,1)S(1)} %get-tuple-element.26.tw_ref, bf16[5,160,128]{2,1,0:T(8,128)(2,1)S(1)} %collective-permute-done.a_ref, bf16[1,160,128]{2,1,0:T(8,128)(2,1)S(1)} %collective-permute-done.1.rest_0_), custom_call_target="tpu_custom_call" | custom-call | flops 157286400 | bytes 2097152 | tf_op jit(solution)/shard_map/early/pallas_call | solution.py:303
  15.2 0.0 collective-permute-done.3.rest_2_
  15.3 0.0 collective-permute-done.2.rest_0_
  15.3 2.1 %cross.1 = (bf16[2,160,128]{2,1,0:T(8,128)(2,1)S(1)}, bf16[2,160,128]{2,1,0:T(8,128)(2,1)S(1)}, bf16[384,768]{1,0:T(8,128)(2,1)S(1)}) custom-call(bf16[8,2,160,128]{3,2,1,0:T(8,128)(2,1)S(1)} %get-tuple-element.23.q_ref, bf16[512,768]{1,0:T(8,128)(2,1)S(1)} %get-tuple-element.24.own_ref, f32[8,8,8,320]{3,2,1,0:T(8,128)S(1)} %get-tuple-element.25.xg_ref, ...), custom_call_target="tpu_custom_call" | custom-call | flops 209715200 | bytes 4194304 | tf_op jit(solution)/shard_map/cross/pallas_call | solution.py:416
  17.4 1.4 %near.1 = (bf16[2,160,128]{2,1,0:T(8,128)(2,1)S(1)}, bf16[2,160,128]{2,1,0:T(8,128)(2,1)S(1)}) custom-call(bf16[8,2,160,128]{3,2,1,0:T(8,128)(2,1)S(1)} %get-tuple-element.23.q_ref, bf16[512,768]{1,0:T(8,128)(2,1)S(1)} %get-tuple-element.24.own_ref, f32[8,8,8,320]{3,2,1,0:T(8,128)S(1)} %get-tuple-element.25.xg_ref, bf16[384,768]{1,0:T(8,128)(2,1)S(1)} %early.1.kv_ref, ...), custom_call_target="tpu_custom_call" | custom-call | flops 209715200 | bytes 4194304 | tf_op jit(solution)/shard_map/near/pallas_call | solution.py:416
  18.8 0.0 copy-start.2
  18.8 0.1 collective-permute-start.4
  18.9 1.6 %collective-permute-start.5 = (bf16[2,160,128]{2,1,0:T(8,128)(2,1)S(1)}, bf16[2,160,128]{2,1,0:T(8,128)(2,1)S(1)}, u32[]{:S(2)}, u32[]{:S(2)}) collective-permute-start(bf16[2,160,128]{2,1,0:T(8,128)(2,1)S(1)} %get-tuple-element.35), channel_id=1, source_target_pairs={{0,2},{1,3},{2,0},{3,1},{4,6},{5,7},{6,4},{7,5},{8,10},{9,11},{10,... | collective-permute-start | bytes 245768 | tf_op jit(solution)/shard_map/ppermute | solution.py:611
  20.5 0.3 %collective-permute-start.6 = (bf16[2,160,128]{2,1,0:T(8,128)(2,1)S(1)}, bf16[2,160,128]{2,1,0:T(8,128)(2,1)S(1)}, u32[]{:S(2)}, u32[]{:S(2)}) collective-permute-start(bf16[2,160,128]{2,1,0:T(8,128)(2,1)S(1)} %get-tuple-element.36), channel_id=1, source_target_pairs={{0,3},{1,2},{2,1},{3,0},{4,7},{5,6},{6,5},{7,4},{8,11},{9,10},{10,... | collective-permute-start | bytes 245768 | tf_op jit(solution)/shard_map/ppermute | solution.py:611
  20.8 0.0 copy-done.2
  20.8 0.0 collective-permute-done.4.rest_1_
  20.8 0.7 %ready.1 = (bf16[256,1024]{1,0:T(8,128)(2,1)S(1)}, f32[2,320,128]{2,1,0:T(8,128)S(1)}) custom-call(f32[1,320]{1,0:T(1,128)S(1)} %reshape.4.gain_ref, bf16[320,1024]{1,0:T(8,128)(2,1)S(1)} %get-tuple-element.21.sw_ref, bf16[2,160,128]{2,1,0:T(8,128)(2,1)S(1)} %get-tuple-element.31.rest_0_, bf16[2,160,128]{2,1,0:T(8,128)(2,1)S(1)} %collective-permute-done.4.rest_1_), custom_call_target="tpu_custom_call" | custom-call | flops 157286400 | bytes 2097152 | tf_op jit(solution)/shard_map/ready/pallas_call | solution.py:462
  21.5 2.5 %collective-permute-done.5.rest_0_ = bf16[2,160,128]{2,1,0:T(8,128)(2,1)S(1)} collective-permute-done((bf16[2,160,128]{2,1,0:T(8,128)(2,1)S(1)}, bf16[2,160,128]{2,1,0:T(8,128)(2,1)S(1)}, u32[]{:S(2)}, u32[]{:S(2)}) %collective-permute-start.5) | collective-permute-done | bytes 81952 | tf_op jit(solution)/shard_map/ppermute | solution.py:611
  24.1 1.2 %collective-permute-done.6.rest_1_ = bf16[2,160,128]{2,1,0:T(8,128)(2,1)S(1)} collective-permute-done((bf16[2,160,128]{2,1,0:T(8,128)(2,1)S(1)}, bf16[2,160,128]{2,1,0:T(8,128)(2,1)S(1)}, u32[]{:S(2)}, u32[]{:S(2)}) %collective-permute-start.6) | collective-permute-done | bytes 81952 | tf_op jit(solution)/shard_map/ppermute | solution.py:611
  25.2 2.6 %spatial.1 = bf16[2,320,256]{2,1,0:T(8,128)(2,1)} custom-call(f32[1,320]{1,0:T(1,128)S(1)} %reshape.4.gain_ref, bf16[320,1024]{1,0:T(8,128)(2,1)S(1)} %get-tuple-element.21.sw_ref, bf16[320,320]{1,0:T(8,128)(2,1)S(1)} %get-tuple-element.22.so_ref, bf16[256,1024]{1,0:T(8,128)(2,1)S(1)} %get-tuple-element.33.packed_ref, ...), custom_call_target="tpu_custom_call" | custom-call | flops 587202560 | bytes 4194304 | tf_op jit(solution)/shard_map/spatial/pallas_call | solution.py:538
  (2 shorter events, 0.0 us)
Async XLA Ops:
  0.0 1.6 %copy-start = (bf16[8,64,320]{2,1,0:T(8,128)(2,1)S(1)}, bf16[8,64,320]{2,1,0:T(8,128)(2,1)}, u32[]{:S(2)}) copy-start(bf16[8,64,320]{2,1,0:T(8,128)(2,1)} %x_ref.3) | copy-start | bytes 983044
  1.7 8.6 %copy-start.1 = (f32[320]{0:T(512)S(1)}, f32[320]{0:T(512)}, u32[]{:S(2)}) copy-start(f32[320]{0:T(512)} %param.10) | copy-start | bytes 3844
  1.7 12.7 %collective-permute-start = (bf16[5,160,128]{2,1,0:T(8,128)(2,1)S(1)}, bf16[5,160,128]{2,1,0:T(8,128)(2,1)S(1)}, u32[]{:S(2)}, u32[]{:S(2)}) collective-permute-start(bf16[5,160,128]{2,1,0:T(8,128)(2,1)S(1)} %get-tuple-element.27), channel_id=1, source_target_pairs={{0,4},{1,5},{2,6},{3,7},{4,0},{5,1},{6,2},{7,3},{8,12},{9,13},{10,... | collective-permute-start | bytes 614408 | tf_op jit(solution)/shard_map/ppermute | solution.py:596
  4.8 10.4 %collective-permute-start.2 = (bf16[4,160,128]{2,1,0:T(8,128)(2,1)S(1)}, bf16[4,160,128]{2,1,0:T(8,128)(2,1)S(1)}, u32[]{:S(2)}, u32[]{:S(2)}) collective-permute-start(bf16[4,160,128]{2,1,0:T(8,128)(2,1)S(1)} %get-tuple-element.29), channel_id=1, source_target_pairs={{0,1},{1,0},{2,3},{3,2},{4,8},{5,9},{6,10},{7,11},{8,4},{9,5},{10,... | collective-permute-start | bytes 491528 | tf_op jit(solution)/shard_map/ppermute | solution.py:597
  4.8 9.6 %collective-permute-start.1 = (bf16[1,160,128]{2,1,0:T(8,128)(2,1)S(1)}, bf16[1,160,128]{2,1,0:T(8,128)(2,1)S(1)}, u32[]{:S(2)}, u32[]{:S(2)}) collective-permute-start(bf16[1,160,128]{2,1,0:T(8,128)(2,1)S(1)} %pick.1.p_ref.rest_1_), channel_id=1, source_target_pairs={{0,8},{4,12},{8,0},{12,4},{1,9},{5,13},{9,1},{13,5},{2,10},{6,14},... | collective-permute-start | bytes 122888 | tf_op jit(solution)/shard_map/ppermute | solution.py:594
  7.4 7.8 %collective-permute-start.3 = (bf16[1,160,128]{2,1,0:T(8,128)(2,1)S(1)}, bf16[1,160,128]{2,1,0:T(8,128)(2,1)S(1)}, u32[]{:S(2)}, u32[]{:S(2)}) collective-permute-start(bf16[1,160,128]{2,1,0:T(8,128)(2,1)S(1)} %pick.1.p_ref.rest_1_), channel_id=1, source_target_pairs={{0,12},{4,8},{8,4},{12,0},{1,13},{5,9},{9,5},{13,1},{2,14},{6,10},... | collective-permute-start | bytes 122888 | tf_op jit(solution)/shard_map/ppermute | solution.py:594
  18.8 1.9 %copy-start.2 = (f32[320]{0:T(512)S(1)}, f32[320]{0:T(512)}, u32[]{:S(2)}) copy-start(f32[320]{0:T(512)} %param.13) | copy-start | bytes 3844
  18.8 1.9 %collective-permute-start.4 = (bf16[2,160,128]{2,1,0:T(8,128)(2,1)S(1)}, bf16[2,160,128]{2,1,0:T(8,128)(2,1)S(1)}, u32[]{:S(2)}, u32[]{:S(2)}) collective-permute-start(bf16[2,160,128]{2,1,0:T(8,128)(2,1)S(1)} %get-tuple-element.32), channel_id=1, source_target_pairs={{0,1},{1,0},{2,3},{3,2},{4,5},{5,4},{6,7},{7,6},{8,9},{9,8},{10,11... | collective-permute-start | bytes 245768 | tf_op jit(solution)/shard_map/ppermute | solution.py:611
  18.9 5.1 %collective-permute-start.5 = (bf16[2,160,128]{2,1,0:T(8,128)(2,1)S(1)}, bf16[2,160,128]{2,1,0:T(8,128)(2,1)S(1)}, u32[]{:S(2)}, u32[]{:S(2)}) collective-permute-start(bf16[2,160,128]{2,1,0:T(8,128)(2,1)S(1)} %get-tuple-element.35), channel_id=1, source_target_pairs={{0,2},{1,3},{2,0},{3,1},{4,6},{5,7},{6,4},{7,5},{8,10},{9,11},{10,... | collective-permute-start | bytes 245768 | tf_op jit(solution)/shard_map/ppermute | solution.py:611
  20.5 4.7 %collective-permute-start.6 = (bf16[2,160,128]{2,1,0:T(8,128)(2,1)S(1)}, bf16[2,160,128]{2,1,0:T(8,128)(2,1)S(1)}, u32[]{:S(2)}, u32[]{:S(2)}) collective-permute-start(bf16[2,160,128]{2,1,0:T(8,128)(2,1)S(1)} %get-tuple-element.36), channel_id=1, source_target_pairs={{0,3},{1,2},{2,1},{3,0},{4,7},{5,6},{6,5},{7,4},{8,11},{9,10},{10,... | collective-permute-start | bytes 245768 | tf_op jit(solution)/shard_map/ppermute | solution.py:611

commit v7 on v5

--- a/solution.py
+++ b/solution.py
@@ -275,23 +275,21 @@
     return jnp.dot(rows, tw_ref[:, whole:], preferred_element_type=jnp.float32).astype(jnp.bfloat16)
 
 
-def early_kernel(gain_ref, tw_ref, a_ref, *rest):
-    *pick_refs, kv_ref, normed_ref = rest
-    dense = [a_ref[i] for i in range(a_ref.shape[0])]
-    for ref in pick_refs:
-        dense += [ref[i] for i in range(ref.shape[0])]
+def early_kernel(gain_ref, tw_ref, *rest):
+    *refs, kv_ref, normed_ref = rest
+    dense = [ref[i] for ref in refs for i in range(min(HALO, ref.shape[0]))]
     pixels = normed_ref.shape[0] * SUB
     kv_ref[...] = remote_pairs(dense, gain_ref[...], tw_ref, normed_ref, pixels)
 
 
-def early(gain, weights, a, picks, pixels, slots):
+def early(gain, weights, frames, pixels, slots):
     channels = weights.shape[0]
     groups = pixels // SUB
     kind = weights.dtype
     return pl.pallas_call(
         early_kernel,
         out_shape=pltpu.VMEM((pixels * slots, weights.shape[1] - channels // LANES * LANES), kind),
-        in_specs=[pl.BlockSpec()] + [VMEM] * (2 + len(picks)),
+        in_specs=[pl.BlockSpec()] + [VMEM] * (1 + len(frames)),
         out_specs=VMEM,
         scratch_shapes=[pltpu.VMEM((groups, slots, SUB, channels), jnp.float32)],
         cost_estimate=pl.CostEstimate(
@@ -299,15 +297,16 @@
         ),
         compiler_params=pltpu.CompilerParams(vmem_limit_bytes=LIMIT),
         name="early",
-    )(gain.reshape(1, channels), weights, a, *picks)
+    )(gain.reshape(1, channels), weights, *frames)
 
 
 def temporal_kernel(
-    clips, early_held, late_held, pix_count, cross,
+    clips, ahead, early_held, late_held, pix_count, cross,
     q_ref, own_ref, xg_ref, kv_ref, gain_ref, tw_ref, to_ref, *rest,
 ):
     halves = pix_count // 2
     scratch = 4 if cross else 2
+    before_refs, rest = rest[:ahead], rest[ahead:]
     last_refs, sends, rest = (
         rest[: len(rest) - halves - scratch],
         rest[len(rest) - halves - scratch : len(rest) - scratch],
@@ -318,7 +317,7 @@
     _, _, first_there, second_there = neighbours(clips)
     if cross:
         late_ref, normed_ref, att_ref, rows_ref = rest
-        dense = [ref[i] for ref in last_refs for i in range(ref.shape[0])]
+        dense = [ref[i] for ref in last_refs for i in range(HALO if ref.shape[0] == HALO + 1 else 0, ref.shape[0])]
         late_ref[...] = remote_pairs(dense, gain_ref[...], tw_ref, normed_ref, pixels)
     else:
         (late_ref,) = last_refs
@@ -331,11 +330,12 @@
     part = frames // 2
     mine, own = part * SUB, frames * SUB
     soon, more = kv_ref.shape[0] // groups, late_ref.shape[0] // groups
-    shape = (mine, own + soon + more)
+    sooner = sum(ref.shape[0] for ref in before_refs) // groups
+    shape = (mine, own + sooner + soon + more)
     row = lax.broadcasted_iota(jnp.int32, shape, 0)
     column = lax.broadcasted_iota(jnp.int32, shape, 1)
     usable = lax.rem(row, SUB) == lax.rem(column, SUB)
-    slot = column // SUB - frames
+    slot = (column - sooner) // SUB - frames
     usable &= (slot < 0) | (slot >= HALO) | first_there
     usable &= (slot < early_held) | (slot >= soon // SUB)
     usable &= (slot < soon // SUB) | (slot >= soon // SUB + HALO) | second_there
@@ -349,6 +349,7 @@
         return jnp.concatenate(
             [
                 own_ref[g * own : (g + 1) * own, span],
+                *(ref[g * sooner : (g + 1) * sooner, span] for ref in before_refs),
                 kv_ref[g * soon : (g + 1) * soon, span],
                 late_ref[g * more : (g + 1) * more, span],
             ],
@@ -384,7 +385,7 @@
 
 
 def temporal(
-    parts, pairs, gain, weights, out_matrix, last, clips, early_held, late_held, pix_count, cross
+    parts, pairs, gain, weights, out_matrix, before, last, clips, early_held, late_held, pix_count, cross
 ):
     q, own, xg = parts
     groups, frames, _, channels = xg.shape
@@ -402,9 +403,9 @@
         out_shape = out_shape + [pltpu.VMEM((pixels * slots, pairs.shape[1]), kind)]
         scratch = [pltpu.VMEM((groups, slots, SUB, channels), jnp.float32)] + scratch
     return pl.pallas_call(
-        functools.partial(temporal_kernel, clips, early_held, late_held, pix_count, cross),
+        functools.partial(temporal_kernel, clips, len(before), early_held, late_held, pix_count, cross),
         out_shape=out_shape,
-        in_specs=[VMEM] * 4 + [pl.BlockSpec()] + [VMEM] * (2 + len(last)),
+        in_specs=[VMEM] * 4 + [pl.BlockSpec()] + [VMEM] * (2 + len(before) + len(last)),
         out_specs=[VMEM] * len(out_shape),
         scratch_shapes=scratch,
         cost_estimate=pl.CostEstimate(
@@ -412,7 +413,7 @@
         ),
         compiler_params=pltpu.CompilerParams(vmem_limit_bytes=LIMIT),
         name="cross" if cross else "near",
-    )(q, own, xg, pairs, gain.reshape(1, channels), weights, out_matrix, *last)
+    )(q, own, xg, pairs, gain.reshape(1, channels), weights, out_matrix, *before, *last)
 
 
 def gather_rows(chunks, rows_ref, channels):
@@ -584,12 +585,15 @@
     q, own, xg, tw, sw, to, so = local(
         x, temporal_gain, temporal_qkv, temporal_out, spatial_qkv, spatial_out
     )
+    each, before = latents.shape[1], []
+    if not gathered:
+        before = [early(temporal_gain, tw, soon + last[:1], each, up(len(soon) + 1, 2))]
+        last = last[1:] + [a]
     last = [b] + last
-    early_held = sum(part.shape[0] for part in [a] + soon)
-    late_held = sum(part.shape[0] for part in last)
-    pairs = early(temporal_gain, tw, a, soon, latents.shape[1], up(early_held, 2))
-    rest = ((q, own, xg), pairs, temporal_gain, tw, to)
-    held = (clips, early_held, late_held, pix_count)
+    late_held = sum(1 if part is a else part.shape[0] for part in last)
+    pairs = early(temporal_gain, tw, [a], each, up(HALO, 2))
+    rest = ((q, own, xg), pairs, temporal_gain, tw, to, before)
+    held = (clips, HALO, late_held, pix_count)
     halves = pix_count // 2
     *sends, late = temporal(*rest, last, *held, True)
 

time: 28.1 us -> 28.4 us (1.011)
  Pallas kernels: 11.1 us -> 11.4 us
    pallas_call x1 -> x2, Pallas kernels: 0.82 us -> 1.1 us  [early(): pl.pallas_call(early_kernel, out_shape=pltpu.VMEM((pixels * slots, weight...]
  transfers between devices with their start and end apart: 7 -> 7, of which waited for: 3 -> 3; matrix products, arithmetic and copies ran while one was open for 0% -> 0% of each run, Pallas kernels for 14% -> 15%
where the time goes in v7:
time: 28.4 us; the launch traced here: 28.2 us
  Pallas kernels  11.4 us (40%)
  starting transfers between devices  10.5 us (37%)
  waiting for transfers between devices  5.5 us (19%)
  between operations  0.75 us (3%)
    ppermute x2, starting transfers between devices, body(): pick = lax.ppermute(p, 'clip', [(i, i ^ step) for i in range(clips)])  5.51 us
    ppermute x3, waiting for transfers between devices, swap(): return lax.ppermute(chunk, 'pix', [(i, i ^ step) for i in range(pix_count)])  3.71 us
    pallas_call x2, Pallas kernels, temporal(): pl.pallas_call(functools.partial(temporal_kernel, clips, len(before), ear...  3.54 us
    ppermute x1, starting transfers between devices, body(): a = lax.ppermute(a, ('clip', 'pix'), border_pairs(clips, pix_count, 0))  3.12 us
    pallas_call x1, Pallas kernels, spatial(): pl.pallas_call(functools.partial(spatial_kernel, halves), out_shape=jax.S...  2.65 us
    pallas_call x1, Pallas kernels, local(): pl.pallas_call(local_kernel, out_shape=[pltpu.VMEM((groups, 2, channels /...  2.27 us
    ppermute x3, starting transfers between devices, swap(): return lax.ppermute(chunk, 'pix', [(i, i ^ step) for i in range(pix_count)])  1.92 us
    ppermute x2, waiting for transfers between devices, body(): pick = lax.ppermute(p, 'clip', [(i, i ^ step) for i in range(clips)])  1.78 us
  transfers between devices with their start and end apart: 7, of which 3 were waited for; matrix products, arithmetic and copies ran while one was open for 0% of the time, Pallas kernels for 15%

profile of v7, /device:TPU:0, one launch (start us, length us, event | category | flops | bytes accessed | tf_op | source)
XLA Modules:
  0.0 28.2 jit_solution(8722524792094259670)
XLA Ops:
  0.7 1.1 %prep.1 = (bf16[8,64,320]{2,1,0:T(8,128)(2,1)S(1)}, bf16[5,160,128]{2,1,0:T(8,128)(2,1)S(1)}, bf16[4,160,128]{2,1,0:T(8,128)(2,1)S(1)}, bf16[1,160,128]{2,1,0:T(8,128)(2,1)S(1)}) custom-call(bf16[8,64,320]{2,1,0:T(8,128)(2,1)} %x_hbm.1, s32[1]{0:T(128)S(6)} %copy.9.s_ref), custom_call_target="tpu_custom_call" | custom-call | tf_op jit(solution)/shard_map/prep/pallas_call | solution.py:155
  1.8 0.0 copy-start
  1.8 3.1 %collective-permute-start = (bf16[5,160,128]{2,1,0:T(8,128)(2,1)S(1)}, bf16[5,160,128]{2,1,0:T(8,128)(2,1)S(1)}, u32[]{:S(2)}, u32[]{:S(2)}) collective-permute-start(bf16[5,160,128]{2,1,0:T(8,128)(2,1)S(1)} %get-tuple-element.30), channel_id=1, source_target_pairs={{0,4},{1,5},{2,6},{3,7},{4,0},{5,1},{6,2},{7,3},{8,12},{9,13},{10,... | collective-permute-start | bytes 614408 | tf_op jit(solution)/shard_map/ppermute | solution.py:583
  4.9 0.0 collective-permute-start.2
  4.9 2.6 %collective-permute-start.1 = (bf16[1,160,128]{2,1,0:T(8,128)(2,1)S(1)}, bf16[1,160,128]{2,1,0:T(8,128)(2,1)S(1)}, u32[]{:S(2)}, u32[]{:S(2)}) collective-permute-start(bf16[1,160,128]{2,1,0:T(8,128)(2,1)S(1)} %get-tuple-element.32.rest_1_), channel_id=1, source_target_pairs={{0,8},{4,12},{8,0},{12,4},{1,9},{5,13},{9,1},{13,5},{2,10},{6,14},... | collective-permute-start | bytes 122888 | tf_op jit(solution)/shard_map/ppermute | solution.py:581
  7.5 2.9 %collective-permute-start.3 = (bf16[1,160,128]{2,1,0:T(8,128)(2,1)S(1)}, bf16[1,160,128]{2,1,0:T(8,128)(2,1)S(1)}, u32[]{:S(2)}, u32[]{:S(2)}) collective-permute-start(bf16[1,160,128]{2,1,0:T(8,128)(2,1)S(1)} %get-tuple-element.32.rest_1_), channel_id=1, source_target_pairs={{0,12},{4,8},{8,4},{12,0},{1,13},{5,9},{9,5},{13,1},{2,14},{6,10},... | collective-permute-start | bytes 122888 | tf_op jit(solution)/shard_map/ppermute | solution.py:581
  10.4 0.0 copy-done
  10.4 2.3 %local.1 = (bf16[8,2,160,128]{3,2,1,0:T(8,128)(2,1)S(1)}, bf16[512,768]{1,0:T(8,128)(2,1)S(1)}, f32[8,8,8,320]{3,2,1,0:T(8,128)S(1)}, bf16[320,1024]{1,0:T(8,128...) custom-call(bf16[8,64,320]{2,1,0:T(8,128)(2,1)S(1)} %get-tuple-element.23.x_re, ...), custom_call_target="tpu_custom_call" | custom-call | flops 314572800 | bytes 4194304 | tf_op jit(solution)/shard_map/local/pallas_call | solution.py:235
  12.7 1.8 %collective-permute-done.1.rest_0_ = bf16[1,160,128]{2,1,0:T(8,128)(2,1)S(1)} collective-permute-done((bf16[1,160,128]{2,1,0:T(8,128)(2,1)S(1)}, bf16[1,160,128]{2,1,0:T(8,128)(2,1)S(1)}, u32[]{:S(2)}, u32[]{:S(2)}) %collective-permute-start.1) | collective-permute-done | bytes 40992 | tf_op jit(solution)/shard_map/ppermute | solution.py:581
  14.5 0.5 %early.3.rest_0_ = bf16[128,768]{1,0:T(8,128)(2,1)S(1)} custom-call(f32[1,320]{1,0:T(1,128)S(1)} %reshape.5.gain_ref, bf16[320,1024]{1,0:T(8,128)(2,1)S(1)} %get-tuple-element.29.tw_ref, bf16[1,160,128]{2,1,0:T(8,128)(2,1)S(1)} %collective-permute-done.1.rest_0_, bf16[1,160,128]{2,1,0:T(8,128)(2,1)S(1)} %get-tuple-element.32.rest_1_), custom_call_target="tpu_custom_call" | custom-call | flops 52428800 | bytes 2097152 | tf_op jit(solution)/shard_map/early/pallas_call | solution.py:289
  15.0 0.0 collective-permute-done.rest_0_.rest_3_
  15.0 0.6 %early.2.kv_ref = bf16[256,768]{1,0:T(8,128)(2,1)S(1)} custom-call(f32[1,320]{1,0:T(1,128)S(1)} %reshape.5.gain_ref, bf16[320,1024]{1,0:T(8,128)(2,1)S(1)} %get-tuple-element.29.tw_ref, bf16[5,160,128]{2,1,0:T(8,128)(2,1)S(1)} %collective-permute-done.rest_0_.rest_3_), custom_call_target="tpu_custom_call" | custom-call | flops 104857600 | bytes 2097152 | tf_op jit(solution)/shard_map/early/pallas_call | solution.py:289
  15.6 0.0 collective-permute-done.3.rest_2_
  15.6 0.0 collective-permute-done.2.rest_1_
  15.6 2.1 %cross.1 = (bf16[2,160,128]{2,1,0:T(8,128)(2,1)S(1)}, bf16[2,160,128]{2,1,0:T(8,128)(2,1)S(1)}, bf16[384,768]{1,0:T(8,128)(2,1)S(1)}) custom-call(bf16[8,2,160,128]{3,2,1,0:T(8,128)(2,1)S(1)} %get-tuple-element.26.q_ref, bf16[512,768]{1,0:T(8,128)(2,1)S(1)} %get-tuple-element.27.own_ref, f32[8,8,8,320]{3,2,1,0:T(8,128)S(1)} %get-tuple-element.28.xg_ref, ...), custom_call_target="tpu_custom_call" | custom-call | flops 209715200 | bytes 4194304 | tf_op jit(solution)/shard_map/cross/pallas_call | solution.py:405
  17.7 1.4 %near.1 = (bf16[2,160,128]{2,1,0:T(8,128)(2,1)S(1)}, bf16[2,160,128]{2,1,0:T(8,128)(2,1)S(1)}) custom-call(bf16[8,2,160,128]{3,2,1,0:T(8,128)(2,1)S(1)} %get-tuple-element.26.q_ref, bf16[512,768]{1,0:T(8,128)(2,1)S(1)} %get-tuple-element.27.own_ref, f32[8,8,8,320]{3,2,1,0:T(8,128)S(1)} %get-tuple-element.28.xg_ref, bf16[256,768]{1,0:T(8,128)(2,1)S(1)} %early.2.kv_ref, ...), custom_call_target="tpu_custom_call" | custom-call | flops 209715200 | bytes 4194304 | tf_op jit(solution)/shard_map/near/pallas_call | solution.py:405
  19.2 0.0 copy-start.1
  19.2 0.1 collective-permute-start.4
  19.3 1.6 %collective-permute-start.5 = (bf16[2,160,128]{2,1,0:T(8,128)(2,1)S(1)}, bf16[2,160,128]{2,1,0:T(8,128)(2,1)S(1)}, u32[]{:S(2)}, u32[]{:S(2)}) collective-permute-start(bf16[2,160,128]{2,1,0:T(8,128)(2,1)S(1)} %get-tuple-element.39), channel_id=1, source_target_pairs={{0,2},{1,3},{2,0},{3,1},{4,6},{5,7},{6,4},{7,5},{8,10},{9,11},{10,... | collective-permute-start | bytes 245768 | tf_op jit(solution)/shard_map/ppermute | solution.py:601
  20.8 0.3 %collective-permute-start.6 = (bf16[2,160,128]{2,1,0:T(8,128)(2,1)S(1)}, bf16[2,160,128]{2,1,0:T(8,128)(2,1)S(1)}, u32[]{:S(2)}, u32[]{:S(2)}) collective-permute-start(bf16[2,160,128]{2,1,0:T(8,128)(2,1)S(1)} %get-tuple-element.40), channel_id=1, source_target_pairs={{0,3},{1,2},{2,1},{3,0},{4,7},{5,6},{6,5},{7,4},{8,11},{9,10},{10,... | collective-permute-start | bytes 245768 | tf_op jit(solution)/shard_map/ppermute | solution.py:601
  21.1 0.0 copy-done.1
  21.1 0.0 collective-permute-done.4.rest_1_
  21.1 0.7 %ready.1 = (bf16[256,1024]{1,0:T(8,128)(2,1)S(1)}, f32[2,320,128]{2,1,0:T(8,128)S(1)}) custom-call(f32[1,320]{1,0:T(1,128)S(1)} %reshape.4.gain_ref, bf16[320,1024]{1,0:T(8,128)(2,1)S(1)} %get-tuple-element.24.sw_ref, bf16[2,160,128]{2,1,0:T(8,128)(2,1)S(1)} %get-tuple-element.35.rest_0_, bf16[2,160,128]{2,1,0:T(8,128)(2,1)S(1)} %collective-permute-done.4.rest_1_), custom_call_target="tpu_custom_call" | custom-call | flops 157286400 | bytes 2097152 | tf_op jit(solution)/shard_map/ready/pallas_call | solution.py:451
  21.9 2.5 %collective-permute-done.5.rest_0_ = bf16[2,160,128]{2,1,0:T(8,128)(2,1)S(1)} collective-permute-done((bf16[2,160,128]{2,1,0:T(8,128)(2,1)S(1)}, bf16[2,160,128]{2,1,0:T(8,128)(2,1)S(1)}, u32[]{:S(2)}, u32[]{:S(2)}) %collective-permute-start.5) | collective-permute-done | bytes 81952 | tf_op jit(solution)/shard_map/ppermute | solution.py:601
  24.4 1.2 %collective-permute-done.6.rest_1_ = bf16[2,160,128]{2,1,0:T(8,128)(2,1)S(1)} collective-permute-done((bf16[2,160,128]{2,1,0:T(8,128)(2,1)S(1)}, bf16[2,160,128]{2,1,0:T(8,128)(2,1)S(1)}, u32[]{:S(2)}, u32[]{:S(2)}) %collective-permute-start.6) | collective-permute-done | bytes 81952 | tf_op jit(solution)/shard_map/ppermute | solution.py:601
  25.6 2.6 %spatial.1 = bf16[2,320,256]{2,1,0:T(8,128)(2,1)} custom-call(f32[1,320]{1,0:T(1,128)S(1)} %reshape.4.gain_ref, bf16[320,1024]{1,0:T(8,128)(2,1)S(1)} %get-tuple-element.24.sw_ref, bf16[320,320]{1,0:T(8,128)(2,1)S(1)} %get-tuple-element.25.so_ref, bf16[256,1024]{1,0:T(8,128)(2,1)S(1)} %get-tuple-element.37.packed_ref, ...), custom_call_target="tpu_custom_call" | custom-call | flops 587202560 | bytes 4194304 | tf_op jit(solution)/shard_map/spatial/pallas_call | solution.py:527
  (2 shorter events, 0.0 us)
Async XLA Ops:
  1.8 8.6 %copy-start = (f32[320]{0:T(512)S(1)}, f32[320]{0:T(512)}, u32[]{:S(2)}) copy-start(f32[320]{0:T(512)} %param.10) | copy-start | bytes 3844
  1.8 13.2 %collective-permute-start = (bf16[5,160,128]{2,1,0:T(8,128)(2,1)S(1)}, bf16[5,160,128]{2,1,0:T(8,128)(2,1)S(1)}, u32[]{:S(2)}, u32[]{:S(2)}) collective-permute-start(bf16[5,160,128]{2,1,0:T(8,128)(2,1)S(1)} %get-tuple-element.30), channel_id=1, source_target_pairs={{0,4},{1,5},{2,6},{3,7},{4,0},{5,1},{6,2},{7,3},{8,12},{9,13},{10,... | collective-permute-start | bytes 614408 | tf_op jit(solution)/shard_map/ppermute | solution.py:583
  4.9 10.7 %collective-permute-start.2 = (bf16[4,160,128]{2,1,0:T(8,128)(2,1)S(1)}, bf16[4,160,128]{2,1,0:T(8,128)(2,1)S(1)}, u32[]{:S(2)}, u32[]{:S(2)}) collective-permute-start(bf16[4,160,128]{2,1,0:T(8,128)(2,1)S(1)} %get-tuple-element.33), channel_id=1, source_target_pairs={{0,1},{1,0},{2,3},{3,2},{4,8},{5,9},{6,10},{7,11},{8,4},{9,5},{10,... | collective-permute-start | bytes 491528 | tf_op jit(solution)/shard_map/ppermute | solution.py:584
  4.9 9.6 %collective-permute-start.1 = (bf16[1,160,128]{2,1,0:T(8,128)(2,1)S(1)}, bf16[1,160,128]{2,1,0:T(8,128)(2,1)S(1)}, u32[]{:S(2)}, u32[]{:S(2)}) collective-permute-start(bf16[1,160,128]{2,1,0:T(8,128)(2,1)S(1)} %get-tuple-element.32.rest_1_), channel_id=1, source_target_pairs={{0,8},{4,12},{8,0},{12,4},{1,9},{5,13},{9,1},{13,5},{2,10},{6,14},... | collective-permute-start | bytes 122888 | tf_op jit(solution)/shard_map/ppermute | solution.py:581
  7.5 8.1 %collective-permute-start.3 = (bf16[1,160,128]{2,1,0:T(8,128)(2,1)S(1)}, bf16[1,160,128]{2,1,0:T(8,128)(2,1)S(1)}, u32[]{:S(2)}, u32[]{:S(2)}) collective-permute-start(bf16[1,160,128]{2,1,0:T(8,128)(2,1)S(1)} %get-tuple-element.32.rest_1_), channel_id=1, source_target_pairs={{0,12},{4,8},{8,4},{12,0},{1,13},{5,9},{9,5},{13,1},{2,14},{6,10},... | collective-permute-start | bytes 122888 | tf_op jit(solution)/shard_map/ppermute | solution.py:581
  19.2 1.9 %copy-start.1 = (f32[320]{0:T(512)S(1)}, f32[320]{0:T(512)}, u32[]{:S(2)}) copy-start(f32[320]{0:T(512)} %param.13) | copy-start | bytes 3844
  19.2 1.9 %collective-permute-start.4 = (bf16[2,160,128]{2,1,0:T(8,128)(2,1)S(1)}, bf16[2,160,128]{2,1,0:T(8,128)(2,1)S(1)}, u32[]{:S(2)}, u32[]{:S(2)}) collective-permute-start(bf16[2,160,128]{2,1,0:T(8,128)(2,1)S(1)} %get-tuple-element.36), channel_id=1, source_target_pairs={{0,1},{1,0},{2,3},{3,2},{4,5},{5,4},{6,7},{7,6},{8,9},{9,8},{10,11... | collective-permute-start | bytes 245768 | tf_op jit(solution)/shard_map/ppermute | solution.py:601
  19.3 5.1 %collective-permute-start.5 = (bf16[2,160,128]{2,1,0:T(8,128)(2,1)S(1)}, bf16[2,160,128]{2,1,0:T(8,128)(2,1)S(1)}, u32[]{:S(2)}, u32[]{:S(2)}) collective-permute-start(bf16[2,160,128]{2,1,0:T(8,128)(2,1)S(1)} %get-tuple-element.39), channel_id=1, source_target_pairs={{0,2},{1,3},{2,0},{3,1},{4,6},{5,7},{6,4},{7,5},{8,10},{9,11},{10,... | collective-permute-start | bytes 245768 | tf_op jit(solution)/shard_map/ppermute | solution.py:601
  20.8 4.7 %collective-permute-start.6 = (bf16[2,160,128]{2,1,0:T(8,128)(2,1)S(1)}, bf16[2,160,128]{2,1,0:T(8,128)(2,1)S(1)}, u32[]{:S(2)}, u32[]{:S(2)}) collective-permute-start(bf16[2,160,128]{2,1,0:T(8,128)(2,1)S(1)} %get-tuple-element.40), channel_id=1, source_target_pairs={{0,3},{1,2},{2,1},{3,0},{4,7},{5,6},{6,5},{7,4},{8,11},{9,10},{10,... | collective-permute-start | bytes 245768 | tf_op jit(solution)/shard_map/ppermute | solution.py:601

commit v8 on v6

--- a/solution.py
+++ b/solution.py
@@ -16,7 +16,7 @@
 SHARPNESS = 1.0 / (math.sqrt(HEAD_DIM) * math.log(2.0))
 DIRECT_CLIPS = 4
 LIMIT = 24 << 20
-LEAD = 8
+LEAD = 12
 SPATIAL_LEAD = 2
 SIDES = ((0, 1),)
 FAR = pl.BlockSpec(memory_space=pltpu.HBM)
@@ -287,23 +287,21 @@
     return jnp.dot(rows, tw_ref[:, whole:], preferred_element_type=jnp.float32).astype(jnp.bfloat16)
 
 
-def early_kernel(gain_ref, tw_ref, a_ref, *rest):
-    *pick_refs, kv_ref, normed_ref = rest
-    dense = [a_ref[i] for i in range(a_ref.shape[0])]
-    for ref in pick_refs:
-        dense += [ref[i] for i in range(ref.shape[0])]
+def early_kernel(gain_ref, tw_ref, *rest):
+    *refs, kv_ref, normed_ref = rest
+    dense = [ref[i] for ref in refs for i in range(min(HALO, ref.shape[0]))]
     pixels = normed_ref.shape[0] * SUB
     kv_ref[...] = remote_pairs(dense, gain_ref[...], tw_ref, normed_ref, pixels)
 
 
-def early(gain, weights, a, picks, pixels, slots):
+def early(gain, weights, frames, pixels, slots):
     channels = weights.shape[0]
     groups = pixels // SUB
     kind = weights.dtype
     return pl.pallas_call(
         early_kernel,
         out_shape=pltpu.VMEM((pixels * slots, weights.shape[1] - channels // LANES * LANES), kind),
-        in_specs=[VMEM] + [VMEM] * (2 + len(picks)),
+        in_specs=[VMEM] + [VMEM] * (1 + len(frames)),
         out_specs=VMEM,
         scratch_shapes=[pltpu.VMEM((groups, slots, SUB, channels), jnp.float32)],
         cost_estimate=pl.CostEstimate(
@@ -311,15 +309,16 @@
         ),
         compiler_params=pltpu.CompilerParams(vmem_limit_bytes=LIMIT),
         name="early",
-    )(gain.reshape(1, channels), weights, a, *picks)
+    )(gain.reshape(1, channels), weights, *frames)
 
 
 def temporal_kernel(
-    clips, early_held, late_held, pix_count, cross,
+    clips, ahead, early_held, late_held, pix_count, cross,
     q_ref, own_ref, xg_ref, kv_ref, gain_ref, tw_ref, to_ref, *rest,
 ):
     halves = pix_count // 2
     scratch = 4 if cross else 2
+    before_refs, rest = rest[:ahead], rest[ahead:]
     last_refs, sends, rest = (
         rest[: len(rest) - halves - scratch],
         rest[len(rest) - halves - scratch : len(rest) - scratch],
@@ -330,7 +329,7 @@
     _, _, first_there, second_there = neighbours(clips)
     if cross:
         late_ref, normed_ref, att_ref, rows_ref = rest
-        dense = [ref[i] for ref in last_refs for i in range(ref.shape[0])]
+        dense = [ref[i] for ref in last_refs for i in range(HALO if ref.shape[0] == HALO + 1 else 0, ref.shape[0])]
         late_ref[...] = remote_pairs(dense, gain_ref[...], tw_ref, normed_ref, pixels)
     else:
         (late_ref,) = last_refs
@@ -343,11 +342,12 @@
     part = frames // 2
     mine, own = part * SUB, frames * SUB
     soon, more = kv_ref.shape[0] // groups, late_ref.shape[0] // groups
-    shape = (mine, own + soon + more)
+    sooner = sum(ref.shape[0] for ref in before_refs) // groups
+    shape = (mine, own + sooner + soon + more)
     row = lax.broadcasted_iota(jnp.int32, shape, 0)
     column = lax.broadcasted_iota(jnp.int32, shape, 1)
     usable = lax.rem(row, SUB) == lax.rem(column, SUB)
-    slot = column // SUB - frames
+    slot = (column - sooner) // SUB - frames
     usable &= (slot < 0) | (slot >= HALO) | first_there
     usable &= (slot < early_held) | (slot >= soon // SUB)
     usable &= (slot < soon // SUB) | (slot >= soon // SUB + HALO) | second_there
@@ -361,6 +361,7 @@
         return jnp.concatenate(
             [
                 own_ref[g * own : (g + 1) * own, span],
+                *(ref[g * sooner : (g + 1) * sooner, span] for ref in before_refs),
                 kv_ref[g * soon : (g + 1) * soon, span],
                 late_ref[g * more : (g + 1) * more, span],
             ],
@@ -396,7 +397,7 @@
 
 
 def temporal(
-    parts, pairs, gain, weights, out_matrix, last, clips, early_held, late_held, pix_count, cross
+    parts, pairs, gain, weights, out_matrix, before, last, clips, early_held, late_held, pix_count, cross
 ):
     q, own, xg = parts
     groups, frames, _, channels = xg.shape
@@ -414,9 +415,9 @@
         out_shape = out_shape + [pltpu.VMEM((pixels * slots, pairs.shape[1]), kind)]
         scratch = [pltpu.VMEM((groups, slots, SUB, channels), jnp.float32)] + scratch
     return pl.pallas_call(
-        functools.partial(temporal_kernel, clips, early_held, late_held, pix_count, cross),
+        functools.partial(temporal_kernel, clips, len(before), early_held, late_held, pix_count, cross),
         out_shape=out_shape,
-        in_specs=[VMEM] * 4 + [VMEM] + [VMEM] * (2 + len(last)),
+        in_specs=[VMEM] * 4 + [VMEM] + [VMEM] * (2 + len(before) + len(last)),
         out_specs=[VMEM] * len(out_shape),
         scratch_shapes=scratch,
         cost_estimate=pl.CostEstimate(
@@ -424,7 +425,7 @@
         ),
         compiler_params=pltpu.CompilerParams(vmem_limit_bytes=LIMIT),
         name="cross" if cross else "near",
-    )(q, own, xg, pairs, gain.reshape(1, channels), weights, out_matrix, *last)
+    )(q, own, xg, pairs, gain.reshape(1, channels), weights, out_matrix, *before, *last)
 
 
 def gather_rows(chunks, rows_ref, channels):
@@ -598,12 +599,15 @@
     q, own, xg, tw, sw, to, so = local(
         x, temporal_gain, temporal_qkv, temporal_out, spatial_qkv, spatial_out
     )
+    each, before = latents.shape[1], []
+    if not gathered:
+        before = [early(temporal_gain, tw, soon + last[:1], each, up(len(soon) + 1, 2))]
+        last = last[1:] + [a]
     last = [b] + last
-    early_held = sum(part.shape[0] for part in [a] + soon)
-    late_held = sum(part.shape[0] for part in last)
-    pairs = early(temporal_gain, tw, a, soon, latents.shape[1], up(early_held, 2))
-    rest = ((q, own, xg), pairs, temporal_gain, tw, to)
-    held = (clips, early_held, late_held, pix_count)
+    late_held = sum(1 if part is a else part.shape[0] for part in last)
+    pairs = early(temporal_gain, tw, [a], each, up(HALO, 2))
+    rest = ((q, own, xg), pairs, temporal_gain, tw, to, before)
+    held = (clips, HALO, late_held, pix_count)
     halves = pix_count // 2
     *sends, late = temporal(*rest, last, *held, True)
 

time: 28 us -> 28.3 us (1.011)
  Pallas kernels: 11 us -> 11.3 us
    pallas_call x1 -> x2, Pallas kernels: 0.81 us -> 1.1 us  [early(): pl.pallas_call(early_kernel, out_shape=pltpu.VMEM((pixels * slots, weight...]
  transfers between devices with their start and end apart: 7 -> 7, of which waited for: 3 -> 3; matrix products, arithmetic and copies ran while one was open for 0% -> 0% of each run, Pallas kernels for 14% -> 15%
where the time goes in v8:
time: 28.3 us; the launch traced here: 28.1 us
  Pallas kernels  11.3 us (40%)
  starting transfers between devices  10.5 us (37%)
  waiting for transfers between devices  5.48 us (19%)
  between operations  0.81 us (3%)
    ppermute x2, starting transfers between devices, body(): pick = lax.ppermute(p, 'clip', [(i, i ^ step) for i in range(clips)])  5.51 us
    ppermute x3, waiting for transfers between devices, swap(): return lax.ppermute(chunk, 'pix', [(i, i ^ step) for i in range(pix_count)])  3.7 us
    pallas_call x2, Pallas kernels, temporal(): pl.pallas_call(functools.partial(temporal_kernel, clips, len(before), ear...  3.54 us
    ppermute x1, starting transfers between devices, body(): a = lax.ppermute(a, ('clip', 'pix'), border_pairs(clips, pix_count, 0))  3.12 us
    pallas_call x1, Pallas kernels, spatial(): pl.pallas_call(functools.partial(spatial_kernel, halves), out_shape=jax.S...  2.65 us
    pallas_call x1, Pallas kernels, local(): pl.pallas_call(local_kernel, out_shape=[pltpu.VMEM((groups, 2, channels /...  2.27 us
    ppermute x3, starting transfers between devices, swap(): return lax.ppermute(chunk, 'pix', [(i, i ^ step) for i in range(pix_count)])  1.92 us
    ppermute x2, waiting for transfers between devices, body(): pick = lax.ppermute(p, 'clip', [(i, i ^ step) for i in range(clips)])  1.78 us
  transfers between devices with their start and end apart: 7, of which 3 were waited for; matrix products, arithmetic and copies ran while one was open for 0% of the time, Pallas kernels for 15%

profile of v8, /device:TPU:0, one launch (start us, length us, event | category | flops | bytes accessed | tf_op | source)
XLA Modules:
  0.0 28.1 jit_solution(298747551482110736)
XLA Ops:
  0.0 0.0 copy-start
  0.7 0.9 %pick.1.p_ref.rest_1_ = bf16[1,160,128]{2,1,0:T(8,128)(2,1)S(1)} custom-call(bf16[8,64,320]{2,1,0:T(8,128)(2,1)} %x_ref.3, s32[1]{0:T(128)S(6)} %copy.9.s_ref), custom_call_target="tpu_custom_call" | custom-call | tf_op jit(solution)/shard_map/pick/pallas_call | solution.py:146
  1.6 0.0 copy-done
  1.6 0.1 prep.1
  1.7 0.0 copy-start.1
  1.7 3.1 %collective-permute-start = (bf16[5,160,128]{2,1,0:T(8,128)(2,1)S(1)}, bf16[5,160,128]{2,1,0:T(8,128)(2,1)S(1)}, u32[]{:S(2)}, u32[]{:S(2)}) collective-permute-start(bf16[5,160,128]{2,1,0:T(8,128)(2,1)S(1)} %get-tuple-element.27), channel_id=1, source_target_pairs={{0,4},{1,5},{2,6},{3,7},{4,0},{5,1},{6,2},{7,3},{8,12},{9,13},{10,... | collective-permute-start | bytes 614408 | tf_op jit(solution)/shard_map/ppermute | solution.py:597
  4.8 0.0 collective-permute-start.2
  4.8 2.6 %collective-permute-start.1 = (bf16[1,160,128]{2,1,0:T(8,128)(2,1)S(1)}, bf16[1,160,128]{2,1,0:T(8,128)(2,1)S(1)}, u32[]{:S(2)}, u32[]{:S(2)}) collective-permute-start(bf16[1,160,128]{2,1,0:T(8,128)(2,1)S(1)} %pick.1.p_ref.rest_1_), channel_id=1, source_target_pairs={{0,8},{4,12},{8,0},{12,4},{1,9},{5,13},{9,1},{13,5},{2,10},{6,14},... | collective-permute-start | bytes 122888 | tf_op jit(solution)/shard_map/ppermute | solution.py:595
  7.4 2.9 %collective-permute-start.3 = (bf16[1,160,128]{2,1,0:T(8,128)(2,1)S(1)}, bf16[1,160,128]{2,1,0:T(8,128)(2,1)S(1)}, u32[]{:S(2)}, u32[]{:S(2)}) collective-permute-start(bf16[1,160,128]{2,1,0:T(8,128)(2,1)S(1)} %pick.1.p_ref.rest_1_), channel_id=1, source_target_pairs={{0,12},{4,8},{8,4},{12,0},{1,13},{5,9},{9,5},{13,1},{2,14},{6,10},... | collective-permute-start | bytes 122888 | tf_op jit(solution)/shard_map/ppermute | solution.py:595
  10.4 0.0 copy-done.1
  10.4 2.3 %local.1 = (bf16[8,2,160,128]{3,2,1,0:T(8,128)(2,1)S(1)}, bf16[512,768]{1,0:T(8,128)(2,1)S(1)}, f32[8,8,8,320]{3,2,1,0:T(8,128)S(1)}, bf16[320,1024]{1,0:T(8,128...) custom-call(bf16[8,64,320]{2,1,0:T(8,128)(2,1)S(1)} %copy-done, ...), custom_call_target="tpu_custom_call" | custom-call | flops 314572800 | bytes 4194304 | tf_op jit(solution)/shard_map/local/pallas_call | solution.py:247
  12.6 1.8 %collective-permute-done.1.rest_0_ = bf16[1,160,128]{2,1,0:T(8,128)(2,1)S(1)} collective-permute-done((bf16[1,160,128]{2,1,0:T(8,128)(2,1)S(1)}, bf16[1,160,128]{2,1,0:T(8,128)(2,1)S(1)}, u32[]{:S(2)}, u32[]{:S(2)}) %collective-permute-start.1) | collective-permute-done | bytes 40992 | tf_op jit(solution)/shard_map/ppermute | solution.py:595
  14.4 0.5 %early.3.rest_0_ = bf16[128,768]{1,0:T(8,128)(2,1)S(1)} custom-call(f32[1,320]{1,0:T(1,128)S(1)} %reshape.5.gain_ref, bf16[320,1024]{1,0:T(8,128)(2,1)S(1)} %get-tuple-element.26.tw_ref, bf16[1,160,128]{2,1,0:T(8,128)(2,1)S(1)} %collective-permute-done.1.rest_0_, bf16[1,160,128]{2,1,0:T(8,128)(2,1)S(1)} %pick.1.p_ref.rest_1_), custom_call_target="tpu_custom_call" | custom-call | flops 52428800 | bytes 2097152 | tf_op jit(solution)/shard_map/early/pallas_call | solution.py:301
  14.9 0.0 collective-permute-done.rest_0_.rest_3_
  14.9 0.6 %early.2.kv_ref = bf16[256,768]{1,0:T(8,128)(2,1)S(1)} custom-call(f32[1,320]{1,0:T(1,128)S(1)} %reshape.5.gain_ref, bf16[320,1024]{1,0:T(8,128)(2,1)S(1)} %get-tuple-element.26.tw_ref, bf16[5,160,128]{2,1,0:T(8,128)(2,1)S(1)} %collective-permute-done.rest_0_.rest_3_), custom_call_target="tpu_custom_call" | custom-call | flops 104857600 | bytes 2097152 | tf_op jit(solution)/shard_map/early/pallas_call | solution.py:301
  15.5 0.0 collective-permute-done.3.rest_2_
  15.6 0.0 collective-permute-done.2.rest_1_
  15.6 2.1 %cross.1 = (bf16[2,160,128]{2,1,0:T(8,128)(2,1)S(1)}, bf16[2,160,128]{2,1,0:T(8,128)(2,1)S(1)}, bf16[384,768]{1,0:T(8,128)(2,1)S(1)}) custom-call(bf16[8,2,160,128]{3,2,1,0:T(8,128)(2,1)S(1)} %get-tuple-element.23.q_ref, bf16[512,768]{1,0:T(8,128)(2,1)S(1)} %get-tuple-element.24.own_ref, f32[8,8,8,320]{3,2,1,0:T(8,128)S(1)} %get-tuple-element.25.xg_ref, ...), custom_call_target="tpu_custom_call" | custom-call | flops 209715200 | bytes 4194304 | tf_op jit(solution)/shard_map/cross/pallas_call | solution.py:417
  17.7 1.5 %near.1 = (bf16[2,160,128]{2,1,0:T(8,128)(2,1)S(1)}, bf16[2,160,128]{2,1,0:T(8,128)(2,1)S(1)}) custom-call(bf16[8,2,160,128]{3,2,1,0:T(8,128)(2,1)S(1)} %get-tuple-element.23.q_ref, bf16[512,768]{1,0:T(8,128)(2,1)S(1)} %get-tuple-element.24.own_ref, f32[8,8,8,320]{3,2,1,0:T(8,128)S(1)} %get-tuple-element.25.xg_ref, bf16[256,768]{1,0:T(8,128)(2,1)S(1)} %early.2.kv_ref, ...), custom_call_target="tpu_custom_call" | custom-call | flops 209715200 | bytes 4194304 | tf_op jit(solution)/shard_map/near/pallas_call | solution.py:417
  19.1 0.0 copy-start.2
  19.1 0.1 collective-permute-start.4
  19.2 1.6 %collective-permute-start.5 = (bf16[2,160,128]{2,1,0:T(8,128)(2,1)S(1)}, bf16[2,160,128]{2,1,0:T(8,128)(2,1)S(1)}, u32[]{:S(2)}, u32[]{:S(2)}) collective-permute-start(bf16[2,160,128]{2,1,0:T(8,128)(2,1)S(1)} %get-tuple-element.35), channel_id=1, source_target_pairs={{0,2},{1,3},{2,0},{3,1},{4,6},{5,7},{6,4},{7,5},{8,10},{9,11},{10,... | collective-permute-start | bytes 245768 | tf_op jit(solution)/shard_map/ppermute | solution.py:615
  20.8 0.3 %collective-permute-start.6 = (bf16[2,160,128]{2,1,0:T(8,128)(2,1)S(1)}, bf16[2,160,128]{2,1,0:T(8,128)(2,1)S(1)}, u32[]{:S(2)}, u32[]{:S(2)}) collective-permute-start(bf16[2,160,128]{2,1,0:T(8,128)(2,1)S(1)} %get-tuple-element.36), channel_id=1, source_target_pairs={{0,3},{1,2},{2,1},{3,0},{4,7},{5,6},{6,5},{7,4},{8,11},{9,10},{10,... | collective-permute-start | bytes 245768 | tf_op jit(solution)/shard_map/ppermute | solution.py:615
  21.0 0.0 copy-done.2
  21.1 0.0 collective-permute-done.4.rest_1_
  21.1 0.7 %ready.1 = (bf16[256,1024]{1,0:T(8,128)(2,1)S(1)}, f32[2,320,128]{2,1,0:T(8,128)S(1)}) custom-call(f32[1,320]{1,0:T(1,128)S(1)} %reshape.4.gain_ref, bf16[320,1024]{1,0:T(8,128)(2,1)S(1)} %get-tuple-element.21.sw_ref, bf16[2,160,128]{2,1,0:T(8,128)(2,1)S(1)} %get-tuple-element.31.rest_0_, bf16[2,160,128]{2,1,0:T(8,128)(2,1)S(1)} %collective-permute-done.4.rest_1_), custom_call_target="tpu_custom_call" | custom-call | flops 157286400 | bytes 2097152 | tf_op jit(solution)/shard_map/ready/pallas_call | solution.py:463
  21.8 2.6 %collective-permute-done.5.rest_0_ = bf16[2,160,128]{2,1,0:T(8,128)(2,1)S(1)} collective-permute-done((bf16[2,160,128]{2,1,0:T(8,128)(2,1)S(1)}, bf16[2,160,128]{2,1,0:T(8,128)(2,1)S(1)}, u32[]{:S(2)}, u32[]{:S(2)}) %collective-permute-start.5) | collective-permute-done | bytes 81952 | tf_op jit(solution)/shard_map/ppermute | solution.py:615
  24.3 1.1 %collective-permute-done.6.rest_1_ = bf16[2,160,128]{2,1,0:T(8,128)(2,1)S(1)} collective-permute-done((bf16[2,160,128]{2,1,0:T(8,128)(2,1)S(1)}, bf16[2,160,128]{2,1,0:T(8,128)(2,1)S(1)}, u32[]{:S(2)}, u32[]{:S(2)}) %collective-permute-start.6) | collective-permute-done | bytes 81952 | tf_op jit(solution)/shard_map/ppermute | solution.py:615
  25.5 2.7 %spatial.1 = bf16[2,320,256]{2,1,0:T(8,128)(2,1)} custom-call(f32[1,320]{1,0:T(1,128)S(1)} %reshape.4.gain_ref, bf16[320,1024]{1,0:T(8,128)(2,1)S(1)} %get-tuple-element.21.sw_ref, bf16[320,320]{1,0:T(8,128)(2,1)S(1)} %get-tuple-element.22.so_ref, bf16[256,1024]{1,0:T(8,128)(2,1)S(1)} %get-tuple-element.33.packed_ref, ...), custom_call_target="tpu_custom_call" | custom-call | flops 587202560 | bytes 4194304 | tf_op jit(solution)/shard_map/spatial/pallas_call | solution.py:539
  (2 shorter events, 0.0 us)
Async XLA Ops:
  0.0 1.6 %copy-start = (bf16[8,64,320]{2,1,0:T(8,128)(2,1)S(1)}, bf16[8,64,320]{2,1,0:T(8,128)(2,1)}, u32[]{:S(2)}) copy-start(bf16[8,64,320]{2,1,0:T(8,128)(2,1)} %x_ref.3) | copy-start | bytes 983044
  1.7 8.6 %copy-start.1 = (f32[320]{0:T(512)S(1)}, f32[320]{0:T(512)}, u32[]{:S(2)}) copy-start(f32[320]{0:T(512)} %param.10) | copy-start | bytes 3844
  1.7 13.2 %collective-permute-start = (bf16[5,160,128]{2,1,0:T(8,128)(2,1)S(1)}, bf16[5,160,128]{2,1,0:T(8,128)(2,1)S(1)}, u32[]{:S(2)}, u32[]{:S(2)}) collective-permute-start(bf16[5,160,128]{2,1,0:T(8,128)(2,1)S(1)} %get-tuple-element.27), channel_id=1, source_target_pairs={{0,4},{1,5},{2,6},{3,7},{4,0},{5,1},{6,2},{7,3},{8,12},{9,13},{10,... | collective-permute-start | bytes 614408 | tf_op jit(solution)/shard_map/ppermute | solution.py:597
  4.8 10.7 %collective-permute-start.2 = (bf16[4,160,128]{2,1,0:T(8,128)(2,1)S(1)}, bf16[4,160,128]{2,1,0:T(8,128)(2,1)S(1)}, u32[]{:S(2)}, u32[]{:S(2)}) collective-permute-start(bf16[4,160,128]{2,1,0:T(8,128)(2,1)S(1)} %get-tuple-element.29), channel_id=1, source_target_pairs={{0,1},{1,0},{2,3},{3,2},{4,8},{5,9},{6,10},{7,11},{8,4},{9,5},{10,... | collective-permute-start | bytes 491528 | tf_op jit(solution)/shard_map/ppermute | solution.py:598
  4.8 9.6 %collective-permute-start.1 = (bf16[1,160,128]{2,1,0:T(8,128)(2,1)S(1)}, bf16[1,160,128]{2,1,0:T(8,128)(2,1)S(1)}, u32[]{:S(2)}, u32[]{:S(2)}) collective-permute-start(bf16[1,160,128]{2,1,0:T(8,128)(2,1)S(1)} %pick.1.p_ref.rest_1_), channel_id=1, source_target_pairs={{0,8},{4,12},{8,0},{12,4},{1,9},{5,13},{9,1},{13,5},{2,10},{6,14},... | collective-permute-start | bytes 122888 | tf_op jit(solution)/shard_map/ppermute | solution.py:595
  7.4 8.1 %collective-permute-start.3 = (bf16[1,160,128]{2,1,0:T(8,128)(2,1)S(1)}, bf16[1,160,128]{2,1,0:T(8,128)(2,1)S(1)}, u32[]{:S(2)}, u32[]{:S(2)}) collective-permute-start(bf16[1,160,128]{2,1,0:T(8,128)(2,1)S(1)} %pick.1.p_ref.rest_1_), channel_id=1, source_target_pairs={{0,12},{4,8},{8,4},{12,0},{1,13},{5,9},{9,5},{13,1},{2,14},{6,10},... | collective-permute-start | bytes 122888 | tf_op jit(solution)/shard_map/ppermute | solution.py:595
  19.1 1.9 %copy-start.2 = (f32[320]{0:T(512)S(1)}, f32[320]{0:T(512)}, u32[]{:S(2)}) copy-start(f32[320]{0:T(512)} %param.13) | copy-start | bytes 3844
  19.1 1.9 %collective-permute-start.4 = (bf16[2,160,128]{2,1,0:T(8,128)(2,1)S(1)}, bf16[2,160,128]{2,1,0:T(8,128)(2,1)S(1)}, u32[]{:S(2)}, u32[]{:S(2)}) collective-permute-start(bf16[2,160,128]{2,1,0:T(8,128)(2,1)S(1)} %get-tuple-element.32), channel_id=1, source_target_pairs={{0,1},{1,0},{2,3},{3,2},{4,5},{5,4},{6,7},{7,6},{8,9},{9,8},{10,11... | collective-permute-start | bytes 245768 | tf_op jit(solution)/shard_map/ppermute | solution.py:615
  19.2 5.1 %collective-permute-start.5 = (bf16[2,160,128]{2,1,0:T(8,128)(2,1)S(1)}, bf16[2,160,128]{2,1,0:T(8,128)(2,1)S(1)}, u32[]{:S(2)}, u32[]{:S(2)}) collective-permute-start(bf16[2,160,128]{2,1,0:T(8,128)(2,1)S(1)} %get-tuple-element.35), channel_id=1, source_target_pairs={{0,2},{1,3},{2,0},{3,1},{4,6},{5,7},{6,4},{7,5},{8,10},{9,11},{10,... | collective-permute-start | bytes 245768 | tf_op jit(solution)/shard_map/ppermute | solution.py:615
  20.8 4.7 %collective-permute-start.6 = (bf16[2,160,128]{2,1,0:T(8,128)(2,1)S(1)}, bf16[2,160,128]{2,1,0:T(8,128)(2,1)S(1)}, u32[]{:S(2)}, u32[]{:S(2)}) collective-permute-start(bf16[2,160,128]{2,1,0:T(8,128)(2,1)S(1)} %get-tuple-element.36), channel_id=1, source_target_pairs={{0,3},{1,2},{2,1},{3,0},{4,7},{5,6},{6,5},{7,4},{8,11},{9,10},{10,... | collective-permute-start | bytes 245768 | tf_op jit(solution)/shard_map/ppermute | solution.py:615
